TPU v7x, 32 devices: a whole 2x2x4 slice. The times are simulated.
32 devices in a mesh: dp: 8 (over z, y), mp: 4 (over x, core).
Axes of the slice: x: 2, y: 2, z: 4, core: 2. Of those that a mesh axis runs over, the one named last changes fastest.
Arguments:
- frames: bfloat16 [16384, 1536], P(('dp', 'mp')), may hold values from -6 to 6
- cond_table: bfloat16 [8, 1536], replicated, may hold values from -6 to 6
- bucket_ids: int32 [8], P('dp'), may hold values from 0 to 7
- prompt: bfloat16 [8, 128, 768], P('dp'), may hold values from -6 to 6
- prompt_len: int32 [8], P('dp'), may hold values from 4 to 128, as said below
- attn_query: bfloat16 [1536, 1536], P('dp', 'mp'), may hold values from -0.15625 to 0.15625
- attn_key: bfloat16 [1536, 1536], P('dp', 'mp'), may hold values from -0.15625 to 0.15625
- attn_value: bfloat16 [1536, 1536], P('dp', 'mp'), may hold values from -0.15625 to 0.15625
- attn_out: bfloat16 [1536, 1536], P('dp', 'mp'), may hold values from -2.5 to 2.5
- cross_query: bfloat16 [1536, 1536], P('dp', 'mp'), may hold values from -0.15625 to 0.15625
- cross_key: bfloat16 [768, 1536], P('dp', 'mp'), may hold values from -0.21875 to 0.21875
- cross_value: bfloat16 [768, 1536], P('dp', 'mp'), may hold values from -0.21875 to 0.21875
- cross_out: bfloat16 [1536, 1536], P('dp', 'mp'), may hold values from -0.875 to 0.875
- glu_gate: bfloat16 [1536, 6144], P('dp', 'mp'), may hold values from -0.15625 to 0.15625
- glu_up: bfloat16 [1536, 6144], P('dp', 'mp'), may hold values from -0.15625 to 0.15625
- glu_down: bfloat16 [1536, 6144], P('dp', 'mp'), may hold values from -0.078125 to 0.078125
- first_gain: bfloat16 [1536], P('dp'), may hold values from 0.5 to 1.5
- second_gain: bfloat16 [1536], P('dp'), may hold values from 0.5 to 1.5
- third_gain: bfloat16 [1536], P('dp'), may hold values from 0.5 to 1.5
- grad_out: bfloat16 [16384, 1536], P(('dp', 'mp')), may hold values from -6 to 6
Outputs:
- block_out: bfloat16 [16384, 1536], P(('dp', 'mp'))
- frames_grad: float32 [16384, 1536], P(('dp', 'mp'))
- cond_grad: float32 [8, 1536], replicated
- attn_query_grad: float32 [1536, 1536], P('dp', 'mp')
- attn_key_grad: float32 [1536, 1536], P('dp', 'mp')
- attn_value_grad: float32 [1536, 1536], P('dp', 'mp')
- attn_out_grad: float32 [1536, 1536], P('dp', 'mp')
- cross_query_grad: float32 [1536, 1536], P('dp', 'mp')
- cross_key_grad: float32 [768, 1536], P('dp', 'mp')
- cross_value_grad: float32 [768, 1536], P('dp', 'mp')
- cross_out_grad: float32 [1536, 1536], P('dp', 'mp')
- glu_gate_grad: float32 [1536, 6144], P('dp', 'mp')
- glu_up_grad: float32 [1536, 6144], P('dp', 'mp')
- glu_down_grad: float32 [1536, 6144], P('dp', 'mp')
- first_gain_grad: float32 [1536], replicated
- second_gain_grad: float32 [1536], replicated
- third_gain_grad: float32 [1536], replicated
Inputs may be any that keep to these rules, and one draw needn't show every extreme that they name: `prompt_len`: one sequence has exactly 128 prompt tokens and another exactly 4.
All inputs are finite; a program needn't handle non-finite values.
Results may differ from a plain program's by a relative error of at most 0.02.
Values may be sent and summed in bfloat16 or wider, within the bound.
A program may use at most 320 MiB of HBM per device.

v0:
```python
import jax
import jax.numpy as jnp
from jax import lax
from jax.sharding import PartitionSpec as P

HD = 64
ROT = 32


def norm_rows(values, gain_row):
    center = values - jnp.mean(values, -1, keepdims=True)
    spread = lax.rsqrt(jnp.mean(center * center, -1, keepdims=True) + 1e-05)
    unit_rows = center * spread
    return (unit_rows * gain_row, unit_rows, spread)


def norm_back(grad_rows, unit_rows, spread, gain_row):
    scaled = grad_rows * gain_row
    result = spread * (
        scaled
        - jnp.mean(scaled, -1, keepdims=True)
        - unit_rows * jnp.mean(scaled * unit_rows, -1, keepdims=True)
    )
    return (result, jnp.sum(grad_rows * unit_rows, 0))


def rotate(tensor, offset, direction):
    count_rows = tensor.shape[-3]
    half_dim = ROT // 2
    position = offset + jnp.arange(count_rows).astype(jnp.float32)
    frequency = jnp.power(10000.0, -2.0 * jnp.arange(half_dim).astype(jnp.float32) / ROT)
    angles = position[:, None] * frequency[None, :]
    cosine = jnp.cos(angles)[:, None, :]
    sine_part = jnp.sin(angles)[:, None, :]
    first_half = tensor[..., :half_dim]
    second_half = tensor[..., half_dim:ROT]
    remainder = tensor[..., ROT:]
    return jnp.concatenate(
        [
            first_half * cosine - direction * second_half * sine_part,
            second_half * cosine + direction * first_half * sine_part,
            remainder,
        ],
        -1,
    )


def project(first_op, second_op):
    return jnp.einsum("...i,ij->...j", first_op, second_op, preferred_element_type=jnp.float32)


def project_back(first_op, second_op):
    return jnp.einsum("...j,ij->...i", first_op, second_op, preferred_element_type=jnp.float32)


def weight_grad(first_op, second_op):
    return jnp.einsum("...i,...j->ij", first_op, second_op, preferred_element_type=jnp.float32)


def attend(queries, key_rows, value_rows, key_mask):
    length, head_count = (queries.shape[0], queries.shape[1])
    block_rows = min(512, length)
    block_count = length // block_rows
    scale = HD ** (-0.5)

    def one_block(query_piece):
        scores = (
            jnp.einsum("qhd,khd->hqk", query_piece, key_rows, preferred_element_type=jnp.float32)
            * scale
        )
        masked = jnp.where(key_mask[None, None, :], scores, -1000000000.0)
        peak = jnp.max(masked, -1, keepdims=True)
        exponent = jnp.exp(masked - peak)
        totals = jnp.sum(exponent, -1, keepdims=True)
        probabilities = (exponent / totals).astype(jnp.bfloat16)
        mixed = jnp.einsum(
            "hqk,khd->qhd", probabilities, value_rows, preferred_element_type=jnp.float32
        )
        return (mixed.astype(jnp.bfloat16), (peak + jnp.log(totals))[..., 0])

    mixed, log_totals = lax.map(one_block, queries.reshape(block_count, block_rows, head_count, HD))
    return (mixed.reshape(length, head_count, HD), log_totals)


def attend_back(queries, key_rows, value_rows, key_mask, grad_mixed, log_totals):
    length, head_count = (queries.shape[0], queries.shape[1])
    block_rows = min(512, length)
    block_count = length // block_rows
    scale = HD ** (-0.5)

    def step(running, pieces):
        query_piece, grad_piece, total_piece = pieces
        scores = (
            jnp.einsum("qhd,khd->hqk", query_piece, key_rows, preferred_element_type=jnp.float32)
            * scale
        )
        masked = jnp.where(key_mask[None, None, :], scores, -1000000000.0)
        probabilities = jnp.exp(masked - total_piece[:, :, None])
        grad_probs = jnp.einsum(
            "qhd,khd->hqk", grad_piece, value_rows, preferred_element_type=jnp.float32
        )
        inner_sum = jnp.sum(grad_probs * probabilities, -1, keepdims=True)
        grad_scores = (probabilities * (grad_probs - inner_sum)).astype(jnp.bfloat16)
        grad_query = (
            jnp.einsum("hqk,khd->qhd", grad_scores, key_rows, preferred_element_type=jnp.float32)
            * scale
        )
        grad_keys = (
            running[0]
            + jnp.einsum(
                "hqk,qhd->khd", grad_scores, query_piece, preferred_element_type=jnp.float32
            )
            * scale
        )
        grad_values = running[1] + jnp.einsum(
            "hqk,qhd->khd",
            probabilities.astype(jnp.bfloat16),
            grad_piece,
            preferred_element_type=jnp.float32,
        )
        return ((grad_keys, grad_values), grad_query)

    zeros_keys = jnp.zeros(key_rows.shape, jnp.float32)
    (grad_keys, grad_values), grad_query = lax.scan(
        step,
        (zeros_keys, zeros_keys),
        (
            queries.reshape(block_count, block_rows, head_count, HD),
            grad_mixed.reshape(block_count, block_rows, head_count, HD),
            log_totals,
        ),
    )
    return (grad_query.reshape(length, head_count, HD), grad_keys, grad_values)


def spread_rows(share):
    return lax.all_gather(share, "mp", axis=0, tiled=True)


def spread_grads(share):
    return lax.all_gather(share, "mp", axis=0, tiled=True)


def branch_total(term, share_rows):
    return lax.psum_scatter(
        term.reshape(share_rows * lax.axis_size("mp"), -1), "mp", scatter_dimension=0, tiled=True
    )


def input_total(term, share_rows):
    return lax.psum_scatter(
        term.reshape(share_rows * lax.axis_size("mp"), -1), "mp", scatter_dimension=0, tiled=True
    )


def per_device(
    frames,
    cond_table,
    bucket_ids,
    prompt,
    prompt_len,
    attn_query,
    attn_key,
    attn_value,
    attn_out,
    cross_query,
    cross_key,
    cross_value,
    cross_out,
    glu_gate,
    glu_up,
    glu_down,
    first_gain,
    second_gain,
    third_gain,
    grad_out,
):
    sequences = bucket_ids.shape[0]
    share_rows, model_width = frames.shape
    length = share_rows * lax.axis_size("mp") // sequences
    buckets = cond_table.shape[0]
    onehot_rows = (bucket_ids[:, None] == jnp.arange(buckets)[None, :]).astype(jnp.float32)
    counts = lax.psum(jnp.sum(onehot_rows, 0), "dp")
    seq_weight = (
        sequences * lax.axis_size("dp") / (buckets * jnp.sum(onehot_rows * counts[None, :], 1))
    )
    local_params = (
        attn_query,
        attn_key,
        attn_value,
        attn_out,
        cross_query,
        cross_key,
        cross_value,
        cross_out,
        glu_gate,
        glu_up,
        glu_down,
        first_gain,
        second_gain,
        third_gain,
    )
    gathered = (
        lax.all_gather(local_params[0], "dp", axis=0, tiled=True),
        lax.all_gather(local_params[1], "dp", axis=0, tiled=True),
        lax.all_gather(local_params[2], "dp", axis=0, tiled=True),
        lax.all_gather(local_params[3], "dp", axis=0, tiled=True),
        lax.all_gather(local_params[4], "dp", axis=0, tiled=True),
        lax.all_gather(local_params[5], "dp", axis=0, tiled=True),
        lax.all_gather(local_params[6], "dp", axis=0, tiled=True),
        lax.all_gather(local_params[7], "dp", axis=0, tiled=True),
        lax.all_gather(local_params[8], "dp", axis=0, tiled=True),
        lax.all_gather(local_params[9], "dp", axis=0, tiled=True),
        lax.all_gather(local_params[10], "dp", axis=0, tiled=True),
        lax.all_gather(local_params[11], "dp", axis=0, tiled=True),
        lax.all_gather(local_params[12], "dp", axis=0, tiled=True),
        lax.all_gather(local_params[13], "dp", axis=0, tiled=True),
    )
    (
        query_full,
        key_full,
        value_full,
        out_full,
        cross_query_full,
        cross_key_full,
        cross_value_full,
        cross_out_full,
        gate_full,
        up_full,
        down_full,
        first_full,
        second_full,
        third_full,
    ) = gathered
    gain_one = first_full.astype(jnp.float32)
    gain_two = second_full.astype(jnp.float32)
    gain_three = third_full.astype(jnp.float32)
    head_count = query_full.shape[1] // HD
    prompt_count = prompt.shape[1]
    share = frames.astype(jnp.float32)
    cond_rows = jnp.dot(
        onehot_rows.astype(jnp.bfloat16), cond_table, preferred_element_type=jnp.float32
    )
    normed_cond, unit_cond, spread_cond = norm_rows(cond_rows, gain_one)
    normed_share, unit_one, spread_one = norm_rows(share, gain_one)
    frames_normed = spread_rows(normed_share.astype(jnp.bfloat16)).reshape(
        sequences, length, model_width
    )
    normed_one = jnp.concatenate([normed_cond.astype(jnp.bfloat16)[:, None, :], frames_normed], 1)
    queries = rotate(
        project(frames_normed, query_full).reshape(sequences, length, head_count, HD), 1.0, 1.0
    ).astype(jnp.bfloat16)
    key_rows = rotate(
        project(normed_one, key_full).reshape(sequences, length + 1, head_count, HD), 0.0, 1.0
    ).astype(jnp.bfloat16)
    value_rows = (
        project(normed_one, value_full)
        .astype(jnp.bfloat16)
        .reshape(sequences, length + 1, head_count, HD)
    )
    self_mask = jnp.full((sequences, length + 1), True)
    mixed, self_totals = jax.vmap(attend)(queries, key_rows, value_rows, self_mask)
    mixed = mixed.reshape(sequences, length, -1)
    after_self = share + branch_total(project_back(mixed, out_full), share_rows)
    normed_share, unit_two, spread_two = norm_rows(after_self, gain_two)
    normed_two = spread_rows(normed_share.astype(jnp.bfloat16)).reshape(
        sequences, length, model_width
    )
    cross_queries = (
        project(normed_two, cross_query_full)
        .astype(jnp.bfloat16)
        .reshape(sequences, length, head_count, HD)
    )
    cross_keys = (
        project(prompt, cross_key_full)
        .astype(jnp.bfloat16)
        .reshape(sequences, prompt_count, head_count, HD)
    )
    cross_values = (
        project(prompt, cross_value_full)
        .astype(jnp.bfloat16)
        .reshape(sequences, prompt_count, head_count, HD)
    )
    prompt_mask = jnp.arange(prompt_count)[None, :] < prompt_len[:, None]
    cross_mixed, cross_totals = jax.vmap(attend)(
        cross_queries, cross_keys, cross_values, prompt_mask
    )
    cross_mixed = cross_mixed.reshape(sequences, length, -1)
    after_cross = after_self + branch_total(project_back(cross_mixed, cross_out_full), share_rows)
    normed_share, unit_three, spread_three = norm_rows(after_cross, gain_three)
    normed_three = spread_rows(normed_share.astype(jnp.bfloat16)).reshape(
        sequences, length, model_width
    )
    gate_value = project(normed_three, gate_full)
    up_value = project(normed_three, up_full)
    hidden = (jax.nn.silu(gate_value) * up_value).astype(jnp.bfloat16)
    result = after_cross + branch_total(project_back(hidden, down_full), share_rows)
    block_out = result.astype(jnp.bfloat16)
    row_index = lax.axis_index("mp") * share_rows + jnp.arange(share_rows)
    row_seq = row_index // length
    row_weight = jnp.sum(
        (row_seq[:, None] == jnp.arange(sequences)[None, :]).astype(jnp.float32)
        * seq_weight[None, :],
        1,
    )
    cotangent = grad_out.astype(jnp.float32) * row_weight[:, None]
    branch_grad = spread_grads(cotangent.astype(jnp.bfloat16)).reshape(
        sequences, length, model_width
    )
    grad_down = weight_grad(branch_grad, hidden)
    grad_hidden = project(branch_grad, down_full)
    sigmoid_gate = jax.nn.sigmoid(gate_value)
    grad_gate_rows = (
        grad_hidden * up_value * sigmoid_gate * (1.0 + gate_value * (1.0 - sigmoid_gate))
    ).astype(jnp.bfloat16)
    grad_up_rows = (grad_hidden * gate_value * sigmoid_gate).astype(jnp.bfloat16)
    grad_gate = weight_grad(normed_three, grad_gate_rows)
    grad_up = weight_grad(normed_three, grad_up_rows)
    normed_grad = input_total(
        project_back(grad_gate_rows, gate_full) + project_back(grad_up_rows, up_full), share_rows
    )
    back_three, grad_third = norm_back(normed_grad, unit_three, spread_three, gain_three)
    carried = cotangent + back_three
    branch_grad = spread_grads(carried.astype(jnp.bfloat16)).reshape(sequences, length, model_width)
    grad_cross_out = weight_grad(branch_grad, cross_mixed)
    grad_cross_mixed = (
        project(branch_grad, cross_out_full)
        .astype(jnp.bfloat16)
        .reshape(sequences, length, head_count, HD)
    )
    back_query, back_keys, back_values = jax.vmap(attend_back)(
        cross_queries, cross_keys, cross_values, prompt_mask, grad_cross_mixed, cross_totals
    )
    back_query = back_query.astype(jnp.bfloat16).reshape(sequences, length, -1)
    back_keys = back_keys.astype(jnp.bfloat16).reshape(sequences, prompt_count, -1)
    back_values = back_values.astype(jnp.bfloat16).reshape(sequences, prompt_count, -1)
    grad_cross_query = weight_grad(normed_two, back_query)
    grad_cross_key = weight_grad(prompt, back_keys)
    grad_cross_value = weight_grad(prompt, back_values)
    normed_grad = input_total(project_back(back_query, cross_query_full), share_rows)
    back_two, grad_second = norm_back(normed_grad, unit_two, spread_two, gain_two)
    carried = carried + back_two
    branch_grad = spread_grads(carried.astype(jnp.bfloat16)).reshape(sequences, length, model_width)
    grad_attn_out = weight_grad(branch_grad, mixed)
    grad_mixed = (
        project(branch_grad, out_full)
        .astype(jnp.bfloat16)
        .reshape(sequences, length, head_count, HD)
    )
    back_query, back_keys, back_values = jax.vmap(attend_back)(
        queries, key_rows, value_rows, self_mask, grad_mixed, self_totals
    )
    back_query = rotate(back_query, 1.0, -1.0).astype(jnp.bfloat16).reshape(sequences, length, -1)
    back_keys = rotate(back_keys, 0.0, -1.0).astype(jnp.bfloat16).reshape(sequences, length + 1, -1)
    back_values = back_values.astype(jnp.bfloat16).reshape(sequences, length + 1, -1)
    grad_attn_query = weight_grad(frames_normed, back_query)
    grad_attn_key = weight_grad(normed_one, back_keys)
    grad_attn_value = weight_grad(normed_one, back_values)
    joined_grad = project_back(back_keys, key_full) + project_back(back_values, value_full)
    frame_grad = joined_grad[:, 1:] + project_back(back_query, query_full)
    normed_grad = input_total(frame_grad, share_rows)
    back_one, grad_first_frames = norm_back(normed_grad, unit_one, spread_one, gain_one)
    cond_back, grad_first_cond = norm_back(joined_grad[:, 0], unit_cond, spread_cond, gain_one)
    carried = carried + back_one
    cond_local = jnp.dot(onehot_rows.T, cond_back, precision=lax.Precision.HIGHEST)
    cond_grad, grad_first, grad_second, grad_third = lax.psum(
        (cond_local, grad_first_frames + grad_first_cond, grad_second, grad_third), ("dp", "mp")
    )
    owned = (
        lax.psum_scatter(grad_attn_query, "dp", scatter_dimension=0, tiled=True),
        lax.psum_scatter(grad_attn_key, "dp", scatter_dimension=0, tiled=True),
        lax.psum_scatter(grad_attn_value, "dp", scatter_dimension=0, tiled=True),
        lax.psum_scatter(grad_attn_out, "dp", scatter_dimension=0, tiled=True),
        lax.psum_scatter(grad_cross_query, "dp", scatter_dimension=0, tiled=True),
        lax.psum_scatter(grad_cross_key, "dp", scatter_dimension=0, tiled=True),
        lax.psum_scatter(grad_cross_value, "dp", scatter_dimension=0, tiled=True),
        lax.psum_scatter(grad_cross_out, "dp", scatter_dimension=0, tiled=True),
        lax.psum_scatter(grad_gate, "dp", scatter_dimension=0, tiled=True),
        lax.psum_scatter(grad_up, "dp", scatter_dimension=0, tiled=True),
        lax.psum_scatter(grad_down, "dp", scatter_dimension=0, tiled=True),
    )
    return (
        block_out,
        carried,
        cond_grad,
        owned[0],
        owned[1],
        owned[2],
        owned[3],
        owned[4],
        owned[5],
        owned[6],
        owned[7],
        owned[8],
        owned[9],
        owned[10],
        grad_first,
        grad_second,
        grad_third,
    )


def solution(mesh):
    return jax.shard_map(
        per_device,
        mesh=mesh,
        in_specs=(
            P(("dp", "mp"), None),
            P(),
            P("dp"),
            P("dp", None, None),
            P("dp"),
            P("dp", "mp"),
            P("dp", "mp"),
            P("dp", "mp"),
            P("dp", "mp"),
            P("dp", "mp"),
            P("dp", "mp"),
            P("dp", "mp"),
            P("dp", "mp"),
            P("dp", "mp"),
            P("dp", "mp"),
            P("dp", "mp"),
            P("dp"),
            P("dp"),
            P("dp"),
            P(("dp", "mp"), None),
        ),
        out_specs=(
            P(("dp", "mp"), None),
            P(("dp", "mp"), None),
            P(),
            P("dp", "mp"),
            P("dp", "mp"),
            P("dp", "mp"),
            P("dp", "mp"),
            P("dp", "mp"),
            P("dp", "mp"),
            P("dp", "mp"),
            P("dp", "mp"),
            P("dp", "mp"),
            P("dp", "mp"),
            P("dp", "mp"),
            P(),
            P(),
            P(),
        ),
        check_vma=False,
    )
```

profile of v0, /device:TPU:0, one launch (start us, length us, event | category | flops | bytes accessed | tf_op | source)
XLA Modules:
  0.0 3312.7 jit_solution(16546919168265027135)
XLA Ops:
  13.9 39.1 %all-reduce.4 = (bf16[1536]{0:T(1024)(128)(2,1)S(1)}, bf16[1536]{0:T(1024)(128)(2,1)}, bf16[1536]{0:T(1024)(128)(2,1)}) all-reduce(bf16[1536]{0:T(1024)(128)(2,1)S(1)} %dynamic-update-slice, bf16[1536]{0:T(1024)(128)(2,1)S(1)} %dynamic-update-slice.1, bf16[1536]{0:T(1024)(128)(2,1)S(1)} %dynamic-update-slice.2), channel_id=1, replica_groups=mesh['dp'=8,'mp'=4] {'dp'}, use_global_device_ids=true, to_apply=%add | all-reduce | flops 4608 | bytes 18432
  66.0 30.4 all-gather.18.cloned.1.call-done
  98.7 39.7 %all-gather.22.cloned.1.call-done = bf16[1536,384]{1,0:T(8,128)(2,1)} async-done(((bf16[192,384]{1,0:T(8,128)(2,1)}), bf16[1536,384]{1,0:T(8,128)(2,1)}) %all-gather.22.cloned.1.call-update) | async-done | bytes 1179664 | tf_op jit(solution)/shard_map/all_gather | solution.py:206
  138.4 47.2 %all-gather.16.cloned.1.call-done = bf16[2048,1536]{1,0:T(8,128)(2,1)} async-done(((bf16[512,1536]{1,0:T(8,128)(2,1)}), bf16[2048,1536]{1,0:T(8,128)(2,1)}) %all-gather.16.cloned.1.call-update) | async-done | bytes 6291472 | tf_op jit(solution)/shard_map/all_gather | solution.py:137
  206.4 139.4 %while.55 = (s32[]{:T(128)}, bf16[4,1,512,6,64]{2,4,3,1,0:T(8,128)(2,1)S(1)}, f32[4,1,6,512]{3,2,1,0:T(8,128)S(1)}, bf16[4,1,512,6,64]{2,4,3,1,0:T(8,128)(2,1)},...) while((s32[]{:T(128)}, bf16[4,1,512,6,64]{2,4,3,1,0:T(8,128)(2,1)S(1)}, ...), condition=%wide.region_7.8_spmd, body=%wide.region_4.7_spmd.sunk | while | flops 1668243456 | bytes 79586912 | solution.py:81
  206.8 13.0 multiply_reduce_fusion.17
  356.6 98.4 %reduce-scatter.22.cloned.1.call-done = f32[512,1536]{1,0:T(8,128)} async-done(((f32[2048,1536]{1,0:T(8,128)}), f32[512,1536]{1,0:T(8,128)}) %reduce-scatter.22.cloned.1.call-update) | async-done | bytes 3145744 | tf_op jit(solution)/shard_map/reduce_scatter | solution.py:145
  461.7 32.8 all_gather.69
  494.9 32.2 all_gather.70
  529.1 20.2 all-gather.26.cloned.1.call-done
  568.3 16.6 while.56
  603.2 97.1 %reduce-scatter.24.cloned.1.call-done = f32[512,1536]{1,0:T(8,128)} async-done(((f32[2048,1536]{1,0:T(8,128)}), f32[512,1536]{1,0:T(8,128)}) %reduce-scatter.24.cloned.1.call-update) | async-done | bytes 3145744 | tf_op jit(solution)/shard_map/reduce_scatter | solution.py:145
  707.4 21.8 psum.35
  732.9 49.9 %all-gather.36.cloned.1.call-done = bf16[1536,1536]{1,0:T(8,128)(2,1)} async-done(((bf16[192,1536]{1,0:T(8,128)(2,1)}), bf16[1536,1536]{1,0:T(8,128)(2,1)}) %all-gather.36.cloned.1.call-update) | async-done | bytes 4718608 | tf_op jit(solution)/shard_map/all_gather | solution.py:213
  782.8 46.5 %all-gather.32.cloned.1.call-done = bf16[2048,1536]{1,0:T(8,128)(2,1)} async-done(((bf16[512,1536]{1,0:T(8,128)(2,1)}), bf16[2048,1536]{1,0:T(8,128)(2,1)}) %all-gather.32.cloned.1.call-update) | async-done | bytes 6291472 | tf_op jit(solution)/shard_map/all_gather | solution.py:137
  829.3 16.0 fusion.147
  845.3 66.1 %all-gather.34.cloned.1.call-done = bf16[1536,1536]{1,0:T(8,128)(2,1)} async-done(((bf16[192,1536]{1,0:T(8,128)(2,1)}), bf16[1536,1536]{1,0:T(8,128)(2,1)}) %all-gather.34.cloned.1.call-update) | async-done | bytes 4718608 | tf_op jit(solution)/shard_map/all_gather | solution.py:212
  911.4 16.0 fusion.146
  927.5 64.1 %all-gather.38.cloned.1.call-done = bf16[1536,1536]{1,0:T(8,128)(2,1)} async-done(((bf16[192,1536]{1,0:T(8,128)(2,1)}), bf16[1536,1536]{1,0:T(8,128)(2,1)}) %all-gather.38.cloned.1.call-update) | async-done | bytes 4718608 | tf_op jit(solution)/shard_map/all_gather | solution.py:214
  991.5 46.0 %all-gather.40.cloned.1.call-done = bf16[2048,1536]{1,0:T(8,128)(2,1)} async-done(((bf16[512,1536]{1,0:T(8,128)(2,1)}), bf16[2048,1536]{1,0:T(8,128)(2,1)}) %all-gather.40.cloned.1.call-update) | async-done | bytes 6291472 | tf_op jit(solution)/shard_map/all_gather | solution.py:141
  1037.5 25.2 multiply_convert_fusion.2
  1062.7 17.0 fusion.149
  1079.7 16.6 convolution_add_fusion.1
  1096.4 17.2 fusion.148
  1113.7 81.8 %reduce-scatter.28.cloned.1.call-done = f32[512,1536]{1,0:T(8,128)} async-done(((f32[2048,1536]{1,0:T(8,128)}), f32[512,1536]{1,0:T(8,128)}) %reduce-scatter.28.cloned.1.call-update) | async-done | bytes 3145744 | tf_op jit(solution)/shard_map/reduce_scatter | solution.py:151
  1199.2 97.9 %reduce-scatter.26.cloned.1.call-done = f32[512,1536]{1,0:T(8,128)} async-done(((f32[2048,1536]{1,0:T(8,128)}), f32[512,1536]{1,0:T(8,128)}) %reduce-scatter.26.cloned.1.call-update) | async-done | bytes 3145744 | tf_op jit(solution)/shard_map/reduce_scatter | solution.py:145
  1303.0 46.5 %all-gather.42.cloned.1.call-done = bf16[2048,1536]{1,0:T(8,128)(2,1)} async-done(((bf16[512,1536]{1,0:T(8,128)(2,1)}), bf16[2048,1536]{1,0:T(8,128)(2,1)}) %all-gather.42.cloned.1.call-update) | async-done | bytes 6291472 | tf_op jit(solution)/shard_map/all_gather | solution.py:141
  1361.2 29.4 while.57
  1401.5 99.1 %reduce-scatter.30.cloned.1.call-done = f32[512,1536]{1,0:T(8,128)} async-done(((f32[2048,1536]{1,0:T(8,128)}), f32[512,1536]{1,0:T(8,128)}) %reduce-scatter.30.cloned.1.call-update) | async-done | bytes 3145744 | tf_op jit(solution)/shard_map/reduce_scatter | solution.py:151
  1507.4 46.5 %all-gather.44.cloned.1.call-done = bf16[2048,1536]{1,0:T(8,128)(2,1)} async-done(((bf16[512,1536]{1,0:T(8,128)(2,1)}), bf16[2048,1536]{1,0:T(8,128)(2,1)}) %all-gather.44.cloned.1.call-update) | async-done | bytes 6291472 | tf_op jit(solution)/shard_map/all_gather | solution.py:141
  1566.5 407.2 %while.58 = (s32[]{:T(128)}, f32[1,2049,6,64]{1,3,2,0:T(8,128)}, f32[1,2049,6,64]{1,3,2,0:T(8,128)}, f32[4,1,512,6,64]{2,0,4,3,1:T(4,128)}, bf16[4,1,512,6,64]{2...) while((s32[]{:T(128)}, f32[1,2049,6,64]{1,3,2,0:T(8,128)}, ...), condition=%wide.region_32.33_spmd.clone, body=%wide.region_30.32_spmd.clone.sunk | while | flops 4108159744 | bytes 212439696 | solution.py:124
  1580.4 14.7 fusion.275
  1595.1 16.5 multiply_reduce_fusion.19
  1611.6 21.2 multiply_convert_fusion.11
  1650.9 16.1 dynamic_update_slice.41
  1667.7 12.8 fusion.273
  1680.6 15.8 fusion.275
  1696.3 16.5 multiply_reduce_fusion.19
  1712.8 21.2 multiply_convert_fusion.11
  1753.1 16.1 dynamic_update_slice.41
  1769.9 12.8 fusion.273
  1782.7 15.8 fusion.275
  1798.5 16.5 multiply_reduce_fusion.19
  1815.0 21.2 multiply_convert_fusion.11
  1855.3 16.1 dynamic_update_slice.41
  1884.9 15.8 fusion.275
  1900.8 16.5 multiply_reduce_fusion.19
  1917.2 21.2 multiply_convert_fusion.11
  1957.5 16.1 dynamic_update_slice.41
  2007.3 16.0 fusion.158
  2023.4 16.7 fusion.156
  2040.2 15.6 fusion.157
  2122.9 151.3 %reduce-scatter.50.cloned.1.call-done = f32[192,1536]{1,0:T(8,128)} async-done(((f32[1536,1536]{1,0:T(8,128)}), f32[192,1536]{1,0:T(8,128)}) %reduce-scatter.50.cloned.1.call-update) | async-done | bytes 1179664 | tf_op jit(solution)/shard_map/reduce_scatter | solution.py:380
  2274.2 166.8 %reduce-scatter.46.cloned.1.call-done = f32[192,1536]{1,0:T(8,128)} async-done(((f32[1536,1536]{1,0:T(8,128)}), f32[192,1536]{1,0:T(8,128)}) %reduce-scatter.46.cloned.1.call-update) | async-done | bytes 1179664 | tf_op jit(solution)/shard_map/reduce_scatter | solution.py:378
  2440.9 166.6 %reduce-scatter.48.cloned.1.call-done = f32[192,1536]{1,0:T(8,128)} async-done(((f32[1536,1536]{1,0:T(8,128)}), f32[192,1536]{1,0:T(8,128)}) %reduce-scatter.48.cloned.1.call-update) | async-done | bytes 1179664 | tf_op jit(solution)/shard_map/reduce_scatter | solution.py:379
  2607.5 67.2 %reduce-scatter.54.cloned.1.call-done = f32[96,384]{1,0:T(8,128)} async-done(((f32[768,384]{1,0:T(8,128)}), f32[96,384]{1,0:T(8,128)}) %reduce-scatter.54.cloned.1.call-update) | async-done | bytes 147472
  2674.7 66.9 %reduce-scatter.52.cloned.1.call-done = f32[96,384]{1,0:T(8,128)} async-done(((f32[768,384]{1,0:T(8,128)}), f32[96,384]{1,0:T(8,128)}) %reduce-scatter.52.cloned.1.call-update) | async-done | bytes 147472
  2741.6 71.9 %reduce-scatter.42.cloned.1.call-done = f32[192,384]{1,0:T(8,128)} async-done(((f32[1536,384]{1,0:T(8,128)}), f32[192,384]{1,0:T(8,128)}) %reduce-scatter.42.cloned.1.call-update) | async-done | bytes 294928 | tf_op jit(solution)/shard_map/reduce_scatter | solution.py:374
  2813.5 72.2 %reduce-scatter.44.cloned.1.call-done = f32[192,384]{1,0:T(8,128)} async-done(((f32[1536,384]{1,0:T(8,128)}), f32[192,384]{1,0:T(8,128)}) %reduce-scatter.44.cloned.1.call-update) | async-done | bytes 294928 | tf_op jit(solution)/shard_map/reduce_scatter | solution.py:377
  2885.7 72.2 %reduce-scatter.40.cloned.1.call-done = f32[192,384]{1,0:T(8,128)} async-done(((f32[1536,384]{1,0:T(8,128)}), f32[192,384]{1,0:T(8,128)}) %reduce-scatter.40.cloned.1.call-update) | async-done | bytes 294928 | tf_op jit(solution)/shard_map/reduce_scatter | solution.py:373
  2957.9 72.0 %reduce-scatter.38.cloned.1.call-done = f32[192,384]{1,0:T(8,128)} async-done(((f32[1536,384]{1,0:T(8,128)}), f32[192,384]{1,0:T(8,128)}) %reduce-scatter.38.cloned.1.call-update) | async-done | bytes 294928 | tf_op jit(solution)/shard_map/reduce_scatter | solution.py:372
  3029.8 72.2 %reduce-scatter.36.cloned.1.call-done = f32[192,384]{1,0:T(8,128)} async-done(((f32[1536,384]{1,0:T(8,128)}), f32[192,384]{1,0:T(8,128)}) %reduce-scatter.36.cloned.1.call-update) | async-done | bytes 294928 | tf_op jit(solution)/shard_map/reduce_scatter | solution.py:371
  3102.0 72.2 %reduce-scatter.34.cloned.1.call-done = f32[192,384]{1,0:T(8,128)} async-done(((f32[1536,384]{1,0:T(8,128)}), f32[192,384]{1,0:T(8,128)}) %reduce-scatter.34.cloned.1.call-update) | async-done | bytes 294928 | tf_op jit(solution)/shard_map/reduce_scatter | solution.py:370
  3174.1 126.2 %all-reduce.7.cloned.1.call-done = (f32[8,1536]{1,0:T(8,128)}, f32[1536]{0:T(1024)}, f32[1536]{0:T(1024)}, f32[1536]{0:T(1024)}) async-done(((f32[8,1536]{1,0:T(8,128)}, f32[1536]{0:T(1024)}, f32[1536]{0:T(1024)}, f32[1536]{0:T(1024)}), (f32[8,1536]{1,0:T(8,128)}, f32[1536]{0:T(1024)}, f32[1536]{0:T(1024)}, f32[1536]{0:T(1024)})) %all-reduce.7.cloned.1.call-update) | async-done | bytes 67600 | tf_op jit(solution)/shard_map/psum | solution.py:366
  (469 shorter events, 537.8 us)
Async XLA Ops:
  7.2 487.4 %copy-start = (bf16[1,128,768]{2,1,0:T(8,128)(2,1)S(1)}, bf16[1,128,768]{2,1,0:T(8,128)(2,1)}, u32[]{:S(2)}) copy-start(bf16[1,128,768]{2,1,0:T(8,128)(2,1)} %param.31) | copy-start | bytes 589828
  7.2 47.5 %copy-start.10 = (bf16[512,1536]{1,0:T(8,128)(2,1)S(1)}, bf16[512,1536]{1,0:T(8,128)(2,1)}, u32[]{:S(2)}) copy-start(bf16[512,1536]{1,0:T(8,128)(2,1)} %param.28) | copy-start | bytes 4718596
  7.2 57.1 %all-gather.20.cloned.1.call-start = ((), (), s32[]{:S(2)}) async-start(), calls=%async_computation.19 | async-start | bytes 1327104 | tf_op jit(solution)/shard_map/all_gather | solution.py:205
  7.9 88.4 %all-gather.18.cloned.1.call-start = ((), (), s32[]{:S(2)}) async-start(), calls=%async_computation.18 | async-start | bytes 1327104 | tf_op jit(solution)/shard_map/all_gather | solution.py:204
  8.7 129.7 %all-gather.22.cloned.1.call-start = ((), (), s32[]{:S(2)}) async-start(), calls=%async_computation.20 | async-start | bytes 1327104 | tf_op jit(solution)/shard_map/all_gather | solution.py:206
  9.4 176.1 %all-gather.16.cloned.1.call-start = ((), (), s32[]{:S(2)}) async-start(), calls=%async_computation.17 | async-start | bytes 7864320 | tf_op jit(solution)/shard_map/all_gather | solution.py:137
  53.0 8.8 copy-start.52
  57.6 289.9 %all-gather.24.cloned.1.call-start = ((), (), s32[]{:S(2)}) async-start(), calls=%async_computation.21 | async-start | bytes 1327104 | tf_op jit(solution)/shard_map/all_gather | solution.py:207
  58.2 396.8 %reduce-scatter.22.cloned.1.call-start = ((), (), s32[]{:S(2)}) async-start(), calls=%async_computation.22 | async-start | bytes 15728640 | tf_op jit(solution)/shard_map/reduce_scatter | solution.py:145
  59.3 126.3 %copy-start.43 = (f32[1536]{0:T(1024)}, f32[1536]{0:T(1024)S(1)}, u32[]{:S(2)}) copy-start(f32[1536]{0:T(1024)S(1)} %convolution_reduce_fusion) | copy-start | bytes 18436
  61.9 139.0 %copy-start.69 = (bf16[1,1,1536]{2,1,0:T(2,128)(2,1)}, bf16[1,1,1536]{2,1,0:T(2,128)(2,1)S(1)}, u32[]{:S(2)}) copy-start(bf16[1,1,1536]{2,1,0:T(2,128)(2,1)S(1)} %broadcast_in_dim.59) | copy-start | bytes 9220
  63.1 136.8 %copy-start.38 = (f32[2048,16]{0,1:T(8,128)}, f32[2048,16]{0,1:T(8,128)S(1)}, u32[]{:S(2)}) copy-start(f32[2048,16]{0,1:T(8,128)S(1)} %get-tuple-element.536) | copy-start | bytes 393220
  64.3 141.4 %copy-start.36 = (f32[2049,16]{0,1:T(8,128)}, f32[2049,16]{0,1:T(8,128)S(1)}, u32[]{:S(2)}) copy-start(f32[2049,16]{0,1:T(8,128)S(1)} %get-tuple-element.533) | copy-start | bytes 393412
  347.5 8.3 copy-start.25
  355.8 173.3 %all-gather.28.cloned.1.call-start = ((), (), s32[]{:S(2)}) async-start(), calls=%async_computation.24 | async-start | bytes 1327104 | tf_op jit(solution)/shard_map/all_gather | solution.py:208
  356.5 192.8 %all-gather.26.cloned.1.call-start = ((), (), s32[]{:S(2)}) async-start(), calls=%async_computation.23 | async-start | bytes 7864320 | tf_op jit(solution)/shard_map/all_gather | solution.py:137
  356.6 101.6 %copy-start.45 = (f32[1536]{0:T(1024)}, f32[1536]{0:T(1024)S(1)}, u32[]{:S(2)}) copy-start(f32[1536]{0:T(1024)S(1)} %convert_element_type.310) | copy-start | bytes 18436
  457.7 242.6 %copy-start.4 = (f32[512,1536]{1,0:T(8,128)}, f32[512,1536]{1,0:T(8,128)S(1)}, u32[]{:S(2)}) copy-start(f32[512,1536]{1,0:T(8,128)S(1)} %get-tuple-element.508) | copy-start | bytes 9437188
  460.9 131.7 %all-gather.30.cloned.1.call-start = ((), (), s32[]{:S(2)}) async-start(), calls=%async_computation.25 | async-start | bytes 1327104 | tf_op jit(solution)/shard_map/all_gather | solution.py:211
  461.7 238.7 %reduce-scatter.24.cloned.1.call-start = ((), (), s32[]{:S(2)}) async-start(), calls=%async_computation.26 | async-start | bytes 15728640 | tf_op jit(solution)/shard_map/reduce_scatter | solution.py:145
  602.4 180.4 %all-gather.36.cloned.1.call-start = ((), (), s32[]{:S(2)}) async-start(), calls=%async_computation.29 | async-start | bytes 5308416 | tf_op jit(solution)/shard_map/all_gather | solution.py:213
  603.1 226.2 %all-gather.32.cloned.1.call-start = ((), (), s32[]{:S(2)}) async-start(), calls=%async_computation.27 | async-start | bytes 7864320 | tf_op jit(solution)/shard_map/all_gather | solution.py:137
  603.2 99.9 %copy-start.47 = (f32[1536]{0:T(1024)}, f32[1536]{0:T(1024)S(1)}, u32[]{:S(2)}) copy-start(f32[1536]{0:T(1024)S(1)} %convert_element_type.315) | copy-start | bytes 18436
  704.3 26.8 copy-start.30
  706.0 205.4 %all-gather.34.cloned.1.call-start = ((), (), s32[]{:S(2)}) async-start(), calls=%async_computation.28 | async-start | bytes 5308416 | tf_op jit(solution)/shard_map/all_gather | solution.py:212
  706.7 284.8 %all-gather.38.cloned.1.call-start = ((), (), s32[]{:S(2)}) async-start(), calls=%async_computation.30 | async-start | bytes 5308416 | tf_op jit(solution)/shard_map/all_gather | solution.py:214
  707.3 330.2 %all-gather.40.cloned.1.call-start = ((), (), s32[]{:S(2)}) async-start(), calls=%async_computation.32 | async-start | bytes 7864320 | tf_op jit(solution)/shard_map/all_gather | solution.py:141
  707.4 138.0 %copy-start.73 = (f32[8]{0:T(128)}, f32[8]{0:T(128)S(1)}, u32[]{:S(2)}) copy-start(f32[8]{0:T(128)S(1)} %compare_convert_fusion) | copy-start | bytes 100
  732.6 462.9 %reduce-scatter.28.cloned.1.call-start = ((), (), s32[]{:S(2)}) async-start(), calls=%async_computation.33 | async-start | bytes 15728640 | tf_op jit(solution)/shard_map/reduce_scatter | solution.py:151
  1037.5 25.2 copy-start.75
  1062.7 17.0 copy-start.76
  1096.3 200.7 %reduce-scatter.26.cloned.1.call-start = ((), (), s32[]{:S(2)}) async-start(), calls=%async_computation.31 | async-start | bytes 15728640 | tf_op jit(solution)/shard_map/reduce_scatter | solution.py:145
  1113.6 82.0 %copy-start.9 = (f32[512,1536]{1,0:T(8,128)S(1)}, f32[512,1536]{1,0:T(8,128)}, u32[]{:S(2)}) copy-start(f32[512,1536]{1,0:T(8,128)} %copy-done.8) | copy-start | bytes 9437188
  1113.6 82.0 %copy-start.48 = (f32[1536]{0:T(1024)S(1)}, f32[1536]{0:T(1024)}, u32[]{:S(2)}) copy-start(f32[1536]{0:T(1024)} %copy-done.47) | copy-start | bytes 18436
  1113.6 82.0 %copy-start.59 = (f32[512]{0:T(512)S(1)}, f32[512]{0:T(512)}, u32[]{:S(2)}) copy-start(f32[512]{0:T(512)} %copy-done.58) | copy-start | bytes 6148
  1113.6 82.0 %copy-start.65 = (f32[512]{0:T(512)S(1)}, f32[512]{0:T(512)}, u32[]{:S(2)}) copy-start(f32[512]{0:T(512)} %copy-done.64) | copy-start | bytes 6148
  1113.7 183.4 %copy-start.68 = (f32[512]{0:T(512)S(1)}, f32[512]{0:T(512)}, u32[]{:S(2)}) copy-start(f32[512]{0:T(512)} %copy-done.67) | copy-start | bytes 6148
  1113.7 235.8 %all-gather.42.cloned.1.call-start = ((), (), s32[]{:S(2)}) async-start(), calls=%async_computation.34 | async-start | bytes 7864320 | tf_op jit(solution)/shard_map/all_gather | solution.py:141
  1302.9 197.7 %reduce-scatter.30.cloned.1.call-start = ((), (), s32[]{:S(2)}) async-start(), calls=%async_computation.35 | async-start | bytes 15728640 | tf_op jit(solution)/shard_map/reduce_scatter | solution.py:151
  1401.4 99.2 %copy-start.5 = (f32[512,1536]{1,0:T(8,128)S(1)}, f32[512,1536]{1,0:T(8,128)}, u32[]{:S(2)}) copy-start(f32[512,1536]{1,0:T(8,128)} %copy-done.4) | copy-start | bytes 9437188
  1401.4 99.2 %copy-start.46 = (f32[1536]{0:T(1024)S(1)}, f32[1536]{0:T(1024)}, u32[]{:S(2)}) copy-start(f32[1536]{0:T(1024)} %copy-done.45) | copy-start | bytes 18436
  1401.4 99.2 %copy-start.55 = (f32[512]{0:T(512)S(1)}, f32[512]{0:T(512)}, u32[]{:S(2)}) copy-start(f32[512]{0:T(512)} %copy-done.54) | copy-start | bytes 6148
  1401.4 99.2 %copy-start.61 = (f32[512]{0:T(512)S(1)}, f32[512]{0:T(512)}, u32[]{:S(2)}) copy-start(f32[512]{0:T(512)} %copy-done.60) | copy-start | bytes 6148
  1401.5 152.4 %all-gather.44.cloned.1.call-start = ((), (), s32[]{:S(2)}) async-start(), calls=%async_computation.36 | async-start | bytes 7864320 | tf_op jit(solution)/shard_map/all_gather | solution.py:141
  1507.3 604.7 %reduce-scatter.32.cloned.1.call-start = ((), (), s32[]{:S(2)}) async-start(), calls=%async_computation.37 | async-start | bytes 15728640 | tf_op jit(solution)/shard_map/reduce_scatter | solution.py:151
  2007.3 266.9 %reduce-scatter.50.cloned.1.call-start = ((), (), s32[]{:S(2)}) async-start(), calls=%async_computation.46 | async-start | bytes 10616832 | tf_op jit(solution)/shard_map/reduce_scatter | solution.py:380
  2023.4 417.6 %reduce-scatter.46.cloned.1.call-start = ((), (), s32[]{:S(2)}) async-start(), calls=%async_computation.44 | async-start | bytes 10616832 | tf_op jit(solution)/shard_map/reduce_scatter | solution.py:378
  2040.2 567.4 %reduce-scatter.48.cloned.1.call-start = ((), (), s32[]{:S(2)}) async-start(), calls=%async_computation.45 | async-start | bytes 10616832 | tf_op jit(solution)/shard_map/reduce_scatter | solution.py:379
  2055.9 618.8 %reduce-scatter.54.cloned.1.call-start = ((), (), s32[]{:S(2)}) async-start(), calls=%async_computation.48 | async-start | bytes 1327104
  2058.6 683.0 %reduce-scatter.52.cloned.1.call-start = ((), (), s32[]{:S(2)}) async-start(), calls=%async_computation.47 | async-start | bytes 1327104
  2060.4 753.1 %reduce-scatter.42.cloned.1.call-start = ((), (), s32[]{:S(2)}) async-start(), calls=%async_computation.42 | async-start | bytes 2654208 | tf_op jit(solution)/shard_map/reduce_scatter | solution.py:374
  2068.6 817.1 %reduce-scatter.44.cloned.1.call-start = ((), (), s32[]{:S(2)}) async-start(), calls=%async_computation.43 | async-start | bytes 2654208 | tf_op jit(solution)/shard_map/reduce_scatter | solution.py:377
  2076.4 881.4 %reduce-scatter.40.cloned.1.call-start = ((), (), s32[]{:S(2)}) async-start(), calls=%async_computation.41 | async-start | bytes 2654208 | tf_op jit(solution)/shard_map/reduce_scatter | solution.py:373
  2084.3 8.5 copy-start.20
  2084.3 945.5 %reduce-scatter.38.cloned.1.call-start = ((), (), s32[]{:S(2)}) async-start(), calls=%async_computation.40 | async-start | bytes 2654208 | tf_op jit(solution)/shard_map/reduce_scatter | solution.py:372
  2092.8 8.4 copy-start.17
  2092.8 1009.2 %reduce-scatter.36.cloned.1.call-start = ((), (), s32[]{:S(2)}) async-start(), calls=%async_computation.39 | async-start | bytes 2654208 | tf_op jit(solution)/shard_map/reduce_scatter | solution.py:371
  2101.1 9.1 copy-start.44
  2101.1 9.1 copy-start.53
  2101.1 10.9 copy-start.50
  2101.1 10.9 copy-start.57
  2101.1 10.9 copy-start.63
  2101.1 1073.0 %reduce-scatter.34.cloned.1.call-start = ((), (), s32[]{:S(2)}) async-start(), calls=%async_computation.38 | async-start | bytes 2654208 | tf_op jit(solution)/shard_map/reduce_scatter | solution.py:370
  2108.9 1191.4 %all-reduce.7.cloned.1.call-start = ((), (), s32[]{:S(2)}) async-start(), calls=%async_computation.49 | async-start | bytes 147456 | tf_op jit(solution)/shard_map/psum | solution.py:366
  (60 other events, 165.2 us)
Sparse Core Ops, SparseCore 0:
  10.2 44.0 all-gather.19
  56.5 39.8 all-gather.17
  98.5 39.8 all-gather.21
  140.4 45.1 all-gather.15
  187.6 41.0 all-gather.23
  355.9 99.0 reduce-scatter.21
  457.2 45.9 all-gather.27
  505.3 43.9 all-gather.25
  551.5 41.0 all-gather.29
  602.5 97.7 reduce-scatter.23
  702.6 80.1 all-gather.35
  784.8 44.5 all-gather.31
  831.5 79.8 all-gather.33
  913.5 78.0 all-gather.37
  992.9 44.5 all-gather.39
  1096.5 99.0 reduce-scatter.27
  1198.0 99.0 reduce-scatter.25
  1303.1 46.3 all-gather.41
  1401.6 99.0 reduce-scatter.29
  1507.5 46.3 all-gather.43
  2007.4 99.0 reduce-scatter.31
  2110.7 163.4 reduce-scatter.49
  2278.3 162.5 reduce-scatter.45
  2445.0 162.5 reduce-scatter.47
  2611.5 63.1 reduce-scatter.53
  2678.5 63.0 reduce-scatter.51
  2745.5 67.9 reduce-scatter.41
  2817.6 68.0 reduce-scatter.43
  2889.8 68.0 reduce-scatter.39
  2961.8 68.0 reduce-scatter.37
  3033.9 68.0 reduce-scatter.35
  3106.1 68.0 reduce-scatter.33
  3181.8 118.5 all-reduce.6
where the time goes:
time: 3320 us; the launch traced here: 3310 us
  waiting for transfers between devices  2160 us (65%)
  matrix products  656 us (20%)
  other arithmetic  189 us (6%)
  local copies, waits for them, and re-layouts  153 us (5%)
  blocking collectives  126 us (4%)
    reduce_scatter x3, waiting for transfers between devices, branch_total(): lax.psum_scatter(term.reshape(share_rows * lax.axis_size('mp'), -1), 'mp'...  293 us
    reduce_scatter x3, waiting for transfers between devices, input_total(): lax.psum_scatter(term.reshape(share_rows * lax.axis_size('mp'), -1), 'mp'...  181 us
    reduce_scatter x1, waiting for transfers between devices, per_device(): lax.psum_scatter(grad_gate, 'dp', scatter_dimension=0, tiled=True)  167 us
    reduce_scatter x1, waiting for transfers between devices, per_device(): lax.psum_scatter(grad_up, 'dp', scatter_dimension=0, tiled=True)  167 us
    reduce_scatter x1, waiting for transfers between devices, per_device(): lax.psum_scatter(grad_down, 'dp', scatter_dimension=0, tiled=True)  151 us
    unnamed x35, waiting for transfers between devices  140 us
    all_gather x3, waiting for transfers between devices, spread_grads(): return lax.all_gather(share, 'mp', axis=0, tiled=True)  139 us
    psum x1, waiting for transfers between devices, per_device(): lax.psum((cond_local, grad_first_frames + grad_first_cond, grad_second, g...  126 us
  transfers between devices with their start and end apart: 33, of which 29 were waited for; matrix products, arithmetic and copies ran while one was open for 12% of the time, Pallas kernels for 0%

commit v1 on v0

v1 whole, which is shorter than its diff:
```python
import functools

import jax
import jax.numpy as jnp
from jax import lax
from jax.experimental import pallas as pl
from jax.experimental.pallas import tpu as pltpu
from jax.sharding import PartitionSpec as P

HD = 64
ROT = 32
LOG2E = 1.4426950408889634
EPS = 1e-05
MESH = pl.DeviceIdType.MESH
NT = (((1,), (1,)), ((), ()))
TN = (((0,), (0,)), ((), ()))
NN = (((1,), (0,)), ((), ()))
BF = jnp.bfloat16
F32 = jnp.float32
ANY = pl.BlockSpec(memory_space=pl.ANY)
VM = 58 << 20


def shape_of(dims, dtype):
    return jax.ShapeDtypeStruct(dims, dtype)


def dot(left, right, dims):
    return lax.dot_general(left, right, dims, preferred_element_type=F32)


def local_params(**extra):
    return pltpu.CompilerParams(vmem_limit_bytes=VM, **extra)


def cost(flops, nbytes, trans=0):
    return pl.CostEstimate(flops=int(flops), bytes_accessed=int(nbytes), transcendentals=int(trans))


def norm_rows(values):
    center = values - jnp.mean(values, -1, keepdims=True)
    spread = lax.rsqrt(jnp.mean(center * center, -1, keepdims=True) + EPS)
    return center * spread, spread


def norm_back(grad_rows, unit_rows, spread, gain_row):
    scaled = grad_rows * gain_row
    result = spread * (
        scaled
        - jnp.mean(scaled, -1, keepdims=True)
        - unit_rows * jnp.mean(scaled * unit_rows, -1, keepdims=True)
    )
    return result, jnp.sum(grad_rows * unit_rows, 0, keepdims=True)


def rope_tables(length, offset):
    lane = jnp.arange(2 * HD) % HD
    half = ROT // 2
    frequency = jnp.power(10000.0, -2.0 * (lane % half).astype(F32) / ROT)
    angles = (offset + jnp.arange(length).astype(F32))[:, None] * frequency[None, :]
    cosine = jnp.where(lane[None] < ROT, jnp.cos(angles), 1.0)
    sine = jnp.sin(angles)
    upper = jnp.where((lane[None] >= half) & (lane[None] < ROT), sine, 0.0)
    lower = jnp.where(lane[None] < half, -sine, 0.0)
    return cosine, upper, lower


def rope(values, cosine, upper, lower):
    half = ROT // 2
    return (
        values * cosine
        + pltpu.roll(values, half, 1) * upper
        + pltpu.roll(values, 2 * HD - half, 1) * lower
    )


def lanes(dims):
    return lax.broadcasted_iota(jnp.int32, dims, 1)


def half_mask(values, head):
    lane = lanes(values.shape)
    keep = (lane < HD) if head == 0 else (lane >= HD)
    return jnp.where(keep, values, jnp.zeros_like(values))


def pieces(column, dims, base):
    high = column.astype(BF).astype(F32)
    rest = column - high
    middle = rest.astype(BF).astype(F32)
    low = rest - middle
    lane = lanes(dims)
    return jnp.where(
        lane == base,
        high,
        jnp.where(lane == base + 1, middle, jnp.where(lane == base + 2, low, 0.0)),
    )


def mp_peers():
    me = lax.axis_index("mp")
    chip, core = me // 2, me % 2
    return me, chip * 2 + (1 - core), (1 - chip) * 2 + core, (1 - chip) * 2 + (1 - core)


def greet(devices):
    barrier = pltpu.get_barrier_semaphore()
    for device in devices:
        pl.semaphore_signal(barrier, inc=1, device_id=device, device_id_type=MESH)
    pl.semaphore_wait(barrier, len(devices))


def remote(source, target, send, recv, device):
    return pltpu.make_async_remote_copy(
        source, target, send, recv, device_id=device, device_id_type=MESH
    )


CHUNKS = 4


class Gather:
    def __init__(self, x_ref, o_ref, lsem, ssem, rsem):
        self.me, self.sib, self.far, self.diag = mp_peers()
        dp = lax.axis_index("dp")
        self.to_sib = {"dp": dp, "mp": self.sib}
        self.to_far = {"dp": dp, "mp": self.far}
        rows = x_ref.shape[0]
        part = rows // CHUNKS

        def slot(i, k):
            return o_ref.at[pl.ds(pl.multiple_of(i * rows + k * part, part), part)]

        self.own = pltpu.make_async_copy(
            x_ref, o_ref.at[pl.ds(pl.multiple_of(self.me * rows, rows), rows)], lsem
        )
        self.across = []
        self.beside = []
        self.onward = []
        for k in range(CHUNKS):
            mine = x_ref.at[pl.ds(k * part, part)]
            self.across.append(
                remote(mine, slot(self.me, k), ssem.at[0, k], rsem.at[0, k], self.to_far)
            )
            self.beside.append(
                remote(mine, slot(self.me, k), ssem.at[1, k], rsem.at[1, k], self.to_sib)
            )
            self.onward.append(
                remote(
                    slot(self.far, k), slot(self.far, k), ssem.at[2, k], rsem.at[2, k], self.to_sib
                )
            )

    def start(self):
        for copy in self.across:
            copy.start()
        self.own.start()
        for copy in self.beside:
            copy.start()

    def forward(self, k):
        self.across[k].wait_recv()
        self.onward[k].start()

    def finish(self):
        for k in range(CHUNKS):
            self.beside[k].wait_recv()
            self.onward[k].wait_recv()
        for k in range(CHUNKS):
            self.across[k].wait_send()
            self.beside[k].wait_send()
            self.onward[k].wait_send()
        self.own.wait()


GATHER_SEMS = [
    pltpu.SemaphoreType.DMA(()),
    pltpu.SemaphoreType.DMA((3, CHUNKS)),
    pltpu.SemaphoreType.DMA((3, CHUNKS)),
]


def gather_kernel(x_ref, o_ref, lsem, ssem, rsem):
    job = Gather(x_ref, o_ref, lsem, ssem, rsem)
    greet([job.to_sib, job.to_far])
    job.start()
    for k in range(CHUNKS):
        job.forward(k)
    job.finish()


def gather_rows(share, ident):
    rows, width = share.shape
    return pl.pallas_call(
        gather_kernel,
        out_shape=shape_of((4 * rows, width), share.dtype),
        in_specs=[ANY],
        out_specs=ANY,
        scratch_shapes=GATHER_SEMS,
        compiler_params=local_params(collective_id=ident, has_side_effects=True),
        name="gather_rows_%d" % ident,
    )(share)


def head_kernel(count, f_ref, w_ref, fo_ref, wo_ref, lsem, ssem, rsem, wl, fs, fr, bs, br):
    job = Gather(f_ref, fo_ref, lsem, ssem, rsem)
    me = lax.axis_index("dp")
    mp = lax.axis_index("mp")
    rows = w_ref.shape[0]

    def ring_at(spot):
        spot = (spot + count) % count
        late = spot // (count // 2)
        return (1 - late) * 2 * spot + late * (2 * (count - 1 - spot) + 1)

    odd = me % 2
    spot = (1 - odd) * (me // 2) + odd * (count - 1 - me // 2)
    ahead = {"dp": ring_at(spot + 1), "mp": mp}
    behind = {"dp": ring_at(spot - 1), "mp": mp}
    greet([job.to_sib, job.to_far, ahead, behind])

    def slot(i):
        return wo_ref.at[pl.ds(pl.multiple_of(i * rows, rows), rows)]

    half = count // 2
    forward = []
    backward = []
    for hop in range(half):
        block = ring_at(spot - hop)
        forward.append(
            remote(w_ref if hop == 0 else slot(block), slot(block), fs.at[hop], fr.at[hop], ahead)
        )
        block = ring_at(spot + hop)
        backward.append(
            remote(w_ref if hop == 0 else slot(block), slot(block), bs.at[hop], br.at[hop], behind)
        )
    forward[0].start()
    backward[0].start()
    job.start()
    own = pltpu.make_async_copy(w_ref, slot(me), wl)
    own.start()
    for hop in range(1, half):
        forward[hop - 1].wait_recv()
        forward[hop].start()
        backward[hop - 1].wait_recv()
        if hop < half - 1:
            backward[hop].start()
        if hop - 1 < CHUNKS:
            job.forward(hop - 1)
    for k in range(min(half - 1, CHUNKS), CHUNKS):
        job.forward(k)
    forward[half - 1].wait_recv()
    job.finish()
    own.wait()
    for hop in range(half):
        forward[hop].wait_send()
        if hop < half - 1:
            backward[hop].wait_send()


def head_gather(frames, packed, count):
    rows, width = frames.shape
    half = count // 2
    sems = [pltpu.SemaphoreType.DMA((half,))] * 4
    return pl.pallas_call(
        functools.partial(head_kernel, count),
        out_shape=(
            shape_of((4 * rows, width), BF),
            shape_of((count * packed.shape[0], packed.shape[1]), BF),
        ),
        in_specs=[ANY, ANY],
        out_specs=(ANY, ANY),
        scratch_shapes=GATHER_SEMS + [pltpu.SemaphoreType.DMA(())] + sems,
        compiler_params=local_params(collective_id=0, has_side_effects=True),
        name="head_gather",
    )(frames, packed)


def scatter_kernel(x_ref, o_ref, mine, ra, rb, rc, sb, lsem, ssem, rsem):
    me, sib, far, diag = mp_peers()
    dp = lax.axis_index("dp")
    to_sib = {"dp": dp, "mp": sib}
    to_far = {"dp": dp, "mp": far}
    rows = o_ref.shape[0]
    part = rows // CHUNKS
    greet([to_sib, to_far])

    def slot(i, k):
        return x_ref.at[pl.ds(pl.multiple_of(i * rows + k * part, part), part)]

    def piece(ref, k):
        return ref.at[pl.ds(k * part, part)]

    def whole(i):
        return x_ref.at[pl.ds(pl.multiple_of(i * rows, rows), rows)]

    first = [
        remote(slot(diag, k), piece(ra, k), ssem.at[0, k], rsem.at[0, k], to_sib)
        for k in range(CHUNKS)
    ]
    second = [
        remote(slot(sib, k), piece(rb, k), ssem.at[1, k], rsem.at[1, k], to_sib)
        for k in range(CHUNKS)
    ]
    third = [
        remote(piece(sb, k), piece(rc, k), ssem.at[2, k], rsem.at[2, k], to_far)
        for k in range(CHUNKS)
    ]
    load0 = pltpu.make_async_copy(whole(far), mine.at[0], lsem.at[0])
    load1 = pltpu.make_async_copy(whole(me), mine.at[1], lsem.at[1])
    load0.start()
    for copy in first:
        copy.start()
    load1.start()
    for copy in second:
        copy.start()
    load0.wait()
    for k in range(CHUNKS):
        first[k].wait_recv()
        span = pl.ds(k * part, part)
        sb[span, :] = (mine[0, span, :].astype(F32) + ra[span, :].astype(F32)).astype(BF)
        third[k].start()
    load1.wait()
    for k in range(CHUNKS):
        second[k].wait_recv()
        span = pl.ds(k * part, part)
        o_ref[span, :] = mine[1, span, :].astype(F32) + rb[span, :].astype(F32)
    for k in range(CHUNKS):
        third[k].wait_recv()
        span = pl.ds(k * part, part)
        o_ref[span, :] += rc[span, :].astype(F32)
    for k in range(CHUNKS):
        first[k].wait_send()
        second[k].wait_send()
        third[k].wait_send()


def scatter_rows(term, ident):
    rows, width = term.shape[0] // 4, term.shape[1]
    return pl.pallas_call(
        scatter_kernel,
        out_shape=shape_of((rows, width), F32),
        in_specs=[ANY],
        out_specs=pl.BlockSpec(memory_space=pltpu.VMEM),
        scratch_shapes=[pltpu.VMEM((2, rows, width), BF)]
        + [pltpu.VMEM((rows, width), BF)] * 4
        + [
            pltpu.SemaphoreType.DMA((2,)),
            pltpu.SemaphoreType.DMA((3, CHUNKS)),
            pltpu.SemaphoreType.DMA((3, CHUNKS)),
        ],
        compiler_params=local_params(collective_id=ident, has_side_effects=True),
        name="scatter_rows_%d" % ident,
    )(term)


def qkv_kernel(x_ref, g_ref, w_ref, c_ref, u_ref, l_ref, n_ref, q_ref, k_ref, v_ref):
    unit, _ = norm_rows(x_ref[...].astype(F32))
    normed = (unit * g_ref[...]).astype(BF)
    n_ref[...] = normed
    width = q_ref.shape[1]
    out = dot(normed, w_ref[...], NN)
    cosine, upper, lower = c_ref[...], u_ref[...], l_ref[...]
    for pair in range(width // 128):
        span = slice(128 * pair, 128 * pair + 128)
        q_ref[:, span] = (rope(out[:, span], cosine, upper, lower) * (LOG2E / 8.0)).astype(BF)
        keys = out[:, width + 128 * pair : width + 128 * pair + 128]
        k_ref[:, span] = rope(keys, cosine, upper, lower).astype(BF)
    v_ref[...] = out[:, 2 * width : 3 * width].astype(BF)


def qkv_project(frames, gain, weights, tables, width):
    length, model = frames.shape
    rows = 256
    block = pl.BlockSpec((rows, model), lambda i: (i, 0))
    table = pl.BlockSpec((rows, 128), lambda i: (i, 0))
    head = pl.BlockSpec((rows, width), lambda i: (i, 0))
    return pl.pallas_call(
        qkv_kernel,
        grid=(length // rows,),
        in_specs=[
            block,
            pl.BlockSpec((1, model), lambda i: (0, 0)),
            pl.BlockSpec((model, 3 * width), lambda i: (0, 0)),
            table,
            table,
            table,
        ],
        out_specs=[block, head, head, head],
        out_shape=[shape_of((length, model), BF)] + [shape_of((length, width), BF)] * 3,
        compiler_params=local_params(),
        cost_estimate=cost(6 * length * model * width, 8 * length * model),
        name="qkv_project",
    )(frames, gain, weights, *tables)


def attend_kernel(bk, q_ref, k_ref, v_ref, k0_ref, v0_ref, o_ref, aug_ref, vaug):
    length = k_ref.shape[0]
    bq = q_ref.shape[0]

    @pl.when(pl.program_id(1) == 0)
    def _():
        vaug[:, :128] = v_ref[...]
        vaug[:, 128:] = jnp.ones((length, 128), BF)

    queries = q_ref[...]
    key0 = k0_ref[0:1, :].astype(F32)
    value0 = v0_ref[0:1, :].astype(F32)
    outs = []
    logs = []
    for head in range(2):
        masked = half_mask(queries, head)
        peak = jnp.sum(masked.astype(F32) * key0, axis=1, keepdims=True)
        total = jnp.concatenate(
            [jnp.broadcast_to(value0, (bq, 128)), jnp.ones((bq, 128), F32)], 1
        )
        for block in range(length // bk):
            span = slice(block * bk, (block + 1) * bk)
            scores = dot(masked, k_ref[span, :], NT)
            higher = jnp.maximum(peak, jnp.max(scores, axis=1, keepdims=True))
            exponent = jnp.exp2(scores - higher).astype(BF)
            total = total * jnp.exp2(peak - higher) + dot(exponent, vaug[span, :], NN)
            peak = higher
        weight = total[:, 128:129]
        outs.append(total[:, :128] * (1.0 / weight))
        logs.append(-(peak + jnp.log2(weight)))
    lane = lanes((bq, 128))
    o_ref[...] = jnp.where(lane < HD, outs[0], outs[1]).astype(BF)
    aug_ref[...] = (pieces(logs[0], (bq, 128), 0) + pieces(logs[1], (bq, 128), HD)).astype(BF)


def attend(queries, keys, values, key0, value0, bq=512, bk=1024):
    length, width = queries.shape
    row = pl.BlockSpec((bq, 128), lambda p, i: (i, p))
    full = pl.BlockSpec((length, 128), lambda p, i: (0, p))
    zero = pl.BlockSpec((16, 128), lambda p, i: (0, p))
    return pl.pallas_call(
        functools.partial(attend_kernel, bk),
        grid=(width // 128, length // bq),
        in_specs=[row, full, full, zero, zero],
        out_specs=[row, row],
        out_shape=[shape_of((length, width), BF)] * 2,
        scratch_shapes=[pltpu.VMEM((length, 256), BF)],
        compiler_params=local_params(),
        cost_estimate=cost(16 * length * length * width, 10 * length * width),
        name="attend",
    )(queries, keys, values, key0, value0)


def attend_back_kernel(
    bk, q_ref, aug_ref, o_ref, do_ref, k_ref, v_ref, k0_ref, v0_ref,
    cq_ref, uq_ref, lq_ref, ck_ref, uk_ref, lk_ref,
    dq_ref, dk_ref, dv_ref, dk0_ref, dv0_ref, kaug, vaug, kt, dka, dva,
):
    length = k_ref.shape[0]
    bq = q_ref.shape[0]
    step = pl.program_id(1)

    @pl.when(step == 0)
    def _():
        lane = lanes((length, 128))
        ones = jnp.where((lane % HD) < 3, 1.0, 0.0).astype(BF)
        kaug[:, :128] = k_ref[...]
        kaug[:, 128:] = ones
        vaug[:, :128] = v_ref[...]
        vaug[:, 128:] = ones
        kt[...] = k_ref[...].astype(F32).T.astype(BF)
        dka[...] = jnp.zeros_like(dka)
        dva[...] = jnp.zeros_like(dva)
        dk0_ref[...] = jnp.zeros_like(dk0_ref)
        dv0_ref[...] = jnp.zeros_like(dv0_ref)

    queries = q_ref[...]
    grads = do_ref[...]
    aug = aug_ref[...]
    product = grads.astype(F32) * o_ref[...].astype(F32)
    lane = lanes((bq, 128))
    ones0 = jnp.where((lanes((16, 128)) % HD) < 3, 1.0, 0.0).astype(BF)
    key0 = jnp.concatenate([k0_ref[...], ones0], 1)
    value0 = jnp.concatenate([v0_ref[...], ones0], 1)
    row0 = lax.broadcasted_iota(jnp.int32, (16, bq), 0) == 0
    qa, da, qm, dm, dq = [], [], [], [], []
    for head in range(2):
        qm.append(half_mask(queries, head))
        dm.append(half_mask(grads, head))
        mine = (lane < HD) if head == 0 else (lane >= HD)
        inner = jnp.sum(jnp.where(mine, product, 0.0), axis=1, keepdims=True)
        qa.append(jnp.concatenate([qm[head], half_mask(aug, head)], 1))
        da.append(
            jnp.concatenate([dm[head], pieces(-inner, (bq, 128), HD * head).astype(BF)], 1)
        )
        prob0 = jnp.where(row0, jnp.exp2(dot(key0, qa[head], NT)), 0.0)
        ds0 = (prob0 * dot(value0, da[head], NT)).astype(BF)
        dv0_ref[...] += dot(prob0.astype(BF), dm[head], NN)
        dk0_ref[...] += dot(ds0, qm[head], NN)
        dq.append(dot(k0_ref[:, HD * head : HD * head + HD], ds0, TN))
    for block in range(length // bk):
        span = slice(block * bk, (block + 1) * bk)
        for head in range(2):
            probs = jnp.exp2(dot(kaug[span, :], qa[head], NT))
            ds = (probs * dot(vaug[span, :], da[head], NT)).astype(BF)
            dva[span, :] += dot(probs.astype(BF), dm[head], NN)
            dka[span, :] += dot(ds, qm[head], NN)
            dq[head] = dq[head] + dot(kt[HD * head : HD * head + HD, span], ds, NN)
    grad_q = jnp.concatenate(dq, 0).T * 0.125
    dq_ref[...] = rope(grad_q, cq_ref[...], -uq_ref[...], -lq_ref[...]).astype(BF)

    @pl.when(step == pl.num_programs(1) - 1)
    def _():
        grad_k = dka[...] * (1.0 / LOG2E)
        dk_ref[...] = rope(grad_k, ck_ref[...], -uk_ref[...], -lk_ref[...]).astype(BF)
        dv_ref[...] = dva[...].astype(BF)
        dk0_ref[...] = dk0_ref[...] * (1.0 / LOG2E)


def attend_back(queries, aug, mixed, grads, keys, values, key0, value0, tables, bq=512, bk=512):
    length, width = queries.shape
    row = pl.BlockSpec((bq, 128), lambda p, i: (i, p))
    full = pl.BlockSpec((length, 128), lambda p, i: (0, p))
    zero = pl.BlockSpec((16, 128), lambda p, i: (0, p))
    tq = pl.BlockSpec((bq, 128), lambda p, i: (i, 0))
    tk = pl.BlockSpec((length, 128), lambda p, i: (0, 0))
    big = shape_of((length, width), BF)
    small = shape_of((16, width), F32)
    return pl.pallas_call(
        functools.partial(attend_back_kernel, bk),
        grid=(width // 128, length // bq),
        in_specs=[row, row, row, row, full, full, zero, zero, tq, tq, tq, tk, tk, tk],
        out_specs=[row, full, full, zero, zero],
        out_shape=[big, big, big, small, small],
        scratch_shapes=[pltpu.VMEM((length, 256), BF)] * 2
        + [pltpu.VMEM((128, length), BF)]
        + [pltpu.VMEM((length, 128), F32)] * 2,
        compiler_params=local_params(),
        cost_estimate=cost(40 * length * length * width, 20 * length * width),
        name="attend_back",
    )(queries, aug, mixed, grads, keys, values, key0, value0, *tables, *tables)


def softmax_keys(scores, length):
    lane = lanes(scores.shape)
    masked = jnp.where(lane < length, scores, -1e9)
    exponent = jnp.exp2(masked - jnp.max(masked, axis=1, keepdims=True))
    return exponent * (1.0 / jnp.sum(exponent, axis=1, keepdims=True))


def cross_kernel(
    len_ref, f_ref, s_ref, g2_ref, g3_ref, wq_ref, wo_ref, kv_ref,
    as_ref, n2_ref, q_ref, m_ref, ac_ref, n3_ref,
):
    groups, model, width = wq_ref.shape
    after_self = f_ref[...].astype(F32) + s_ref[...]
    as_ref[...] = after_self
    unit, _ = norm_rows(after_self)
    normed = (unit * g2_ref[...]).astype(BF)
    n2_ref[...] = normed
    rows = normed.shape[0]
    lane = lanes((rows, 128))
    total = after_self
    for group in range(groups):
        queries = (dot(normed, wq_ref[group], NN) * (LOG2E / 8.0)).astype(BF)
        base = group * width
        q_ref[:, base : base + width] = queries
        for pair in range(width // 128):
            span = slice(128 * pair, 128 * pair + 128)
            values = kv_ref[group, :, width + 128 * pair : width + 128 * pair + 128]
            outs = []
            for head in range(2):
                scores = dot(half_mask(queries[:, span], head), kv_ref[group, :, span], NT)
                probs = softmax_keys(scores, len_ref[0])
                outs.append(dot(probs.astype(BF), values, NN))
            m_ref[:, base + 128 * pair : base + 128 * pair + 128] = jnp.where(
                lane < HD, outs[0], outs[1]
            ).astype(BF)
        total = total + dot(m_ref[:, base : base + width], wo_ref[group], NT)
    ac_ref[...] = total
    unit, _ = norm_rows(total)
    n3_ref[...] = (unit * g3_ref[...]).astype(BF)


def cross_forward(plen, frames, summed, gain2, gain3, weights, prompt_kv):
    share, model = frames.shape
    groups, _, both = weights.shape
    width = both // 2
    rows = 256
    block = pl.BlockSpec((rows, model), lambda i: (i, 0))
    gain = pl.BlockSpec((1, model), lambda i: (0, 0))
    once = pl.Buffered(1)
    return pl.pallas_call(
        cross_kernel,
        grid=(share // rows,),
        in_specs=[
            pl.BlockSpec(memory_space=pltpu.SMEM),
            block,
            block,
            gain,
            gain,
            pl.BlockSpec((groups, model, width), lambda i: (0, 0, 0), pipeline_mode=once),
            pl.BlockSpec((groups, model, width), lambda i: (0, 0, 1), pipeline_mode=once),
            pl.BlockSpec(prompt_kv.shape, lambda i: (0, 0, 0)),
        ],
        out_specs=[block] * 6,
        out_shape=[
            shape_of((share, model), F32),
            shape_of((share, model), BF),
            shape_of((share, model), BF),
            shape_of((share, model), BF),
            shape_of((share, model), F32),
            shape_of((share, model), BF),
        ],
        compiler_params=local_params(),
        cost_estimate=cost(4 * share * model * model, 4 * model * model + 20 * share * model),
        name="cross_forward",
    )(plen, frames, summed, gain2, gain3, weights, weights, prompt_kv)


def cross_back_kernel(
    len_ref, w_ref, go_ref, e_ref, ac_ref, as_ref, g2_ref, g3_ref, q_ref, wq_ref, wo_ref, kv_ref,
    cb_ref, dq_ref, c3_ref, c3b_ref, dkv_ref, dg2_ref, dg3_ref,
):
    groups, model, width = wq_ref.shape

    @pl.when(pl.program_id(0) == 0)
    def _():
        dkv_ref[...] = jnp.zeros_like(dkv_ref)
        dg2_ref[...] = jnp.zeros_like(dg2_ref)
        dg3_ref[...] = jnp.zeros_like(dg3_ref)

    unit, spread = norm_rows(ac_ref[...])
    back, part = norm_back(e_ref[...], unit, spread, g3_ref[...])
    dg3_ref[...] += part
    carried = go_ref[...].astype(F32) * w_ref[0] + back
    cross_back = carried.astype(BF)
    cb_ref[...] = cross_back
    rows = cross_back.shape[0]
    lane = lanes((rows, 128))
    total = jnp.zeros((rows, model), F32)
    for group in range(groups):
        grads = dot(cross_back, wo_ref[group], NN).astype(BF)
        base = group * width
        for pair in range(width // 128):
            span = slice(128 * pair, 128 * pair + 128)
            vspan = slice(width + 128 * pair, width + 128 * pair + 128)
            wide = slice(base + 128 * pair, base + 128 * pair + 128)
            outs = []
            for head in range(2):
                queries = half_mask(q_ref[:, wide], head)
                masked = half_mask(grads[:, span], head)
                probs = softmax_keys(dot(queries, kv_ref[group, :, span], NT), len_ref[0])
                dprobs = dot(masked, kv_ref[group, :, vspan], NT)
                inner = jnp.sum(dprobs * probs, axis=1, keepdims=True)
                ds = (probs * (dprobs - inner)).astype(BF)
                outs.append(dot(ds, kv_ref[group, :, span], NN))
                dkv_ref[group, :, span] += dot(ds, queries, TN) * (1.0 / LOG2E)
                dkv_ref[group, :, vspan] += dot(probs.astype(BF), masked, TN)
            dq_ref[:, wide] = (jnp.where(lane < HD, outs[0], outs[1]) * 0.125).astype(BF)
        total = total + dot(dq_ref[:, base : base + width], wq_ref[group], NT)
    unit, spread = norm_rows(as_ref[...])
    back, part = norm_back(total, unit, spread, g2_ref[...])
    dg2_ref[...] += part
    carried = carried + back
    c3_ref[...] = carried
    c3b_ref[...] = carried.astype(BF)


def cross_backward(plen, weight, grad_out, summed, after_cross, after_self, gain2, gain3,
                   queries, weights, prompt_kv):
    share, model = grad_out.shape
    groups, _, both = weights.shape
    width = both // 2
    rows = 256
    block = pl.BlockSpec((rows, model), lambda i: (i, 0))
    gain = pl.BlockSpec((1, model), lambda i: (0, 0))
    smem = pl.BlockSpec(memory_space=pltpu.SMEM)
    once = pl.Buffered(1)
    return pl.pallas_call(
        cross_back_kernel,
        grid=(share // rows,),
        in_specs=[
            smem,
            smem,
            block,
            block,
            block,
            block,
            gain,
            gain,
            block,
            pl.BlockSpec((groups, model, width), lambda i: (0, 0, 0), pipeline_mode=once),
            pl.BlockSpec((groups, model, width), lambda i: (0, 0, 1), pipeline_mode=once),
            pl.BlockSpec(prompt_kv.shape, lambda i: (0, 0, 0)),
        ],
        out_specs=[block, block, block, block, pl.BlockSpec(prompt_kv.shape, lambda i: (0, 0, 0)),
                   gain, gain],
        out_shape=[
            shape_of((share, model), BF),
            shape_of((share, model), BF),
            shape_of((share, model), F32),
            shape_of((share, model), BF),
            shape_of(prompt_kv.shape, F32),
            shape_of((1, model), F32),
            shape_of((1, model), F32),
        ],
        compiler_params=local_params(),
        cost_estimate=cost(4 * share * model * model, 4 * model * model + 24 * share * model),
        name="cross_backward",
    )(plen, weight, grad_out, summed, after_cross, after_self, gain2, gain3, queries,
      weights, weights, prompt_kv)


def glu_kernel(n_ref, c_ref, w_ref, h_ref, d_ref):
    width = h_ref.shape[1]
    normed = n_ref[...]
    gate = dot(normed, w_ref[:, :width], NN)
    up = dot(normed, w_ref[:, width : 2 * width], NN)
    grads = dot(c_ref[...], w_ref[:, 2 * width :], NN)
    sig = 1.0 / (1.0 + jnp.exp(-gate))
    silu = gate * sig
    h_ref[...] = (silu * up).astype(BF)
    d_ref[:, :width] = (grads * up * sig * (1.0 + gate * (1.0 - sig))).astype(BF)
    d_ref[:, width:] = (grads * silu).astype(BF)


def glu_block(normed, cot, weights):
    length, model = normed.shape
    width = weights.shape[1] // 3
    rows = 512
    block = pl.BlockSpec((rows, model), lambda i: (i, 0))
    return pl.pallas_call(
        glu_kernel,
        grid=(length // rows,),
        in_specs=[block, block, pl.BlockSpec(weights.shape, lambda i: (0, 0))],
        out_specs=[
            pl.BlockSpec((rows, width), lambda i: (i, 0)),
            pl.BlockSpec((rows, 2 * width), lambda i: (i, 0)),
        ],
        out_shape=[shape_of((length, width), BF), shape_of((length, 2 * width), BF)],
        compiler_params=local_params(),
        cost_estimate=cost(6 * length * model * width, 6 * length * model),
        name="glu_block",
    )(normed, cot, weights)


def sum_kernel(count, *refs):
    total = dot(refs[0][...], refs[count][...], NT)
    for i in range(1, count):
        total = total + dot(refs[i][...], refs[count + i][...], NT)
    refs[2 * count][...] = total.astype(BF)


def sum_products(lefts, rights, column):
    length = lefts[0].shape[0]
    model = rights[0].shape[0]
    rows = 256
    count = len(lefts)
    once = pl.Buffered(1)
    in_specs = [pl.BlockSpec((rows, left.shape[1]), lambda i: (i, 0)) for left in lefts]
    for left, index in zip(lefts, column):
        in_specs.append(
            pl.BlockSpec(
                (model, left.shape[1]), functools.partial(lambda at, i: (0, at), index),
                pipeline_mode=once,
            )
        )
    depth = sum(left.shape[1] for left in lefts)
    return pl.pallas_call(
        functools.partial(sum_kernel, count),
        grid=(length // rows,),
        in_specs=in_specs,
        out_specs=pl.BlockSpec((rows, model), lambda i: (i, 0)),
        out_shape=shape_of((length, model), BF),
        compiler_params=local_params(),
        cost_estimate=cost(2 * length * model * depth, 2 * (length + model) * (depth + model)),
        name="sum_products_%d" % count,
    )(*lefts, *rights)


def weight_grad(left, right):
    return dot(left, right, TN)


def spread_dp(share):
    return lax.all_gather(share, "dp", axis=0, tiled=True)


def owner_sum(term):
    return lax.psum_scatter(term, "dp", scatter_dimension=0, tiled=True)


GLU_PARTS = 3


def per_device(
    frames, cond_table, bucket_ids, prompt, prompt_len,
    attn_query, attn_key, attn_value, attn_out,
    cross_query, cross_key, cross_value, cross_out,
    glu_gate, glu_up, glu_down, first_gain, second_gain, third_gain, grad_out,
):
    groups = lax.axis_size("mp")
    count = lax.axis_size("dp")
    sequences = bucket_ids.shape[0]
    assert sequences == 1 and groups == 4
    share, model = frames.shape
    length = share * groups
    buckets = cond_table.shape[0]
    own_rows, width = attn_query.shape
    hidden = glu_gate.shape[1] // GLU_PARTS

    onehot = (bucket_ids[:, None] == jnp.arange(buckets)[None, :]).astype(F32)
    extra = jnp.concatenate(
        [
            first_gain[:, None],
            second_gain[:, None],
            third_gain[:, None],
            jnp.broadcast_to(onehot.astype(BF), (own_rows, buckets)),
            jnp.zeros((own_rows, 128 - 3 - buckets), BF),
        ],
        1,
    )
    packed = jnp.concatenate([attn_query, attn_key, attn_value, extra], 1)
    frames_all, first = head_gather(frames, packed, count)
    gains = first[:, 3 * width : 3 * width + 3].astype(F32).T
    gain1, gain2, gain3 = gains[0:1], gains[1:2], gains[2:3]
    marks = first[:, 3 * width + 3 : 3 * width + 3 + buckets].reshape(count, own_rows, buckets)
    counts = jnp.sum(marks[:, 0].astype(F32), 0)
    seq_weight = sequences * count / (buckets * jnp.sum(onehot * counts[None, :], 1))

    prompt_pack = jnp.concatenate([cross_key, cross_value], 1).reshape(own_rows, width)
    second = spread_dp(jnp.concatenate([attn_out, cross_query, cross_out, prompt_pack], 1))
    out_full = second[:, :width]
    prompt_full = second[:, 3 * width :].reshape(model // 2, 2 * width)
    cross_full = lax.all_gather(second[:, width : 3 * width], "mp", axis=0, tiled=False)
    kv_local = dot(prompt[0], prompt_full, NN).astype(BF)
    prompt_kv = lax.all_gather(kv_local, "mp", axis=0, tiled=False)
    grad_all = lax.all_gather(grad_out, "mp", axis=0, tiled=True)
    glu_full = []
    for j in range(GLU_PARTS):
        span = slice(j * hidden, (j + 1) * hidden)
        glu_full.append(
            spread_dp(jnp.concatenate([glu_gate[:, span], glu_up[:, span], glu_down[:, span]], 1))
        )
    cot_all = (grad_all.astype(F32) * seq_weight[0]).astype(BF)

    tables = rope_tables(length, 1.0)
    cond_row = dot(onehot.astype(BF), cond_table, NN)
    unit_cond, spread_cond = norm_rows(cond_row)
    normed_cond = (unit_cond * gain1).astype(BF)
    kv0 = dot(normed_cond, first[:, width : 3 * width], NN).astype(BF)
    kv0 = jnp.pad(kv0, ((0, 15), (0, 0)))
    key0, value0 = kv0[:, :width], kv0[:, width:]
    normed_one, queries, keys, values = qkv_project(frames_all, gain1, first, tables, width)
    mixed, aug = attend(queries, keys, values, key0, value0)
    self_out = scatter_rows(sum_products([mixed], [second], [0]), 1)

    after_self, normed_two, cross_q, cross_mixed, after_cross, normed_three = cross_forward(
        prompt_len, frames, self_out, gain2, gain3, cross_full, prompt_kv
    )
    normed_three = gather_rows(normed_three, 2)

    hiddens, dgus, glu_grads = [], [], []
    for j in range(GLU_PARTS):
        h, d = glu_block(normed_three, cot_all, glu_full[j])
        hiddens.append(h)
        dgus.append(d)
        grad = jnp.concatenate([weight_grad(normed_three, d), weight_grad(cot_all, h)], 1)
        glu_grads.append(owner_sum(grad.astype(BF)))
    back_term = scatter_rows(sum_products(dgus, glu_full, [0] * GLU_PARTS), 3)
    out_term = lax.psum_scatter(
        sum_products(hiddens, glu_full, [2] * GLU_PARTS), "mp", scatter_dimension=0, tiled=True
    )
    block_out = (after_cross + out_term.astype(F32)).astype(BF)

    cross_back, grad_cq, carried, carried_low, grad_kv, dg2, dg3 = cross_backward(
        prompt_len, seq_weight, grad_out, back_term, after_cross, after_self, gain2, gain3,
        cross_q, cross_full, prompt_kv,
    )
    carried_all = gather_rows(carried_low, 4)
    cross_term = jnp.concatenate(
        [
            jnp.einsum("rd,rjc->jdc", normed_two, grad_cq.reshape(share, groups, width),
                       preferred_element_type=F32),
            jnp.einsum("rd,rjc->jdc", cross_back, cross_mixed.reshape(share, groups, width),
                       preferred_element_type=F32),
        ],
        2,
    ).astype(BF)
    cross_sum = lax.psum_scatter(cross_term, "mp", scatter_dimension=0, tiled=False)
    grad_kv = lax.psum_scatter(grad_kv, "mp", scatter_dimension=0, tiled=False).astype(BF)
    grad_prompt = dot(prompt[0], grad_kv, TN).astype(BF).reshape(model, width)
    grad_out_weight = weight_grad(carried_all, mixed).astype(BF)
    second_grad = owner_sum(jnp.concatenate([grad_out_weight, cross_sum, grad_prompt], 1))

    grad_mixed = dot(carried_all, out_full, NN).astype(BF)
    dq, dk, dv, dk0, dv0 = attend_back(
        queries, aug, mixed, grad_mixed, keys, values, key0, value0, tables
    )
    dk0 = dk0[:1].astype(BF)
    dv0 = dv0[:1].astype(BF)
    last_term = scatter_rows(sum_products([dq, dk, dv], [first] * 3, [0, 1, 2]), 5)
    edge = normed_cond.astype(F32)
    first_grad = owner_sum(
        jnp.concatenate(
            [
                weight_grad(normed_one, dq),
                weight_grad(normed_one, dk) + edge.T * dk0.astype(F32),
                weight_grad(normed_one, dv) + edge.T * dv0.astype(F32),
            ],
            1,
        ).astype(BF)
    )
    unit_one, spread_one = norm_rows(frames.astype(F32))
    back_one, dg1 = norm_back(last_term, unit_one, spread_one, gain1)
    frames_grad = carried + back_one
    cond_term = dot(dk0, first[:, width : 2 * width], NT) + dot(
        dv0, first[:, 2 * width : 3 * width], NT
    )
    cond_back, dg1_cond = norm_back(cond_term, unit_cond, spread_cond, gain1)
    sums = lax.psum(
        jnp.concatenate([onehot.T * cond_back, dg1 + dg1_cond, dg2, dg3], 0), ("dp", "mp")
    )

    first_grad = first_grad.astype(F32)
    second_grad = second_grad.astype(F32)
    prompt_grad = second_grad[:, 3 * width :].reshape(own_rows // 2, 2 * width)
    glu_grads = [grad.astype(F32) for grad in glu_grads]
    glu_out = [
        jnp.concatenate([grad[:, i * hidden : (i + 1) * hidden] for grad in glu_grads], 1)
        for i in range(3)
    ]
    return (
        block_out,
        frames_grad,
        sums[:buckets],
        first_grad[:, :width],
        first_grad[:, width : 2 * width],
        first_grad[:, 2 * width :],
        second_grad[:, :width],
        second_grad[:, width : 2 * width],
        prompt_grad[:, :width],
        prompt_grad[:, width:],
        second_grad[:, 2 * width : 3 * width],
        glu_out[0],
        glu_out[1],
        glu_out[2],
        sums[buckets],
        sums[buckets + 1],
        sums[buckets + 2],
    )


def solution(mesh):
    both = P(("dp", "mp"), None)
    weight = P("dp", "mp")
    return jax.shard_map(
        per_device,
        mesh=mesh,
        in_specs=(both, P(), P("dp"), P("dp", None, None), P("dp"))
        + (weight,) * 11
        + (P("dp"),) * 3
        + (both,),
        out_specs=(both, both, P()) + (weight,) * 11 + (P(),) * 3,
        check_vma=False,
    )
```

time: 3320 us -> 1530 us (0.46)
  waiting for transfers between devices: 2160 us -> 637 us
  Pallas kernels: 0 us -> 614 us
  matrix products: 656 us -> 94.7 us
  other arithmetic: 189 us -> 56.9 us
  blocking collectives: 126 us -> 8.32 us
  local copies, waits for them, and re-layouts: 153 us -> 88.2 us
    reduce_scatter x15 -> x3, waiting for transfers between devices: 1390 us -> 46.1 us  [the longest x1 46.1 us: per_device(): lax.psum_scatter(sum_products(hiddens, glu_full, [2] * GLU_PARTS), 'mp',...]
    pallas_call x0 -> x18, Pallas kernels: none -> 614 us  [the longest x3 122 us: scatter_rows(): pl.pallas_call(scatter_kernel, out_shape=shape_of((rows, width), F32), in...]
    dot_general x88 -> x19, matrix products: 656 us -> 94.7 us  [the longest x17 87.1 us: dot(): return lax.dot_general(left, right, dims, preferred_element_type=F32)]
    all_gather x15 -> x6, waiting for transfers between devices: 506 us -> 137 us  [the longest x4 137 us: spread_dp(): return lax.all_gather(share, 'dp', axis=0, tiled=True)]
    unnamed x35 -> x20, waiting for transfers between devices: 140 us -> 454 us
    psum x1, waiting for transfers between devices: 126 us -> 0.01 us  [per_device(): lax.psum(jnp.concatenate([onehot.T * cond_back, dg1 + dg1_cond, dg2, dg3]...]
    convert_element_type x24 -> x5, other arithmetic: 103 us -> 9.71 us  [the longest x1 6.67 us: per_device(): cot_all = (grad_all.astype(F32) * seq_weight[0]).astype(BF)]
    dynamic_update_slice x8 -> x0, local copies, waits for them, and re-layouts: 67.5 us -> none  [attend_back(): lax.scan(step, (zeros_keys, zeros_keys), (queries.reshape(block_count, bl...]
  transfers between devices with their start and end apart: 33 -> 15, of which waited for: 29 -> 8; matrix products, arithmetic and copies ran while one was open for 12% -> 15% of each run, Pallas kernels for 0% -> 32%
where the time goes in v1:
time: 1530 us; the launch traced here: 1520 us
  waiting for transfers between devices  637 us (42%)
  Pallas kernels  614 us (40%)
  matrix products  94.7 us (6%)
  local copies, waits for them, and re-layouts  88.2 us (6%)
  other arithmetic  56.9 us (4%)
  between operations  19.7 us (1%)
    unnamed x20, waiting for transfers between devices  454 us
    all_gather x4, waiting for transfers between devices, spread_dp(): return lax.all_gather(share, 'dp', axis=0, tiled=True)  137 us
    pallas_call x3, Pallas kernels, scatter_rows(): pl.pallas_call(scatter_kernel, out_shape=shape_of((rows, width), F32), in...  122 us
    pallas_call x2, Pallas kernels, gather_rows(): pl.pallas_call(gather_kernel, out_shape=shape_of((4 * rows, width), share...  100 us
    dot_general x17, matrix products, dot(): return lax.dot_general(left, right, dims, preferred_element_type=F32)  87.1 us
    pallas_call x1, Pallas kernels, attend_back(): pl.pallas_call(functools.partial(attend_back_kernel, bk), grid=(width //...  86.3 us
    pallas_call x1, Pallas kernels, head_gather(): pl.pallas_call(functools.partial(head_kernel, count), out_shape=(shape_of...  71.8 us
    pallas_call x4, Pallas kernels, sum_products(): pl.pallas_call(functools.partial(sum_kernel, count), grid=(length // rows...  65.9 us
  transfers between devices with their start and end apart: 15, of which 8 were waited for; matrix products, arithmetic and copies ran while one was open for 15% of the time, Pallas kernels for 32%

profile of v1, /device:TPU:0, one launch (start us, length us, event | category | flops | bytes accessed | tf_op | source)
XLA Modules:
  0.0 1520.9 jit_solution(1093783227114402885)
XLA Ops:
  8.3 1.9 pad_maximum_fusion.9
  11.1 82.3 %all-gather.9.cloned.1.call-done.refs_1_ = bf16[1536,1536]{1,0:T(8,128)(2,1)} async-done(((bf16[192,1536]{1,0:T(8,128)(2,1)}), bf16[1536,1536]{1,0:T(8,128)(2,1)}) %all-gather.9.cloned.1.call-update) | async-done | bytes 4718608 | tf_op jit(solution)/shard_map/all_gather | solution.py:783
  93.4 3.2 slice.194
  101.9 71.8 %head_gather.1 = (bf16[2048,1536]{1,0:T(8,128)(2,1)}, bf16[1536,1280]{1,0:T(8,128)(2,1)}) custom-call(bf16[512,1536]{1,0:T(8,128)(2,1)} %f_ref.3, bf16[192,1280]{1,0:T(8,128)(2,1)} %concatenate.53.w_ref), custom_call_target="tpu_custom_call" | custom-call | tf_op jit(solution)/shard_map/head_gather/pallas_call | solution.py:265
  173.8 6.3 copy.72
  184.8 2.8 fusion.32
  191.4 5.8 fusion.35
  197.2 16.4 %qkv_project.1 = (bf16[2048,1536]{1,0:T(8,128)(2,1)}, bf16[2048,384]{1,0:T(8,128)(2,1)}, bf16[2048,384]{1,0:T(8,128)(2,1)}, bf16[2048,384]{1,0:T(8,128)(2,1)}) custom-call(bf16[2048,1536]{1,0:T(8,128)(2,1)} %get-tuple-element.49.x_ref, f32[1,1536]{1,0:T(1,128)} %get-tuple-element.173.g_ref, ...), custom_call_target="tpu_custom_call" | custom-call | flops 7247757312 | bytes 25165824 | tf_op jit(solution)/shard_map/qkv_project/pallas_call | solution.py:378
  213.6 41.7 %attend.1 = (bf16[2048,384]{1,0:T(8,128)(2,1)}, bf16[2048,384]{1,0:T(8,128)(2,1)}) custom-call(bf16[2048,384]{1,0:T(8,128)(2,1)} %get-tuple-element.51.q_ref, bf16[2048,384]{1,0:T(8,128)(2,1)} %get-tuple-element.52.k_ref, bf16[2048,384]{1,0:T(8,128)(2,1)} %get-tuple-element.53.v_ref, bf16[16,384]{1,0:T(8,128)(2,1)} %get-tuple-element.178.k0_ref, ...), custom_call_target="tpu_custom_call" | custom-call | flops 25769803776 | bytes 7864320 | tf_op jit(solution)/shard_map/attend/pallas_call | solution.py:437
  255.3 9.1 sum_products_1.1.x_ref
  264.4 40.7 %scatter_rows_1.1.s_ref = f32[512,1536]{1,0:T(8,128)} custom-call(bf16[2048,1536]{1,0:T(8,128)(2,1)} %sum_products_1.1.x_ref), custom_call_target="tpu_custom_call" | custom-call | tf_op jit(solution)/shard_map/scatter_rows_1/pallas_call | solution.py:340
  307.3 8.3 all-gather.1
  316.8 6.7 multiply_convert_fusion.c_ref
  323.5 21.8 %cross_forward.1 = (f32[512,1536]{1,0:T(8,128)}, bf16[512,1536]{1,0:T(8,128)(2,1)}, bf16[512,1536]{1,0:T(8,128)(2,1)}, bf16[512,1536]{1,0:T(8,128)(2,1)}, f32[51...) custom-call(s32[1]{0:T(128)S(6)} %copy.102.len_ref, bf16[512,1536]{1,0:T(8,128)(2,1)} %f_ref.3, ...), custom_call_target="tpu_custom_call" | custom-call | flops 4831838208 | bytes 25165824 | tf_op jit(solution)/shard_map/cross_forward/pallas_call | solution.py:589
  345.3 49.6 %gather_rows_2.1.n_ref = bf16[2048,1536]{1,0:T(8,128)(2,1)} custom-call(bf16[512,1536]{1,0:T(8,128)(2,1)} %get-tuple-element.56.x_ref), custom_call_target="tpu_custom_call" | custom-call | tf_op jit(solution)/shard_map/gather_rows_2/pallas_call | solution.py:194
  394.9 15.5 %glu_block.3 = (bf16[2048,512]{1,0:T(8,128)(2,1)}, bf16[2048,1024]{1,0:T(8,128)(2,1)}) custom-call(bf16[2048,1536]{1,0:T(8,128)(2,1)} %gather_rows_2.1.n_ref, bf16[2048,1536]{1,0:T(8,128)(2,1)} %multiply_convert_fusion.c_ref, bf16[1536,1536]{1,0:T(8,128)(2,1)} %all-gather.13.cloned.1.call-done.w_ref.refs_3_), custom_call_target="tpu_custom_call" | custom-call | flops 9663676416 | bytes 18874368 | tf_op jit(solution)/shard_map/glu_block/pallas_call | solution.py:729
  410.3 15.5 %glu_block.4 = (bf16[2048,512]{1,0:T(8,128)(2,1)}, bf16[2048,1024]{1,0:T(8,128)(2,1)}) custom-call(bf16[2048,1536]{1,0:T(8,128)(2,1)} %gather_rows_2.1.n_ref, bf16[2048,1536]{1,0:T(8,128)(2,1)} %multiply_convert_fusion.c_ref, bf16[1536,1536]{1,0:T(8,128)(2,1)} %all-gather.15.cloned.1.call-done.w_ref.refs_4_), custom_call_target="tpu_custom_call" | custom-call | flops 9663676416 | bytes 18874368 | tf_op jit(solution)/shard_map/glu_block/pallas_call | solution.py:729
  425.9 54.9 %all-gather.17.cloned.1.call-done.w_ref.refs_5_ = bf16[1536,1536]{1,0:T(8,128)(2,1)} async-done(((bf16[192,1536]{1,0:T(8,128)(2,1)}), bf16[1536,1536]{1,0:T(8,128)(2,1)}) %all-gather.17.cloned.1.call-update) | async-done | bytes 4718608 | tf_op jit(solution)/shard_map/all_gather | solution.py:783
  480.8 15.6 %glu_block.5 = (bf16[2048,512]{1,0:T(8,128)(2,1)}, bf16[2048,1024]{1,0:T(8,128)(2,1)}) custom-call(bf16[2048,1536]{1,0:T(8,128)(2,1)} %gather_rows_2.1.n_ref, bf16[2048,1536]{1,0:T(8,128)(2,1)} %multiply_convert_fusion.c_ref, bf16[1536,1536]{1,0:T(8,128)(2,1)} %all-gather.17.cloned.1.call-done.w_ref.refs_5_), custom_call_target="tpu_custom_call" | custom-call | flops 9663676416 | bytes 18874368 | tf_op jit(solution)/shard_map/glu_block/pallas_call | solution.py:729
  496.4 26.6 %sum_products_3.4.x_ref = bf16[2048,1536]{1,0:T(8,128)(2,1)} custom-call(bf16[2048,1024]{1,0:T(8,128)(2,1)} %get-tuple-element.60.refs_0_, bf16[2048,1024]{1,0:T(8,128)(2,1)} %get-tuple-element.61.refs_1_, bf16[2048,1024]{1,0:T(8,128)(2,1)} %get-tuple-element.62.refs_2_, bf16[1536,1536]{1,0:T(8,128)(2,1)} %all-gather.13.cloned.1.call-done.w_ref.refs_3_, ...), custom_call_target="tpu_custom_call" | custom-call | flops 19327352832 | bytes 33030144 | tf_op jit(solution)/shard_map/sum_products_3/pallas_call | solution.py:766
  523.0 40.7 %scatter_rows_3.1.e_ref = f32[512,1536]{1,0:T(8,128)} custom-call(bf16[2048,1536]{1,0:T(8,128)(2,1)} %sum_products_3.4.x_ref), custom_call_target="tpu_custom_call" | custom-call | tf_op jit(solution)/shard_map/scatter_rows_3/pallas_call | solution.py:340
  563.7 41.7 %cross_backward.1 = (bf16[512,1536]{1,0:T(8,128)(2,1)}, bf16[512,1536]{1,0:T(8,128)(2,1)}, f32[512,1536]{1,0:T(8,128)}, bf16[512,1536]{1,0:T(8,128)(2,1)}, f32[4...) custom-call(s32[1]{0:T(128)S(6)} %copy.102.len_ref, f32[1]{0:T(128)} %bitcast.8.w_ref, ...), custom_call_target="tpu_custom_call" | custom-call | flops 4831838208 | bytes 28311552 | tf_op jit(solution)/shard_map/cross_backward/pallas_call | solution.py:676
  605.6 3.0 copy.88
  609.2 4.7 convert_bitcast_fusion.1
  614.0 2.8 convert_bitcast_fusion
  616.8 3.9 pad_maximum_fusion
  623.0 50.4 %gather_rows_4.1 = bf16[2048,1536]{1,0:T(8,128)(2,1)} custom-call(bf16[512,1536]{1,0:T(8,128)(2,1)} %get-tuple-element.67.x_ref), custom_call_target="tpu_custom_call" | custom-call | tf_op jit(solution)/shard_map/gather_rows_4/pallas_call | solution.py:194
  673.4 7.7 convolution_convert_fusion.8.do_ref
  681.1 86.3 %attend_back.1 = (bf16[2048,384]{1,0:T(8,128)(2,1)}, bf16[2048,384]{1,0:T(8,128)(2,1)}, bf16[2048,384]{1,0:T(8,128)(2,1)}, f32[16,384]{1,0:T(8,128)}, f32[16,384]{1,0:T(8,128)}) custom-call(bf16[2048,384]{1,0:T(8,128)(2,1)} %get-tuple-element.51.q_ref, bf16[2048,384]{1,0:T(8,128)(2,1)} %get-tuple-element.66.aug_ref, ...), custom_call_target="tpu_custom_call" | custom-call | flops 64424509440 | bytes 15728640 | tf_op jit(solution)/shard_map/attend_back/pallas_call | solution.py:525
  768.9 15.0 sum_products_3.5.x_ref
  783.9 40.7 %scatter_rows_5.1 = f32[512,1536]{1,0:T(8,128)} custom-call(bf16[2048,1536]{1,0:T(8,128)(2,1)} %sum_products_3.5.x_ref), custom_call_target="tpu_custom_call" | custom-call | tf_op jit(solution)/shard_map/scatter_rows_5/pallas_call | solution.py:340
  828.1 3.1 fusion.9
  834.0 6.0 convolution_convert_fusion.7
  840.0 6.6 fusion.11
  846.7 3.7 fusion.12
  850.4 3.2 pad_maximum_fusion.5
  853.6 5.8 copy.90
  859.7 7.0 convolution_convert_fusion.5
  866.8 9.1 convolution_convert_fusion.2
  875.9 2.5 pad_maximum_fusion.2
  878.4 6.6 copy.94
  885.3 7.0 convolution_convert_fusion.4
  892.4 9.1 convolution_convert_fusion.1
  901.5 2.4 pad_maximum_fusion.3
  903.9 6.6 copy.96
  911.1 7.0 convolution_convert_fusion.3
  918.1 9.1 convolution_convert_fusion
  927.2 2.5 pad_maximum_fusion.4
  929.8 6.6 copy.98
  936.5 15.2 %sum_products_3.3 = bf16[2048,1536]{1,0:T(8,128)(2,1)} custom-call(bf16[2048,512]{1,0:T(8,128)(2,1)} %get-tuple-element.57.refs_0_, bf16[2048,512]{1,0:T(8,128)(2,1)} %get-tuple-element.58.refs_1_, bf16[2048,512]{1,0:T(8,128)(2,1)} %get-tuple-element.59.refs_2_, bf16[1536,1536]{1,0:T(8,128)(2,1)} %all-gather.13.cloned.1.call-done.w_ref.refs_3_, ...), custom_call_target="tpu_custom_call" | custom-call | flops 9663676416 | bytes 22020096 | tf_op jit(solution)/shard_map/sum_products_3/pallas_call | solution.py:766
  953.1 6.4 convolution_convert_fusion.6
  962.5 3.0 reshape.213
  967.1 3.8 pad_maximum_fusion.1
  970.9 6.6 copy.92
  977.5 5.5 fusion.8
  986.0 66.6 %reduce-scatter.25.cloned.1.call-done = bf16[192,1152]{1,0:T(8,128)(2,1)} async-done(((bf16[1536,1152]{1,0:T(8,128)(2,1)}), bf16[192,1152]{1,0:T(8,128)(2,1)}) %reduce-scatter.25.cloned.1.call-update) | async-done | bytes 442384
  1056.6 95.0 %reduce-scatter.29.cloned.1.call-done = bf16[192,1536]{1,0:T(8,128)(2,1)} async-done(((bf16[1536,1536]{1,0:T(8,128)(2,1)}), bf16[192,1536]{1,0:T(8,128)(2,1)}) %reduce-scatter.29.cloned.1.call-update) | async-done | bytes 589840
  1152.9 97.6 %reduce-scatter.31.cloned.1.call-done = bf16[192,1536]{1,0:T(8,128)(2,1)} async-done(((bf16[1536,1536]{1,0:T(8,128)(2,1)}), bf16[192,1536]{1,0:T(8,128)(2,1)}) %reduce-scatter.31.cloned.1.call-update) | async-done | bytes 589840
  1251.9 97.8 %reduce-scatter.33.cloned.1.call-done = bf16[192,1536]{1,0:T(8,128)(2,1)} async-done(((bf16[1536,1536]{1,0:T(8,128)(2,1)}), bf16[192,1536]{1,0:T(8,128)(2,1)}) %reduce-scatter.33.cloned.1.call-update) | async-done | bytes 589840
  1358.3 2.8 pad_maximum_fusion.6
  1361.0 3.3 copy.85
  1364.3 46.1 %reduce-scatter.19.cloned.1.call-done = bf16[512,1536]{1,0:T(8,128)(2,1)} async-done(((bf16[2048,1536]{1,0:T(8,128)(2,1)}), bf16[512,1536]{1,0:T(8,128)(2,1)}) %reduce-scatter.19.cloned.1.call-update) | async-done | bytes 1572880 | tf_op jit(solution)/shard_map/reduce_scatter | solution.py:868
  1410.4 3.0 add_convert_fusion
  1413.4 95.8 %reduce-scatter.27.cloned.1.call-done = bf16[192,1536]{1,0:T(8,128)(2,1)} async-done(((bf16[1536,1536]{1,0:T(8,128)(2,1)}), bf16[192,1536]{1,0:T(8,128)(2,1)}) %reduce-scatter.27.cloned.1.call-update) | async-done | bytes 589840
  (185 shorter events, 55.2 us)
Async XLA Ops:
  7.2 299.6 %copy-start = (bf16[1,128,768]{2,1,0:T(8,128)(2,1)S(1)}, bf16[1,128,768]{2,1,0:T(8,128)(2,1)}, u32[]{:S(2)}) copy-start(bf16[1,128,768]{2,1,0:T(8,128)(2,1)} %param.23) | copy-start | bytes 589828
  7.2 86.2 %all-gather.9.cloned.1.call-start = ((), (), s32[]{:S(2)}) async-start(), calls=%async_computation.8 | async-start | bytes 5308416 | tf_op jit(solution)/shard_map/all_gather | solution.py:783
  10.2 306.6 %all-gather.11.cloned.1.call-start = ((), (), s32[]{:S(2)}) async-start(), calls=%async_computation.9 | async-start | bytes 7864320 | tf_op jit(solution)/shard_map/all_gather | solution.py:835
  11.0 85.7 %copy-start.6 = (bf16[192,1536]{1,0:T(8,128)(2,1)S(1)}, bf16[192,1536]{1,0:T(8,128)(2,1)}, u32[]{:S(2)}) copy-start(bf16[192,1536]{1,0:T(8,128)(2,1)} %param.35) | copy-start | bytes 1769476
  11.0 85.8 %copy-start.7 = (bf16[192,1536]{1,0:T(8,128)(2,1)S(1)}, bf16[192,1536]{1,0:T(8,128)(2,1)}, u32[]{:S(2)}) copy-start(bf16[192,1536]{1,0:T(8,128)(2,1)} %param.33) | copy-start | bytes 1769476
  11.0 85.8 %copy-start.8 = (bf16[192,1536]{1,0:T(8,128)(2,1)S(1)}, bf16[192,1536]{1,0:T(8,128)(2,1)}, u32[]{:S(2)}) copy-start(bf16[192,1536]{1,0:T(8,128)(2,1)} %param.34) | copy-start | bytes 1769476
  11.0 312.5 %all-gather.19.cloned.1.call-start = ((), (), s32[]{:S(2)}) async-start(), calls=%async_computation.17 | async-start | bytes 11796480 | tf_op jit(solution)/shard_map/all_gather | solution.py:832
  96.7 298.2 %all-gather.13.cloned.1.call-start = ((), (), s32[]{:S(2)}) async-start(), calls=%async_computation.10 | async-start | bytes 5308416 | tf_op jit(solution)/shard_map/all_gather | solution.py:783
  96.9 3.6 copy-start.20
  96.9 3.7 copy-start.21
  96.9 3.8 copy-start.22
  96.9 3.9 copy-start.11
  97.0 3.9 copy-start.12
  97.0 3.9 copy-start.13
  97.9 312.5 %all-gather.15.cloned.1.call-start = ((), (), s32[]{:S(2)}) async-start(), calls=%async_computation.11 | async-start | bytes 5308416 | tf_op jit(solution)/shard_map/all_gather | solution.py:783
  98.8 382.0 %all-gather.17.cloned.1.call-start = ((), (), s32[]{:S(2)}) async-start(), calls=%async_computation.12 | async-start | bytes 5308416 | tf_op jit(solution)/shard_map/all_gather | solution.py:783
  99.8 859.8 %reduce-scatter.23.cloned.1.call-start = ((), (), s32[]{:S(2)}) async-start(), calls=%async_computation.16 | async-start | bytes 1966080 | tf_op jit(solution)/shard_map/reduce_scatter | solution.py:888
  173.7 7.6 copy-start.15
  181.5 32.1 %copy-start.9 = (f32[1536]{0:T(1024)}, f32[1536]{0:T(1024)S(1)}, u32[]{:S(2)}) copy-start(f32[1536]{0:T(1024)S(1)} %convolution_reduce_fusion) | copy-start | bytes 18436
  305.0 1.3 slice-start
  605.5 3.0 copy-start.5
  605.5 361.6 %reduce-scatter.21.cloned.1.call-start = ((), (), s32[]{:S(2)}) async-start(), calls=%async_computation.15 | async-start | bytes 11796480 | tf_op jit(solution)/shard_map/reduce_scatter | solution.py:887
  609.2 4.7 copy-start.23
  620.7 1.4 copy-start.1
  620.8 362.3 %all-reduce.3.cloned.1.call-start = ((), (), s32[]{:S(2)}) async-start(), calls=%async_computation.14 | async-start | bytes 196608 | tf_op jit(solution)/shard_map/psum | solution.py:918
  783.9 40.8 %copy-start.17 = (f32[16,384]{1,0:T(8,128)S(1)}, f32[16,384]{1,0:T(8,128)}, u32[]{:S(2)}) copy-start(f32[16,384]{1,0:T(8,128)} %get-tuple-element.71) | copy-start | bytes 73732
  783.9 42.5 %copy-start.16 = (f32[16,384]{1,0:T(8,128)S(1)}, f32[16,384]{1,0:T(8,128)}, u32[]{:S(2)}) copy-start(f32[16,384]{1,0:T(8,128)} %get-tuple-element.72) | copy-start | bytes 73732
  783.9 44.2 %copy-start.14 = (f32[1536]{0:T(1024)S(1)}, f32[1536]{0:T(1024)}, u32[]{:S(2)}) copy-start(f32[1536]{0:T(1024)} %get-tuple-element.170) | copy-start | bytes 18436
  826.4 4.9 copy-start.10
  826.4 6.9 copy-start.18
  826.4 6.9 copy-start.19
  834.0 6.0 copy-start.25
  834.0 12.6 slice-start.1
  840.0 6.6 slice-start.2
  840.0 6.6 copy-start.24
  850.3 202.3 %reduce-scatter.25.cloned.1.call-start = ((), (), s32[]{:S(2)}) async-start(), calls=%async_computation.18 | async-start | bytes 3981312
  859.4 292.1 %reduce-scatter.29.cloned.1.call-start = ((), (), s32[]{:S(2)}) async-start(), calls=%async_computation.20 | async-start | bytes 5308416
  859.7 7.1 copy-start.28
  885.0 365.5 %reduce-scatter.31.cloned.1.call-start = ((), (), s32[]{:S(2)}) async-start(), calls=%async_computation.21 | async-start | bytes 5308416
  885.3 7.0 copy-start.27
  910.6 439.1 %reduce-scatter.33.cloned.1.call-start = ((), (), s32[]{:S(2)}) async-start(), calls=%async_computation.22 | async-start | bytes 5308416
  911.1 7.0 copy-start.26
  936.4 473.9 %reduce-scatter.19.cloned.1.call-start = ((), (), s32[]{:S(2)}) async-start(), calls=%async_computation.13 | async-start | bytes 7864320 | tf_op jit(solution)/shard_map/reduce_scatter | solution.py:868
  951.7 1.4 copy-start.4
  951.7 557.4 %reduce-scatter.27.cloned.1.call-start = ((), (), s32[]{:S(2)}) async-start(), calls=%async_computation.19 | async-start | bytes 5308416
  1354.1 1.6 copy-start.3
  1358.3 52.1 %copy-start.2 = (f32[512,1536]{1,0:T(8,128)S(1)}, f32[512,1536]{1,0:T(8,128)}, u32[]{:S(2)}) copy-start(f32[512,1536]{1,0:T(8,128)} %get-tuple-element.55.ac_ref) | copy-start | bytes 9437188
Sparse Core Ops, SparseCore 0:
  10.8 82.5 all-gather.8
  95.0 77.6 all-gather.10
  174.8 63.7 all-gather.18
  240.7 79.8 all-gather.12
  322.6 78.0 all-gather.14
  402.7 78.0 all-gather.16
  605.6 31.2 reduce-scatter.22
  639.7 82.1 reduce-scatter.20
  850.5 118.2 all-reduce.2
  972.7 79.9 reduce-scatter.24
  1056.8 94.7 reduce-scatter.28
  1155.5 94.9 reduce-scatter.30
  1254.6 94.9 reduce-scatter.32
  1352.2 58.1 reduce-scatter.18
  1413.9 95.2 reduce-scatter.26

commit v2 on v1

v2 whole, which is shorter than its diff:
```python
import functools

import jax
import jax.numpy as jnp
import numpy as np
from jax import lax
from jax.experimental import pallas as pl
from jax.experimental.pallas import tpu as pltpu
from jax.sharding import PartitionSpec as P

HD = 64
ROT = 32
LOG2E = 1.4426950408889634
EPS = 1e-05
MESH = pl.DeviceIdType.MESH
NT = (((1,), (1,)), ((), ()))
TN = (((0,), (0,)), ((), ()))
NN = (((1,), (0,)), ((), ()))
BF = jnp.bfloat16
F32 = jnp.float32
ANY = pl.BlockSpec(memory_space=pl.ANY)
VM = 58 << 20


def shape_of(dims, dtype):
    return jax.ShapeDtypeStruct(dims, dtype)


def dot(left, right, dims):
    return lax.dot_general(left, right, dims, preferred_element_type=F32)


def local_params(**extra):
    return pltpu.CompilerParams(vmem_limit_bytes=VM, **extra)


def cost(flops, nbytes, trans=0):
    return pl.CostEstimate(flops=int(flops), bytes_accessed=int(nbytes), transcendentals=int(trans))


def norm_rows(values):
    center = values - jnp.mean(values, -1, keepdims=True)
    spread = lax.rsqrt(jnp.mean(center * center, -1, keepdims=True) + EPS)
    return center * spread, spread


def norm_back(grad_rows, unit_rows, spread, gain_row):
    scaled = grad_rows * gain_row
    result = spread * (
        scaled
        - jnp.mean(scaled, -1, keepdims=True)
        - unit_rows * jnp.mean(scaled * unit_rows, -1, keepdims=True)
    )
    return result, jnp.sum(grad_rows * unit_rows, 0, keepdims=True)


def rope_tables(length, offset):
    lane = np.arange(2 * HD) % HD
    half = ROT // 2
    frequency = np.power(10000.0, -2.0 * (lane % half) / ROT)
    angles = (offset + np.arange(length))[:, None] * frequency[None, :]
    cosine = np.where(lane[None] < ROT, np.cos(angles), 1.0)
    sine = np.sin(angles)
    upper = np.where((lane[None] >= half) & (lane[None] < ROT), sine, 0.0)
    lower = np.where(lane[None] < half, -sine, 0.0)
    return [jnp.asarray(table.astype(np.float32)) for table in (cosine, upper, lower)]


def rope(values, cosine, upper, lower):
    half = ROT // 2
    return (
        values * cosine
        + pltpu.roll(values, half, 1) * upper
        + pltpu.roll(values, 2 * HD - half, 1) * lower
    )


def lanes(dims):
    return lax.broadcasted_iota(jnp.int32, dims, 1)


def half_mask(values, head):
    lane = lanes(values.shape)
    keep = (lane < HD) if head == 0 else (lane >= HD)
    return jnp.where(keep, values, jnp.zeros_like(values))


def pieces(column, dims, base):
    high = column.astype(BF).astype(F32)
    rest = column - high
    middle = rest.astype(BF).astype(F32)
    low = rest - middle
    lane = lanes(dims)
    return jnp.where(
        lane == base,
        high,
        jnp.where(lane == base + 1, middle, jnp.where(lane == base + 2, low, 0.0)),
    )


def mp_peers():
    me = lax.axis_index("mp")
    chip, core = me // 2, me % 2
    return me, chip * 2 + (1 - core), (1 - chip) * 2 + core, (1 - chip) * 2 + (1 - core)


def greet(devices):
    barrier = pltpu.get_barrier_semaphore()
    for device in devices:
        pl.semaphore_signal(barrier, inc=1, device_id=device, device_id_type=MESH)
    pl.semaphore_wait(barrier, len(devices))


def remote(source, target, send, recv, device):
    return pltpu.make_async_remote_copy(
        source, target, send, recv, device_id=device, device_id_type=MESH
    )


CHUNKS = 4
BUSY = cost(1, 140 << 20)


def gather_scratch(rows, width):
    return [
        pltpu.VMEM((rows, width), BF),
        pltpu.SemaphoreType.DMA((2,)),
        pltpu.SemaphoreType.DMA((3, CHUNKS)),
        pltpu.SemaphoreType.DMA((3, CHUNKS)),
    ]


class Gather:
    def __init__(self, x_ref, o_ref, sems, columns=None):
        bounce, lsem, ssem, rsem = sems
        self.me, self.sib, self.far, _ = mp_peers()
        dp = lax.axis_index("dp")
        self.to_sib = {"dp": dp, "mp": self.sib}
        self.to_far = {"dp": dp, "mp": self.far}
        rows = x_ref.shape[0]
        part = rows // CHUNKS

        def slot(i, k):
            return o_ref.at[pl.ds(pl.multiple_of(i * rows + k * part, part), part)]

        def source(first, size):
            if columns is None:
                return x_ref.at[pl.ds(first, size)]
            return x_ref.at[pl.ds(first, size), columns]

        self.load = pltpu.make_async_copy(source(0, rows), bounce, lsem.at[0])
        self.store = pltpu.make_async_copy(
            bounce, o_ref.at[pl.ds(pl.multiple_of(self.me * rows, rows), rows)], lsem.at[1]
        )
        self.across = []
        self.beside = []
        self.onward = []
        for k in range(CHUNKS):
            mine = source(k * part, part)
            self.across.append(
                remote(mine, slot(self.me, k), ssem.at[0, k], rsem.at[0, k], self.to_far)
            )
            self.beside.append(
                remote(mine, slot(self.me, k), ssem.at[1, k], rsem.at[1, k], self.to_sib)
            )
            self.onward.append(
                remote(
                    slot(self.far, k), slot(self.far, k), ssem.at[2, k], rsem.at[2, k], self.to_sib
                )
            )

    def start(self):
        for copy in self.across:
            copy.start()
        self.load.start()
        for copy in self.beside:
            copy.start()
        self.load.wait()
        self.store.start()

    def forward(self, k):
        self.across[k].wait_recv()
        self.onward[k].start()

    def finish(self):
        for k in range(CHUNKS):
            self.beside[k].wait_recv()
            self.onward[k].wait_recv()
        for k in range(CHUNKS):
            self.across[k].wait_send()
            self.beside[k].wait_send()
            self.onward[k].wait_send()
        self.store.wait()


def scatter_scratch(rows, width):
    return [pltpu.VMEM((2, rows, width), BF)] + [pltpu.VMEM((rows, width), BF)] * 4 + [
        pltpu.SemaphoreType.DMA((2,)),
        pltpu.SemaphoreType.DMA((3, CHUNKS)),
        pltpu.SemaphoreType.DMA((3, CHUNKS)),
    ]


class Scatter:
    def __init__(self, x_ref, o_ref, scratch):
        mine, ra, rb, rc, sb, lsem, ssem, rsem = scratch
        me, sib, far, diag = mp_peers()
        dp = lax.axis_index("dp")
        self.to_sib = {"dp": dp, "mp": sib}
        self.to_far = {"dp": dp, "mp": far}
        self.o_ref, self.mine, self.ra, self.rb, self.rc, self.sb = o_ref, mine, ra, rb, rc, sb
        rows = ra.shape[0]
        part = rows // CHUNKS
        self.spans = [pl.ds(k * part, part) for k in range(CHUNKS)]

        def slot(i, k):
            return x_ref.at[pl.ds(pl.multiple_of(i * rows + k * part, part), part)]

        def whole(i):
            return x_ref.at[pl.ds(pl.multiple_of(i * rows, rows), rows)]

        self.first, self.second, self.third = [], [], []
        for k, span in enumerate(self.spans):
            self.first.append(
                remote(slot(diag, k), ra.at[span], ssem.at[0, k], rsem.at[0, k], self.to_sib)
            )
            self.second.append(
                remote(slot(sib, k), rb.at[span], ssem.at[1, k], rsem.at[1, k], self.to_sib)
            )
            self.third.append(
                remote(sb.at[span], rc.at[span], ssem.at[2, k], rsem.at[2, k], self.to_far)
            )
        self.load0 = pltpu.make_async_copy(whole(far), mine.at[0], lsem.at[0])
        self.load1 = pltpu.make_async_copy(whole(me), mine.at[1], lsem.at[1])

    def start(self):
        self.load0.start()
        for copy in self.first:
            copy.start()
        self.load1.start()
        for copy in self.second:
            copy.start()

    def fold(self):
        self.load0.wait()
        for k, span in enumerate(self.spans):
            self.first[k].wait_recv()
            total = self.mine[0, span, :].astype(F32) + self.ra[span, :].astype(F32)
            self.sb[span, :] = total.astype(BF)
            self.third[k].start()

    def local(self):
        self.load1.wait()
        for k in range(CHUNKS):
            self.second[k].wait_recv()

    def land(self):
        for k, span in enumerate(self.spans):
            self.third[k].wait_recv()
            total = self.mine[1, span, :].astype(F32) + self.rb[span, :].astype(F32)
            self.o_ref[span, :] = (total + self.rc[span, :].astype(F32)).astype(self.o_ref.dtype)

    def finish(self):
        for k in range(CHUNKS):
            self.first[k].wait_send()
            self.second[k].wait_send()
            self.third[k].wait_send()


def sum_scratch(rows, width):
    return [pltpu.VMEM((4, rows, width), BF)] + [pltpu.VMEM((rows, width), BF)] * 4 + [
        pltpu.SemaphoreType.DMA((3, CHUNKS)),
        pltpu.SemaphoreType.DMA((3, CHUNKS)),
    ]


class LocalSum:
    def __init__(self, o_ref, scratch):
        terms, ra, rb, rc, sb, ssem, rsem = scratch
        _, sib, far, _ = mp_peers()
        dp = lax.axis_index("dp")
        self.to_sib = {"dp": dp, "mp": sib}
        self.to_far = {"dp": dp, "mp": far}
        self.o_ref, self.terms, self.ra, self.rb, self.rc, self.sb = o_ref, terms, ra, rb, rc, sb
        rows = ra.shape[0]
        part = rows // CHUNKS
        self.spans = [pl.ds(k * part, part) for k in range(CHUNKS)]
        self.first, self.second, self.third = [], [], []
        for k, span in enumerate(self.spans):
            self.first.append(
                remote(terms.at[0, span], ra.at[span], ssem.at[0, k], rsem.at[0, k], self.to_sib)
            )
            self.second.append(
                remote(terms.at[2, span], rb.at[span], ssem.at[1, k], rsem.at[1, k], self.to_sib)
            )
            self.third.append(
                remote(sb.at[span], rc.at[span], ssem.at[2, k], rsem.at[2, k], self.to_far)
            )

    def put(self, step, value):
        half = value.shape[0]
        self.terms[step // 2, pl.ds(pl.multiple_of((step % 2) * half, half), half), :] = value

    def after_step(self, step):
        @pl.when(step == 1)
        def _():
            for copy in self.first:
                copy.start()

        @pl.when(step == 3)
        def _():
            for k, span in enumerate(self.spans):
                self.first[k].wait_recv()
                total = self.terms[1, span, :].astype(F32) + self.ra[span, :].astype(F32)
                self.sb[span, :] = total.astype(BF)
                self.third[k].start()

        @pl.when(step == 5)
        def _():
            for copy in self.second:
                copy.start()

    def land(self):
        for k, span in enumerate(self.spans):
            self.second[k].wait_recv()
            self.third[k].wait_recv()
            total = self.terms[3, span, :].astype(F32) + self.rb[span, :].astype(F32)
            self.o_ref[span, :] = (total + self.rc[span, :].astype(F32)).astype(self.o_ref.dtype)

    def finish(self):
        for copy in self.first + self.second + self.third:
            copy.wait_send()


def order_block(step):
    me = lax.axis_index("mp")
    chip, core = me // 2, me % 2
    other = 1 - step // 4
    cross = 1 - (step // 2) % 2
    quarter = (chip + other - 2 * chip * other) * 2 + (core + cross - 2 * core * cross)
    return quarter * 2 + step % 2


def arrival_quarter(turn):
    me = lax.axis_index("mp")
    chip, core = me // 2, me % 2
    other = turn // 2
    cross = turn % 2
    return (chip + other - 2 * chip * other) * 2 + (core + cross - 2 * core * cross)


class Ring:
    def __init__(self, count):
        self.count = count
        self.half = count // 2
        me = lax.axis_index("dp")
        mp = lax.axis_index("mp")
        odd = me % 2
        self.me = me
        self.spot = (1 - odd) * (me // 2) + odd * (count - 1 - me // 2)
        self.ahead = {"dp": self.at(1), "mp": mp}
        self.behind = {"dp": self.at(-1), "mp": mp}

    def at(self, distance):
        spot = (self.spot + distance + self.count) % self.count
        late = spot // self.half
        return (1 - late) * 2 * spot + late * (2 * (self.count - 1 - spot) + 1)


def ring_scratch(rows, width, half):
    return [pltpu.VMEM((rows, width), BF), pltpu.SemaphoreType.DMA((2,))] + [
        pltpu.SemaphoreType.DMA((half,))
    ] * 4


class RingGather:
    def __init__(self, count, w_ref, o_ref, scratch):
        bounce, lsem, fs, fr, bs, br = scratch
        ring = Ring(count)
        self.ahead, self.behind, self.half = ring.ahead, ring.behind, ring.half
        rows = w_ref.shape[0]

        def slot(i):
            return o_ref.at[pl.ds(pl.multiple_of(i * rows, rows), rows)]

        self.forward = []
        self.backward = []
        for hop in range(self.half):
            block = ring.at(-hop)
            source = w_ref if hop == 0 else slot(block)
            self.forward.append(
                remote(source, slot(block), fs.at[hop], fr.at[hop], ring.ahead)
            )
            block = ring.at(hop)
            source = w_ref if hop == 0 else slot(block)
            if hop < self.half - 1:
                self.backward.append(
                    remote(source, slot(block), bs.at[hop], br.at[hop], ring.behind)
                )
        self.load = pltpu.make_async_copy(w_ref, bounce, lsem.at[0])
        self.store = pltpu.make_async_copy(bounce, slot(ring.me), lsem.at[1])

    def start(self):
        self.forward[0].start()
        self.backward[0].start()
        self.load.start()

    def place(self):
        self.load.wait()
        self.store.start()

    def hop(self, hop):
        self.forward[hop - 1].wait_recv()
        self.forward[hop].start()
        self.backward[hop - 1].wait_recv()
        if hop < self.half - 1:
            self.backward[hop].start()

    def finish(self):
        self.forward[self.half - 1].wait_recv()
        self.store.wait()
        for copy in self.forward + self.backward:
            copy.wait_send()


def plain_gather_kernel(x_ref, o_ref, *scratch):
    job = Gather(x_ref, o_ref, scratch)
    greet([job.to_sib, job.to_far])
    job.start()
    for k in range(CHUNKS):
        job.forward(k)
    job.finish()


def plain_gather(share, ident):
    rows, width = share.shape
    return pl.pallas_call(
        plain_gather_kernel,
        out_shape=shape_of((4 * rows, width), share.dtype),
        in_specs=[ANY],
        out_specs=ANY,
        scratch_shapes=gather_scratch(rows, width),
        compiler_params=local_params(collective_id=ident, has_side_effects=True),
        cost_estimate=BUSY,
        name="plain_gather_%d" % ident,
    )(share)


def head_kernel(count, f_ref, g_ref, w_ref, fo_ref, go_ref, wo_ref, *scratch):
    job = Gather(f_ref, fo_ref, scratch[0:4])
    late = Gather(g_ref, go_ref, scratch[4:8])
    ring = RingGather(count, w_ref, wo_ref, scratch[8:])
    greet([job.to_sib, job.to_far, ring.ahead, ring.behind])
    ring.start()
    job.start()
    ring.place()
    ring.hop(1)
    for k in range(CHUNKS):
        job.forward(k)
    late.start()
    for hop in range(2, ring.half):
        ring.hop(hop)
    for k in range(CHUNKS):
        late.forward(k)
    job.finish()
    late.finish()
    ring.finish()


def head_gather(frames, grads, packed, count):
    rows, width = frames.shape
    wide = shape_of((4 * rows, width), BF)
    return pl.pallas_call(
        functools.partial(head_kernel, count),
        out_shape=(wide, wide, shape_of((count * packed.shape[0], packed.shape[1]), BF)),
        in_specs=[ANY] * 3,
        out_specs=(ANY,) * 3,
        scratch_shapes=gather_scratch(rows, width) * 2 + ring_scratch(*packed.shape, count // 2),
        compiler_params=local_params(collective_id=0, has_side_effects=True),
        cost_estimate=BUSY,
        name="head_gather",
    )(frames, grads, packed)


SMALL = 16


def tail_kernel(
    count, buckets, q_ref, k_ref, v_ref, wq_ref, wk_ref, wv_ref,
    a_ref, b_ref, f_ref, c_ref, g1_ref, dg2_ref, dg3_ref, mark_ref, cb_ref,
    dg1_ref, o_ref, s_ref, *scratch,
):
    outs = scratch[:5]
    scratch = scratch[5:]
    total, held = scratch[0:2]
    job = LocalSum(total, scratch[2:9])
    lf, lb, rf, rb, lsem, fs, fr, bs, br, sent, got, ss, rs = scratch[9:]
    step = pl.program_id(0)
    ring = Ring(count)
    half = ring.half
    rows = outs[0].shape[0]
    split = a_ref.shape[1]
    mp = lax.axis_index("mp")
    partners = [job.to_sib, job.to_far]
    bit = 1
    while bit < count:
        partners.append({"dp": ring.me + bit * (1 - 2 * ((ring.me // bit) % 2)), "mp": mp})
        bit *= 2

    def loads(block, target, sem):
        span = pl.ds(pl.multiple_of(block * rows, rows), rows)
        return [
            pltpu.make_async_copy(a_ref.at[span], target.at[:, pl.ds(0, split)], sem.at[0]),
            pltpu.make_async_copy(
                b_ref.at[span], target.at[:, pl.ds(split, b_ref.shape[1])], sem.at[1]
            ),
        ]

    forward, backward, local_f, local_b = [], [], [], []
    for hop in range(half):
        local_f.append(loads(ring.at(half - hop), lf.at[hop], lsem.at[0, hop]))
        forward.append(remote(lf.at[hop], rf.at[hop], fs.at[hop], fr.at[hop], ring.ahead))
        if hop < half - 1:
            local_b.append(loads(ring.at(hop + 1 - half), lb.at[hop], lsem.at[1, hop]))
            backward.append(remote(lb.at[hop], rb.at[hop], bs.at[hop], br.at[hop], ring.behind))
    local_b.append(loads(ring.me, lb.at[half - 1], lsem.at[1, half - 1]))
    @pl.when(step == 0)
    def _():
        greet(partners + [ring.ahead, ring.behind])
        for hop in range(half):
            for copy in local_f[hop] + local_b[hop]:
                copy.start()
        for copy in local_f[0] + local_b[0]:
            copy.wait()
        forward[0].start()
        backward[0].start()

    @pl.when(step < 8)
    def _():
        term = (
            dot(q_ref[...], wq_ref[...], NT)
            + dot(k_ref[...], wk_ref[...], NT)
            + dot(v_ref[...], wv_ref[...], NT)
        )
        job.put(step, term.astype(BF))

    job.after_step(step)

    def ring_hop(hop):
        for copy in local_f[hop]:
            copy.wait()
        forward[hop - 1].wait_recv()
        lf[hop] = (lf[hop].astype(F32) + rf[hop - 1].astype(F32)).astype(BF)
        forward[hop].start()
        for copy in local_b[hop]:
            copy.wait()
        backward[hop - 1].wait_recv()
        if hop < half - 1:
            lb[hop] = (lb[hop].astype(F32) + rb[hop - 1].astype(F32)).astype(BF)
            backward[hop].start()

    @pl.when(step == 8)
    def _():
        for hop in range(1, half - 1):
            ring_hop(hop)
        job.land()
        unit, spread = norm_rows(f_ref[...].astype(F32))
        back, part = norm_back(total[...], unit, spread, g1_ref[...])
        o_ref[...] = c_ref[...] + back
        row = lax.broadcasted_iota(jnp.int32, held.shape, 0)
        held[...] = (
            mark_ref[...] * cb_ref[...]
            + jnp.where(row == buckets, part + dg1_ref[...], 0.0)
            + jnp.where(row == buckets + 1, dg2_ref[...], 0.0)
            + jnp.where(row == buckets + 2, dg3_ref[...], 0.0)
        )
        ring_hop(half - 1)
        for i, partner in enumerate(partners):
            sent[i] = held[...]
            copy = remote(sent.at[i], got.at[i], ss.at[i], rs.at[i], partner)
            copy.start()
            copy.wait_recv()
            held[...] += got[i]
            copy.wait_send()
        s_ref[...] = held[...]
        forward[half - 1].wait_recv()
        base = 0
        for out in outs:
            span = slice(base, base + out.shape[1])
            base += out.shape[1]
            out[...] = (
                lb[half - 1, :, span].astype(F32)
                + rf[half - 1, :, span].astype(F32)
                + rb[half - 2, :, span].astype(F32)
            )
        for copy in forward + backward:
            copy.wait_send()
        job.finish()


def tail_sums(
    count, buckets, grads_qkv, weights, grads, more, frames, carried, gain1, dg2, dg3, mark,
    cond_back, dg1,
):
    share, model = frames.shape
    width = grads_qkv[0].shape[1]
    block = 2 * share // 4
    rows = grads.shape[0] // count
    wide = grads.shape[1] + more.shape[1]
    half = count // 2
    steps = 2 + (count - 1).bit_length()
    once = pl.Buffered(1)

    def full(array):
        return pl.BlockSpec(array.shape, lambda i: (0,) * array.ndim, pipeline_mode=once)

    slots = pltpu.VMEM((half, rows, wide), BF)
    hops = pltpu.SemaphoreType.DMA((half,))
    small = pltpu.VMEM((steps, SMALL, model), F32)
    out_shape = (shape_of((share, model), F32), shape_of((SMALL, model), F32)) + (
        shape_of((rows, wide // 5), F32),
    ) * 5
    whole = [frames, carried, gain1, dg2, dg3, mark, cond_back, dg1]
    return pl.pallas_call(
        functools.partial(tail_kernel, count, buckets),
        grid=(9,),
        out_shape=out_shape,
        in_specs=[
            pl.BlockSpec((block, width), lambda i: (order_block(jnp.minimum(i, 7)), 0))
            for _ in range(3)
        ]
        + [
            pl.BlockSpec(
                (model, width), functools.partial(lambda at, i: (0, at), at), pipeline_mode=once
            )
            for at in range(3)
        ]
        + [ANY, ANY]
        + [full(array) for array in whole],
        out_specs=tuple(pl.BlockSpec(out.shape, lambda i: (0, 0)) for out in out_shape),
        scratch_shapes=[pltpu.VMEM((share, model), F32), pltpu.VMEM((SMALL, model), F32)]
        + sum_scratch(share, model)
        + [slots] * 4
        + [pltpu.SemaphoreType.DMA((2, half, 2))]
        + [hops] * 4
        + [small, small, pltpu.SemaphoreType.DMA((steps,)), pltpu.SemaphoreType.DMA((steps,))],
        compiler_params=local_params(collective_id=6, has_side_effects=True),
        cost_estimate=BUSY,
        name="tail_sums",
    )(*grads_qkv, weights, weights, weights, grads, more, *whole)


def out_kernel(m_ref, w_ref, kv_ref, o_ref, kvo_ref, *scratch):
    side = Gather(kv_ref, kvo_ref, scratch[:4])
    job = LocalSum(o_ref, scratch[4:])
    step = pl.program_id(0)

    @pl.when(step == 0)
    def _():
        greet([job.to_sib, job.to_far])
        side.start()

    job.put(step, dot(m_ref[...], w_ref[...], NT).astype(BF))
    job.after_step(step)

    @pl.when(step == 7)
    def _():
        for k in range(CHUNKS):
            side.forward(k)
        job.land()
        side.finish()
        job.finish()


def out_project(mixed, weights, side):
    length, width = mixed.shape
    model = weights.shape[0]
    rows = length // 8
    share = length // 4
    return pl.pallas_call(
        out_kernel,
        grid=(8,),
        out_shape=(shape_of((share, model), F32), shape_of((4 * side.shape[0], side.shape[1]), BF)),
        in_specs=[
            pl.BlockSpec((rows, width), lambda i: (order_block(i), 0)),
            pl.BlockSpec((model, width), lambda i: (0, 0), pipeline_mode=pl.Buffered(1)),
            ANY,
        ],
        out_specs=(pl.BlockSpec((share, model), lambda i: (0, 0)), ANY),
        scratch_shapes=gather_scratch(*side.shape) + sum_scratch(share, model),
        compiler_params=local_params(collective_id=1, has_side_effects=True),
        cost_estimate=BUSY,
        name="out_project",
    )(mixed, weights, side)


def glu_back_kernel(
    d0_ref, d1_ref, g0_ref, g1_ref, h0_ref, h1_ref, w0_ref, w1_ref, o_ref, t_ref, *scratch
):
    job = LocalSum(o_ref, scratch)
    step = pl.program_id(0)

    @pl.when(step == 0)
    def _():
        greet([job.to_sib, job.to_far])

    @pl.when(step < 8)
    def _():
        term = dot(d0_ref[...], g0_ref[...], NT) + dot(d1_ref[...], g1_ref[...], NT)
        job.put(step, term.astype(BF))

    job.after_step(step)

    @pl.when(step >= 8)
    def _():
        term = dot(h0_ref[...], w0_ref[...], NT) + dot(h1_ref[...], w1_ref[...], NT)
        t_ref[...] = term.astype(BF)

    @pl.when(step == 15)
    def _():
        job.land()
        job.finish()


def glu_back(dgus, hiddens, weights):
    length = dgus[0].shape[0]
    model = weights[0].shape[0]
    rows = length // 8
    share = length // 4
    once = pl.Buffered(1)
    in_specs = []
    for d in dgus:
        in_specs.append(
            pl.BlockSpec((rows, d.shape[1]), lambda i: (order_block(jnp.minimum(i, 7)), 0))
        )
    for d in dgus:
        in_specs.append(pl.BlockSpec((model, d.shape[1]), lambda i: (0, 0), pipeline_mode=once))
    for h in hiddens:
        in_specs.append(pl.BlockSpec((rows, h.shape[1]), lambda i: (jnp.maximum(i - 8, 0), 0)))
    for h in hiddens:
        in_specs.append(pl.BlockSpec((model, h.shape[1]), lambda i: (0, 2), pipeline_mode=once))
    return pl.pallas_call(
        glu_back_kernel,
        grid=(16,),
        out_shape=(shape_of((share, model), F32), shape_of((length, model), BF)),
        in_specs=in_specs,
        out_specs=(
            pl.BlockSpec((share, model), lambda i: (0, 0)),
            pl.BlockSpec((rows, model), lambda i: (jnp.maximum(i - 8, 0), 0)),
        ),
        scratch_shapes=sum_scratch(share, model),
        compiler_params=local_params(collective_id=3, has_side_effects=True),
        cost_estimate=BUSY,
        name="glu_back",
    )(*dgus, *weights, *hiddens, *weights)


def mid_kernel(
    c_ref, t_ref, n_ref, cb_ref, q_ref, cm_ref, w_ref, m_ref,
    x_ref, g_ref, dw_ref, s_ref, slots, total, ssem, rsem, *scratch,
):
    small = Scatter(t_ref, s_ref, scratch)
    me, sib, far, diag = mp_peers()
    dp = lax.axis_index("dp")
    to_sib = {"dp": dp, "mp": sib}
    to_far = {"dp": dp, "mp": far}
    step = pl.program_id(0)
    rows = c_ref.shape[0]
    part = rows // CHUNKS
    spans = [pl.ds(k * part, part) for k in range(CHUNKS)]
    beside = remote(c_ref, slots.at[0], ssem.at[0], rsem.at[0], to_sib)
    across = [
        remote(c_ref.at[span], slots.at[1, span], ssem.at[1 + k], rsem.at[1 + k], to_far)
        for k, span in enumerate(spans)
    ]
    onward = [
        remote(
            slots.at[1, span],
            slots.at[2, span],
            ssem.at[1 + CHUNKS + k],
            rsem.at[1 + CHUNKS + k],
            to_sib,
        )
        for k, span in enumerate(spans)
    ]

    @pl.when(step == 0)
    def _():
        greet([to_sib, to_far])
        for copy in across:
            copy.start()
        small.start()
        beside.start()

    @pl.when(step == 1)
    def _():
        small.fold()
        small.local()

    @pl.when(step < 8)
    def _():
        width = q_ref.shape[1]
        x_ref[:, :width] = dot(n_ref[...], q_ref[...], TN).astype(BF)
        x_ref[:, width:] = dot(cb_ref[...], cm_ref[...], TN).astype(BF)

    def use(grads):
        g_ref[...] = dot(grads, w_ref[...], NN).astype(BF)
        return dot(grads, m_ref[...], TN)

    @pl.when(step == 8)
    def _():
        total[...] = use(c_ref[...])

    @pl.when(step == 9)
    def _():
        beside.wait_recv()
        total[...] += use(slots[0])

    @pl.when(step == 10)
    def _():
        small.land()
        for k in range(CHUNKS):
            across[k].wait_recv()
            onward[k].start()
        total[...] += use(slots[1])

    @pl.when(step == 11)
    def _():
        for copy in onward:
            copy.wait_recv()
        dw_ref[...] = (total[...] + use(slots[2])).astype(BF)
        small.finish()
        beside.wait_send()
        for copy in across + onward:
            copy.wait_send()


def mid_gather(carried, term, normed, cross_back, grad_cq, cross_mixed, weights, mixed, groups):
    share, model = carried.shape
    length, width = mixed.shape
    short, narrow = term.shape[0] // 4, term.shape[1]
    tile = 2 * model // 4
    once = pl.Buffered(1)
    fixed = pl.BlockSpec((share, model), lambda i: (0, 0), pipeline_mode=once)
    left = pl.BlockSpec((share, tile), lambda i: (0, jnp.minimum(i, 7) % 2))
    right = pl.BlockSpec((share, width), lambda i: (0, jnp.minimum(i, 7) // 2))

    def turn(i):
        return (arrival_quarter(jnp.maximum(i - 8, 0)), 0)

    return pl.pallas_call(
        mid_kernel,
        grid=(12,),
        in_specs=[
            fixed,
            ANY,
            left,
            left,
            right,
            right,
            pl.BlockSpec((model, width), lambda i: (0, 0), pipeline_mode=once),
            pl.BlockSpec((share, width), turn),
        ],
        out_specs=(
            pl.BlockSpec((tile, 2 * width), lambda i: (jnp.minimum(i, 7), 0)),
            pl.BlockSpec((share, width), turn),
            pl.BlockSpec((model, width), lambda i: (0, 0)),
            pl.BlockSpec((short, narrow), lambda i: (0, 0)),
        ),
        out_shape=(
            shape_of((groups * model, 2 * width), BF),
            shape_of((length, width), BF),
            shape_of((model, width), BF),
            shape_of((short, narrow), F32),
        ),
        scratch_shapes=[
            pltpu.VMEM((3, share, model), BF),
            pltpu.VMEM((model, width), F32),
            pltpu.SemaphoreType.DMA((1 + 2 * CHUNKS,)),
            pltpu.SemaphoreType.DMA((1 + 2 * CHUNKS,)),
        ]
        + scatter_scratch(short, narrow),
        compiler_params=local_params(collective_id=4, has_side_effects=True),
        cost_estimate=BUSY,
        name="mid_gather",
    )(carried, term, normed, cross_back, grad_cq, cross_mixed, weights, mixed)


def qkv_kernel(x_ref, g_ref, w_ref, c_ref, u_ref, l_ref, n_ref, q_ref, k_ref, v_ref):
    unit, _ = norm_rows(x_ref[...].astype(F32))
    normed = (unit * g_ref[...]).astype(BF)
    n_ref[...] = normed
    width = q_ref.shape[1]
    out = dot(normed, w_ref[...], NN)
    cosine, upper, lower = c_ref[...], u_ref[...], l_ref[...]
    for pair in range(width // 128):
        span = slice(128 * pair, 128 * pair + 128)
        q_ref[:, span] = (rope(out[:, span], cosine, upper, lower) * (LOG2E / 8.0)).astype(BF)
        keys = out[:, width + 128 * pair : width + 128 * pair + 128]
        k_ref[:, span] = rope(keys, cosine, upper, lower).astype(BF)
    v_ref[...] = out[:, 2 * width : 3 * width].astype(BF)


def qkv_project(frames, gain, weights, tables, width):
    length, model = frames.shape
    rows = 256
    block = pl.BlockSpec((rows, model), lambda i: (i, 0))
    table = pl.BlockSpec((rows, 128), lambda i: (i, 0))
    head = pl.BlockSpec((rows, width), lambda i: (i, 0))
    return pl.pallas_call(
        qkv_kernel,
        grid=(length // rows,),
        in_specs=[
            block,
            pl.BlockSpec((1, model), lambda i: (0, 0)),
            pl.BlockSpec((model, 3 * width), lambda i: (0, 0)),
            table,
            table,
            table,
        ],
        out_specs=[block, head, head, head],
        out_shape=[shape_of((length, model), BF)] + [shape_of((length, width), BF)] * 3,
        compiler_params=local_params(),
        cost_estimate=cost(6 * length * model * width, 8 * length * model),
        name="qkv_project",
    )(frames, gain, weights, *tables)


def attend_kernel(
    bk, first, count, q_ref, k_ref, v_ref, k0_ref, v0_ref, x_ref, w_ref,
    o_ref, aug_ref, xo_ref, wo_ref, vaug, *scratch,
):
    length = k_ref.shape[0]
    bq = q_ref.shape[0]
    step = pl.program_id(0) * pl.num_programs(1) + pl.program_id(1)
    wide = xo_ref.shape[1]
    job = Gather(x_ref, xo_ref, scratch[:4], pl.ds(first, wide))
    ring = RingGather(count, w_ref, wo_ref, scratch[4:])
    last = pl.num_programs(0) * pl.num_programs(1) - 1

    @pl.when(step == 0)
    def _():
        greet([job.to_sib, job.to_far, ring.ahead, ring.behind])
        ring.start()
        job.start()
        ring.place()

    for hop in range(1, ring.half):

        @pl.when(step == min(4 * hop, 11))
        def _(hop=hop):
            ring.hop(hop)

    @pl.when(pl.program_id(1) == 0)
    def _():
        vaug[:, :128] = v_ref[...]
        vaug[:, 128:] = jnp.ones((length, 128), BF)

    queries = q_ref[...]
    key0 = k0_ref[0:1, :].astype(F32)
    value0 = v0_ref[0:1, :].astype(F32)
    outs = []
    logs = []
    for head in range(2):
        masked = half_mask(queries, head)
        peak = jnp.sum(masked.astype(F32) * key0, axis=1, keepdims=True)
        total = jnp.concatenate(
            [jnp.broadcast_to(value0, (bq, 128)), jnp.ones((bq, 128), F32)], 1
        )
        for block in range(length // bk):
            span = slice(block * bk, (block + 1) * bk)
            scores = dot(masked, k_ref[span, :], NT)
            higher = jnp.maximum(peak, jnp.max(scores, axis=1, keepdims=True))
            exponent = jnp.exp2(scores - higher).astype(BF)
            total = total * jnp.exp2(peak - higher) + dot(exponent, vaug[span, :], NN)
            peak = higher
        weight = total[:, 128:129]
        outs.append(total[:, :128] * (1.0 / weight))
        logs.append(-(peak + jnp.log2(weight)))
    lane = lanes((bq, 128))
    o_ref[...] = jnp.where(lane < HD, outs[0], outs[1]).astype(BF)
    aug_ref[...] = (pieces(logs[0], (bq, 128), 0) + pieces(logs[1], (bq, 128), HD)).astype(BF)

    @pl.when(step == last)
    def _():
        for k in range(CHUNKS):
            job.forward(k)
        job.finish()
        ring.finish()


def attend(queries, keys, values, key0, value0, packed, first, share, count, bq=512, bk=1024):
    length, width = queries.shape
    row = pl.BlockSpec((bq, 128), lambda p, i: (i, p))
    full = pl.BlockSpec((length, 128), lambda p, i: (0, p))
    zero = pl.BlockSpec((16, 128), lambda p, i: (0, p))
    return pl.pallas_call(
        functools.partial(attend_kernel, bk, first, count),
        grid=(width // 128, length // bq),
        in_specs=[row, full, full, zero, zero, ANY, ANY],
        out_specs=[row, row, ANY, ANY],
        out_shape=[shape_of((length, width), BF)] * 2
        + [
            shape_of((4 * packed.shape[0], packed.shape[1] - first), BF),
            shape_of((count * share.shape[0], share.shape[1]), BF),
        ],
        scratch_shapes=[pltpu.VMEM((length, 256), BF)]
        + gather_scratch(packed.shape[0], packed.shape[1] - first)
        + ring_scratch(*share.shape, count // 2),
        compiler_params=local_params(collective_id=7, has_side_effects=True),
        cost_estimate=cost(16 * length * length * width, 10 * length * width),
        name="attend",
    )(queries, keys, values, key0, value0, packed, share)


def attend_back_kernel(
    bk, q_ref, aug_ref, o_ref, do_ref, k_ref, v_ref, k0_ref, v0_ref,
    cq_ref, uq_ref, lq_ref, ck_ref, uk_ref, lk_ref,
    x_ref, dq_ref, dk_ref, dv_ref, dk0_ref, dv0_ref, xo_ref,
    kaug, vaug, kt, dka, dva, *scratch,
):
    length = k_ref.shape[0]
    bq = q_ref.shape[0]
    step = pl.program_id(1)
    turn = pl.program_id(0) * pl.num_programs(1) + step
    job = Scatter(x_ref, xo_ref, scratch)

    @pl.when(turn == 0)
    def _():
        greet([job.to_sib, job.to_far])
        job.start()

    @pl.when(turn == 1)
    def _():
        job.fold()
        job.local()

    @pl.when(turn == pl.num_programs(0) * pl.num_programs(1) - 1)
    def _():
        job.land()
        job.finish()

    @pl.when(step == 0)
    def _():
        lane = lanes((length, 128))
        ones = jnp.where((lane % HD) < 3, 1.0, 0.0).astype(BF)
        kaug[:, :128] = k_ref[...]
        kaug[:, 128:] = ones
        vaug[:, :128] = v_ref[...]
        vaug[:, 128:] = ones
        kt[...] = k_ref[...].astype(F32).T.astype(BF)
        dka[...] = jnp.zeros_like(dka)
        dva[...] = jnp.zeros_like(dva)
        dk0_ref[...] = jnp.zeros_like(dk0_ref)
        dv0_ref[...] = jnp.zeros_like(dv0_ref)

    queries = q_ref[...]
    grads = do_ref[...]
    aug = aug_ref[...]
    product = grads.astype(F32) * o_ref[...].astype(F32)
    lane = lanes((bq, 128))
    ones0 = jnp.where((lanes((16, 128)) % HD) < 3, 1.0, 0.0).astype(BF)
    key0 = jnp.concatenate([k0_ref[...], ones0], 1)
    value0 = jnp.concatenate([v0_ref[...], ones0], 1)
    row0 = lax.broadcasted_iota(jnp.int32, (16, bq), 0) == 0
    qa, da, qm, dm, dq = [], [], [], [], []
    for head in range(2):
        qm.append(half_mask(queries, head))
        dm.append(half_mask(grads, head))
        mine = (lane < HD) if head == 0 else (lane >= HD)
        inner = jnp.sum(jnp.where(mine, product, 0.0), axis=1, keepdims=True)
        qa.append(jnp.concatenate([qm[head], half_mask(aug, head)], 1))
        da.append(
            jnp.concatenate([dm[head], pieces(-inner, (bq, 128), HD * head).astype(BF)], 1)
        )
        prob0 = jnp.where(row0, jnp.exp2(dot(key0, qa[head], NT)), 0.0)
        ds0 = (prob0 * dot(value0, da[head], NT)).astype(BF)
        dv0_ref[...] += dot(prob0.astype(BF), dm[head], NN)
        dk0_ref[...] += dot(ds0, qm[head], NN)
        dq.append(dot(k0_ref[:, HD * head : HD * head + HD], ds0, TN))
    for block in range(length // bk):
        span = slice(block * bk, (block + 1) * bk)
        for head in range(2):
            probs = jnp.exp2(dot(kaug[span, :], qa[head], NT))
            ds = (probs * dot(vaug[span, :], da[head], NT)).astype(BF)
            dva[span, :] += dot(probs.astype(BF), dm[head], NN)
            dka[span, :] += dot(ds, qm[head], NN)
            dq[head] = dq[head] + dot(kt[HD * head : HD * head + HD, span], ds, NN)
    grad_q = jnp.concatenate(dq, 0).T * 0.125
    dq_ref[...] = rope(grad_q, cq_ref[...], -uq_ref[...], -lq_ref[...]).astype(BF)

    @pl.when(step == pl.num_programs(1) - 1)
    def _():
        grad_k = dka[...] * (1.0 / LOG2E)
        dk_ref[...] = rope(grad_k, ck_ref[...], -uk_ref[...], -lk_ref[...]).astype(BF)
        dv_ref[...] = dva[...].astype(BF)
        dk0_ref[...] = dk0_ref[...] * (1.0 / LOG2E)


def attend_back(
    queries, aug, mixed, grads, keys, values, key0, value0, tables, extra, bq=512, bk=512
):
    length, width = queries.shape
    row = pl.BlockSpec((bq, 128), lambda p, i: (i, p))
    full = pl.BlockSpec((length, 128), lambda p, i: (0, p))
    zero = pl.BlockSpec((16, 128), lambda p, i: (0, p))
    tq = pl.BlockSpec((bq, 128), lambda p, i: (i, 0))
    tk = pl.BlockSpec((length, 128), lambda p, i: (0, 0), pipeline_mode=pl.Buffered(1))
    sums = pl.BlockSpec((extra.shape[0] // 4, extra.shape[1]), lambda p, i: (0, 0))
    big = shape_of((length, width), BF)
    small = shape_of((16, width), F32)
    return pl.pallas_call(
        functools.partial(attend_back_kernel, bk),
        grid=(width // 128, length // bq),
        in_specs=[row, row, row, row, full, full, zero, zero, tq, tq, tq, tk, tk, tk, ANY],
        out_specs=[row, full, full, zero, zero, sums],
        out_shape=[big, big, big, small, small]
        + [shape_of((extra.shape[0] // 4, extra.shape[1]), BF)],
        scratch_shapes=[pltpu.VMEM((length, 256), BF)] * 2
        + [pltpu.VMEM((128, length), BF)]
        + [pltpu.VMEM((length, 128), F32)] * 2
        + scatter_scratch(extra.shape[0] // 4, extra.shape[1]),
        compiler_params=local_params(collective_id=8, has_side_effects=True),
        cost_estimate=cost(40 * length * length * width, 20 * length * width),
        name="attend_back",
    )(queries, aug, mixed, grads, keys, values, key0, value0, *tables, *tables, extra)


def softmax_keys(scores, length):
    key = lax.broadcasted_iota(jnp.int32, scores.shape, 0)
    masked = jnp.where(key < length, scores, -1e9)
    exponent = jnp.exp2(masked - jnp.max(masked, axis=0, keepdims=True))
    return exponent * (1.0 / jnp.sum(exponent, axis=0, keepdims=True))


def cross_kernel(
    len_ref, f_ref, s_ref, g2_ref, g3_ref, wq_ref, wo_ref, kv_ref,
    as_ref, n2_ref, q_ref, m_ref, ac_ref, n3_ref,
):
    groups, model, width = wq_ref.shape
    after_self = f_ref[...].astype(F32) + s_ref[...]
    as_ref[...] = after_self
    unit, _ = norm_rows(after_self)
    normed = (unit * g2_ref[...]).astype(BF)
    n2_ref[...] = normed
    rows = normed.shape[0]
    lane = lanes((rows, 128))
    total = after_self
    for group in range(groups):
        queries = (dot(normed, wq_ref[group], NN) * (LOG2E / 8.0)).astype(BF)
        base = group * width
        q_ref[:, base : base + width] = queries
        for pair in range(width // 128):
            span = slice(128 * pair, 128 * pair + 128)
            values = kv_ref[group, :, width + 128 * pair : width + 128 * pair + 128]
            outs = []
            for head in range(2):
                scores = dot(kv_ref[group, :, span], half_mask(queries[:, span], head), NT)
                probs = softmax_keys(scores, len_ref[0])
                outs.append(dot(probs.astype(BF), values, TN))
            m_ref[:, base + 128 * pair : base + 128 * pair + 128] = jnp.where(
                lane < HD, outs[0], outs[1]
            ).astype(BF)
        total = total + dot(m_ref[:, base : base + width], wo_ref[group], NT)
    ac_ref[...] = total
    unit, _ = norm_rows(total)
    n3_ref[...] = (unit * g3_ref[...]).astype(BF)


def cross_forward(plen, frames, summed, gain2, gain3, weights, prompt_kv):
    share, model = frames.shape
    groups, _, both = weights.shape
    width = both // 2
    rows = 256
    block = pl.BlockSpec((rows, model), lambda i: (i, 0))
    gain = pl.BlockSpec((1, model), lambda i: (0, 0))
    once = pl.Buffered(1)
    return pl.pallas_call(
        cross_kernel,
        grid=(share // rows,),
        in_specs=[
            pl.BlockSpec(memory_space=pltpu.SMEM),
            block,
            block,
            gain,
            gain,
            pl.BlockSpec((groups, model, width), lambda i: (0, 0, 0), pipeline_mode=once),
            pl.BlockSpec((groups, model, width), lambda i: (0, 0, 1), pipeline_mode=once),
            pl.BlockSpec(prompt_kv.shape, lambda i: (0, 0, 0)),
        ],
        out_specs=[block] * 6,
        out_shape=[
            shape_of((share, model), F32),
            shape_of((share, model), BF),
            shape_of((share, model), BF),
            shape_of((share, model), BF),
            shape_of((share, model), F32),
            shape_of((share, model), BF),
        ],
        compiler_params=local_params(),
        cost_estimate=cost(4 * share * model * model, 4 * model * model + 20 * share * model),
        name="cross_forward",
    )(plen, frames, summed, gain2, gain3, weights, weights, prompt_kv)


def cross_back_kernel(
    len_ref, w_ref, go_ref, e_ref, ac_ref, as_ref, g2_ref, g3_ref, q_ref, wq_ref, wo_ref, kv_ref,
    t_ref, cb_ref, dq_ref, c3_ref, c3b_ref, dkv_ref, dg2_ref, dg3_ref, bo_ref, total_ref, dkv, hold, *scratch,
):
    groups, model, width = wq_ref.shape
    job = Scatter(t_ref, total_ref, scratch)
    last = pl.num_programs(0) - 1

    @pl.when(pl.program_id(0) == 0)
    def _():
        greet([job.to_sib, job.to_far])
        job.start()
        job.fold()
        job.local()

    @pl.when(pl.program_id(0) == 0)
    def _():
        dkv[...] = jnp.zeros_like(dkv)
        dg2_ref[...] = jnp.zeros_like(dg2_ref)
        dg3_ref[...] = jnp.zeros_like(dg3_ref)

    unit, spread = norm_rows(ac_ref[...])
    back, part = norm_back(e_ref[...], unit, spread, g3_ref[...])
    dg3_ref[...] += part
    carried = go_ref[...].astype(F32) * w_ref[0] + back
    cross_back = carried.astype(BF)
    cb_ref[...] = cross_back
    rows = cross_back.shape[0]
    lane = lanes((rows, 128))
    total = jnp.zeros((rows, model), F32)
    for group in range(groups):
        grads = dot(cross_back, wo_ref[group], NN).astype(BF)
        base = group * width
        for pair in range(width // 128):
            span = slice(128 * pair, 128 * pair + 128)
            vspan = slice(width + 128 * pair, width + 128 * pair + 128)
            wide = slice(base + 128 * pair, base + 128 * pair + 128)
            outs = []
            for head in range(2):
                queries = half_mask(q_ref[:, wide], head)
                masked = half_mask(grads[:, span], head)
                probs = softmax_keys(dot(kv_ref[group, :, span], queries, NT), len_ref[0])
                dprobs = dot(kv_ref[group, :, vspan], masked, NT)
                inner = jnp.sum(dprobs * probs, axis=0, keepdims=True)
                ds = (probs * (dprobs - inner)).astype(BF)
                outs.append(dot(ds, kv_ref[group, :, span], TN))
                dkv[group, :, span] += dot(ds, queries, NN) * (1.0 / LOG2E)
                dkv[group, :, vspan] += dot(probs.astype(BF), masked, NN)
            dq_ref[:, wide] = (jnp.where(lane < HD, outs[0], outs[1]) * 0.125).astype(BF)
        total = total + dot(dq_ref[:, base : base + width], wq_ref[group], NT)
    unit, spread = norm_rows(as_ref[...])
    back, part = norm_back(total, unit, spread, g2_ref[...])
    dg2_ref[...] += part
    carried = carried + back
    c3_ref[...] = carried
    c3b_ref[...] = carried.astype(BF)
    hold[pl.ds(pl.multiple_of(pl.program_id(0) * rows, rows), rows), :] = ac_ref[...]

    @pl.when(pl.program_id(0) == last)
    def _():
        job.land()
        bo_ref[...] = (hold[...] + total_ref[...]).astype(BF)
        dkv_ref[...] = dkv[...].astype(BF)
        job.finish()


def cross_backward(plen, weight, grad_out, summed, after_cross, after_self, gain2, gain3,
                   queries, weights, prompt_kv, term):
    share, model = grad_out.shape
    groups, _, both = weights.shape
    width = both // 2
    rows = 256
    block = pl.BlockSpec((rows, model), lambda i: (i, 0))
    gain = pl.BlockSpec((1, model), lambda i: (0, 0))
    smem = pl.BlockSpec(memory_space=pltpu.SMEM)
    once = pl.Buffered(1)
    return pl.pallas_call(
        cross_back_kernel,
        grid=(share // rows,),
        in_specs=[
            smem,
            smem,
            block,
            block,
            block,
            block,
            gain,
            gain,
            block,
            pl.BlockSpec((groups, model, width), lambda i: (0, 0, 0), pipeline_mode=once),
            pl.BlockSpec((groups, model, width), lambda i: (0, 0, 1), pipeline_mode=once),
            pl.BlockSpec(prompt_kv.shape, lambda i: (0, 0, 0)),
            ANY,
        ],
        out_specs=[block, block, block, block, pl.BlockSpec(prompt_kv.shape, lambda i: (0, 0, 0)),
                   gain, gain, pl.BlockSpec((share, model), lambda i: (0, 0))],
        out_shape=[
            shape_of((share, model), BF),
            shape_of((share, model), BF),
            shape_of((share, model), F32),
            shape_of((share, model), BF),
            shape_of(prompt_kv.shape, BF),
            shape_of((1, model), F32),
            shape_of((1, model), F32),
            shape_of((share, model), BF),
        ],
        scratch_shapes=[
            pltpu.VMEM((share, model), F32),
            pltpu.VMEM(prompt_kv.shape, F32),
            pltpu.VMEM((share, model), F32),
        ]
        + scatter_scratch(share, model),
        compiler_params=local_params(collective_id=9, has_side_effects=True),
        cost_estimate=cost(4 * share * model * model, 4 * model * model + 24 * share * model),
        name="cross_backward",
    )(plen, weight, grad_out, summed, after_cross, after_self, gain2, gain3, queries,
      weights, weights, prompt_kv, term)


def glu_kernel(scaled, *refs):
    if scaled:
        n_ref, c_ref, w_ref, h_ref, d_ref = refs
        cot = c_ref[...]
    else:
        s_ref, n_ref, c_ref, w_ref, h_ref, d_ref, o_ref = refs
        cot = (c_ref[...].astype(F32) * s_ref[0]).astype(BF)
        o_ref[...] = cot
    width = h_ref.shape[1]
    normed = n_ref[...]
    piece = 256
    for base in range(0, width, piece):
        gate = dot(normed, w_ref[:, base : base + piece], NN)
        up = dot(normed, w_ref[:, width + base : width + base + piece], NN)
        grads = dot(cot, w_ref[:, 2 * width + base : 2 * width + base + piece], NN)
        sig = 1.0 / (1.0 + jnp.exp(-gate))
        silu = gate * sig
        h_ref[:, base : base + piece] = (silu * up).astype(BF)
        grad_gate = grads * up * sig * (1.0 + gate * (1.0 - sig))
        d_ref[:, base : base + piece] = grad_gate.astype(BF)
        d_ref[:, width + base : width + base + piece] = (grads * silu).astype(BF)


def glu_block(normed, cot, weights, scale=None):
    length, model = normed.shape
    width = weights.shape[1] // 3
    rows = 512
    block = pl.BlockSpec((rows, model), lambda i: (i, 0))
    first = scale is not None
    return pl.pallas_call(
        functools.partial(glu_kernel, not first),
        grid=(length // rows,),
        in_specs=[pl.BlockSpec(memory_space=pltpu.SMEM)] * first
        + [
            block,
            block,
            pl.BlockSpec(weights.shape, lambda i: (0, 0), pipeline_mode=pl.Buffered(1)),
        ],
        out_specs=[
            pl.BlockSpec((rows, width), lambda i: (i, 0)),
            pl.BlockSpec((rows, 2 * width), lambda i: (i, 0)),
        ]
        + [block] * first,
        out_shape=[shape_of((length, width), BF), shape_of((length, 2 * width), BF)]
        + [shape_of((length, model), BF)] * first,
        compiler_params=local_params(),
        cost_estimate=cost(6 * length * model * width, 6 * length * model),
        name="glu_block_%d" % width,
    )(*([scale] if first else []), normed, cot, weights)


def grads_kernel(picks, count, *refs):
    lefts, rest = refs[:count], refs[count:]
    out = rest[-1]
    base = 0
    for at, pick in enumerate(picks):
        right = rest[at][...]
        total = dot(lefts[pick][...], right, TN)
        if len(rest) > len(picks) + 1:
            edge, edges = rest[len(picks)], rest[len(picks) + 1 + at]
            total = total + dot(edge[...], edges[...], TN)
        out[:, base : base + right.shape[1]] = total.astype(BF)
        base += right.shape[1]


def weight_grads(lefts, rights, picks, edge=None, edges=(), tile=256):
    length, model = lefts[0].shape
    wide = sum(right.shape[1] for right in rights)
    once = pl.Buffered(1)
    fixed = lambda i: (0, 0)
    in_specs = [pl.BlockSpec((length, tile), lambda i: (0, i)) for _ in lefts]
    in_specs += [pl.BlockSpec(right.shape, fixed, pipeline_mode=once) for right in rights]
    extra = []
    if edge is not None:
        in_specs.append(pl.BlockSpec((edge.shape[0], tile), lambda i: (0, i)))
        in_specs += [pl.BlockSpec(array.shape, fixed) for array in edges]
        extra = [edge, *edges]
    return pl.pallas_call(
        functools.partial(grads_kernel, picks, len(lefts)),
        grid=(model // tile,),
        in_specs=in_specs,
        out_specs=pl.BlockSpec((tile, wide), lambda i: (i, 0)),
        out_shape=shape_of((model, wide), BF),
        compiler_params=local_params(),
        cost_estimate=cost(2 * length * model * wide, 2 * length * (2 * model + wide)),
        name="weight_grads_%d" % wide,
    )(*lefts, *rights, *extra)


def spread_dp(share):
    return lax.all_gather(share, "dp", axis=0, tiled=True)


def owner_sum(term):
    return lax.psum_scatter(term, "dp", scatter_dimension=0, tiled=True)


def after(value, *others):
    return lax.optimization_barrier((value,) + others)[0]


GLU_PARTS = ((0, 1), (1, 6))


def per_device(
    frames, cond_table, bucket_ids, prompt, prompt_len,
    attn_query, attn_key, attn_value, attn_out,
    cross_query, cross_key, cross_value, cross_out,
    glu_gate, glu_up, glu_down, first_gain, second_gain, third_gain, grad_out,
):
    groups = lax.axis_size("mp")
    count = lax.axis_size("dp")
    sequences = bucket_ids.shape[0]
    assert sequences == 1 and groups == 4
    share, model = frames.shape
    length = share * groups
    buckets = cond_table.shape[0]
    own_rows, width = attn_query.shape
    unit = glu_gate.shape[1] // GLU_PARTS[-1][1]
    context = prompt.shape[2]

    onehot = (bucket_ids[:, None] == jnp.arange(buckets)[None, :]).astype(F32)
    extra = jnp.concatenate(
        [
            first_gain[:, None],
            second_gain[:, None],
            third_gain[:, None],
            jnp.broadcast_to(onehot.astype(BF), (own_rows, buckets)),
            jnp.zeros((own_rows, 128 - 3 - buckets), BF),
        ],
        1,
    )
    prompt_pack = jnp.concatenate([cross_key, cross_value], 1).reshape(own_rows, width)
    packed = jnp.concatenate(
        [attn_query, attn_key, attn_value, extra, attn_out, prompt_pack, cross_query, cross_out], 1
    )
    frames_all, grad_all, first = head_gather(frames, grad_out, packed, count)
    glu_gate, glu_up, glu_down, first = lax.optimization_barrier(
        (glu_gate, glu_up, glu_down, first)
    )
    second = first[:, 3 * width + 128 : 5 * width + 128]
    glu_share = []
    for low, high in GLU_PARTS:
        span = slice(low * unit, high * unit)
        glu_share.append(
            jnp.concatenate([glu_gate[:, span], glu_up[:, span], glu_down[:, span]], 1)
        )
    glu_rest = spread_dp(glu_share[1])

    side = first[:, 3 * width : 3 * width + 128]
    gains = dot(jnp.eye(8, 128, dtype=BF), side, NT)
    gain1, gain2, gain3 = gains[0:1], gains[1:2], gains[2:3]
    marks = side.reshape(count, own_rows, 128)[:, 0, 3 : 3 + buckets]
    counts = jnp.sum(marks.astype(F32), 0)
    seq_weight = sequences * count / (buckets * jnp.sum(onehot * counts[None, :], 1))

    tables = rope_tables(length, 1.0)
    cond_row = dot(onehot.astype(BF), cond_table, NN)
    unit_cond, spread_cond = norm_rows(cond_row)
    normed_cond = jnp.pad((unit_cond * gain1).astype(BF), ((0, 15), (0, 0)))
    kv0 = dot(normed_cond, first[:, width : 3 * width], NN).astype(BF)
    key0, value0 = kv0[:, :width], kv0[:, width:]
    normed_one, queries, keys, values = qkv_project(frames_all, gain1, first, tables, width)
    mixed, aug, cross_full, glu_first = attend(
        queries, keys, values, key0, value0, first, 5 * width + 128, glu_share[0], count
    )
    glu_full = (glu_first, glu_rest)
    cross_full = cross_full.reshape(groups, model, 2 * width)
    out_full = second[:, :width]
    prompt_full = second[:, width:].reshape(context, 2 * width)
    prompt_local = dot(prompt[0], prompt_full, NN).astype(BF)
    self_out, prompt_kv = out_project(mixed, out_full, prompt_local)
    prompt_kv = prompt_kv.reshape(groups, prompt.shape[1], 2 * width)

    after_self, normed_two, cross_q, cross_mixed, after_cross, normed_three = cross_forward(
        prompt_len, frames, self_out, gain2, gain3, cross_full, prompt_kv
    )
    normed_three = plain_gather(normed_three, 2)

    h0, d0, cot_all = glu_block(normed_three, grad_all, glu_full[0], seq_weight)
    pack0 = weight_grads([normed_three, cot_all], [d0, h0], (0, 1))
    h1, d1 = glu_block(after(normed_three, pack0), cot_all, glu_full[1])
    pack1 = weight_grads([normed_three, cot_all], [d1, h1], (0, 1))
    glu_grads = [owner_sum(pack0)]
    glu_grads.append(owner_sum(pack1))
    back_term, out_term = glu_back([after(d0, pack1), d1], [h0, h1], glu_full)

    cross_back, grad_cq, carried, carried_low, grad_kv, dg2, dg3, block_out = cross_backward(
        prompt_len, seq_weight, grad_out, back_term, after_cross, after_self, gain2, gain3,
        cross_q, cross_full, prompt_kv, out_term,
    )
    cross_term, grad_mixed, grad_out_weight, grad_kv = mid_gather(
        carried_low, grad_kv.reshape(-1, 2 * width), normed_two, cross_back, grad_cq, cross_mixed,
        out_full, mixed, groups,
    )
    grad_prompt = dot(prompt[0], grad_kv.astype(BF), TN).astype(BF).reshape(model, width)
    second_pack = jnp.concatenate([grad_out_weight, grad_prompt], 1)
    dq, dk, dv, dk0, dv0, cross_sum = attend_back(
        queries, aug, mixed, grad_mixed, keys, values, key0, value0, tables, cross_term
    )
    second_grad = owner_sum(after(second_pack, glu_grads[1], dk0))
    dk0 = dk0.astype(BF)
    dv0 = dv0.astype(BF)
    first_pack = weight_grads(
        [normed_one], [dq, dk, dv], (0, 0, 0), normed_cond, [jnp.zeros_like(dk0), dk0, dv0]
    )
    cond_term = dot(dk0, first[:, width : 2 * width], NT) + dot(
        dv0, first[:, 2 * width : 3 * width], NT
    )
    cond_back, dg1_cond = norm_back(cond_term[:1], unit_cond, spread_cond, gain1)
    mark = jnp.pad(onehot.T, ((0, SMALL - buckets), (0, 0)))
    frames_grad, sums, *first_grads = tail_sums(
        count, buckets, [dq, dk, dv], first, first_pack, cross_sum, frames, carried, gain1, dg2,
        dg3, mark, cond_back, dg1_cond,
    )

    second_grad = second_grad.astype(F32)
    prompt_grad = second_grad[:, width:].reshape(context // count, 2 * width)
    glu_out = []
    for i in range(3):
        cuts = []
        for (low, high), grad in zip(GLU_PARTS, glu_grads):
            size = (high - low) * unit
            cuts.append(grad[:, i * size : (i + 1) * size].astype(F32))
        glu_out.append(jnp.concatenate(cuts, 1))
    return (
        block_out,
        frames_grad,
        sums[:buckets],
        *first_grads[:3],
        second_grad[:, :width],
        first_grads[3],
        prompt_grad[:, :width],
        prompt_grad[:, width:],
        first_grads[4],
        glu_out[0],
        glu_out[1],
        glu_out[2],
        sums[buckets],
        sums[buckets + 1],
        sums[buckets + 2],
    )


def solution(mesh):
    both = P(("dp", "mp"), None)
    weight = P("dp", "mp")
    return jax.shard_map(
        per_device,
        mesh=mesh,
        in_specs=(both, P(), P("dp"), P("dp", None, None), P("dp"))
        + (weight,) * 11
        + (P("dp"),) * 3
        + (both,),
        out_specs=(both, both, P()) + (weight,) * 11 + (P(),) * 3,
        check_vma=False,
    )
```

time: 1530 us -> 841 us (0.55)
  waiting for transfers between devices: 637 us -> 21.4 us
  Pallas kernels: 614 us -> 736 us
  matrix products: 94.7 us -> 9.3 us
  local copies, waits for them, and re-layouts: 88.2 us -> 31 us
  other arithmetic: 56.9 us -> 14.4 us
    unnamed x20 -> x4, waiting for transfers between devices: 454 us -> 0.73 us
    all_gather x4 -> x1, waiting for transfers between devices: 137 us -> 0.01 us  [spread_dp(): return lax.all_gather(share, 'dp', axis=0, tiled=True)]
    pallas_call x14 -> x12, Pallas kernels: 448 us -> 558 us  [the longest x1 102 us: head_gather(): pl.pallas_call(functools.partial(head_kernel, count), out_shape=(wide, wi...]
    dot_general x17 -> x7, matrix products: 87.1 us -> 9.3 us  [dot(): return lax.dot_general(left, right, dims, preferred_element_type=F32)]
    unnamed x81 -> x51, local copies, waits for them, and re-layouts: 52.9 us -> 9.69 us
    reduce_scatter x3, waiting for transfers between devices: 46.1 us -> 20.7 us  [owner_sum(): return lax.psum_scatter(term, 'dp', scatter_dimension=0, tiled=True)]
    concatenate x11 -> x3, other arithmetic: 25 us -> 5.72 us  [the longest x1 2.88 us: per_device(): second_pack = jnp.concatenate([grad_out_weight, grad_prompt], 1)]
  transfers between devices with their start and end apart: 15 -> 4, of which waited for: 8 -> 1; matrix products, arithmetic and copies ran while one was open for 15% -> 4% of each run, Pallas kernels for 32% -> 68%
where the time goes in v2:
time: 841 us; the launch traced here: 831 us
  Pallas kernels  736 us (88%)
  local copies, waits for them, and re-layouts  31 us (4%)
  waiting for transfers between devices  21.4 us (3%)
  between operations  19.1 us (2%)
  other arithmetic  14.4 us (2%)
  matrix products  9.3 us (1%)
    pallas_call x1, Pallas kernels, head_gather(): pl.pallas_call(functools.partial(head_kernel, count), out_shape=(wide, wi...  102 us
    pallas_call x1, Pallas kernels, tail_sums(): pl.pallas_call(functools.partial(tail_kernel, count, buckets), grid=(9,),...  96 us
    pallas_call x1, Pallas kernels, attend_back(): pl.pallas_call(functools.partial(attend_back_kernel, bk), grid=(width //...  90.9 us
    pallas_call x1, Pallas kernels, attend(): pl.pallas_call(functools.partial(attend_kernel, bk, first, count), grid=(...  66.4 us
    pallas_call x3, Pallas kernels, weight_grads(): pl.pallas_call(functools.partial(grads_kernel, picks, len(lefts)), grid=(...  60.4 us
    pallas_call x1, Pallas kernels, glu_back(): pl.pallas_call(glu_back_kernel, grid=(16,), out_shape=(shape_of((share, m...  56.1 us
    pallas_call x1, Pallas kernels, cross_backward(): pl.pallas_call(cross_back_kernel, grid=(share // rows,), in_specs=[smem,...  49.9 us
    pallas_call x1, Pallas kernels, mid_gather(): pl.pallas_call(mid_kernel, grid=(12,), in_specs=[fixed, ANY, left, left,...  49.7 us
  transfers between devices with their start and end apart: 4, of which 1 were waited for; matrix products, arithmetic and copies ran while one was open for 4% of the time, Pallas kernels for 68%

profile of v2, /device:TPU:0, one launch (start us, length us, event | category | flops | bytes accessed | tf_op | source)
XLA Modules:
  0.0 831.1 jit_solution(9212131370323686641)
XLA Ops:
  8.0 0.7 broadcast_in_dim.34
  8.7 0.7 broadcast_in_dim.35
  9.5 0.7 broadcast_in_dim.36
  10.2 0.9 pad_maximum_fusion.3
  11.2 3.0 concatenate.34.w_ref
  14.3 101.7 %head_gather.1 = (bf16[2048,1536]{1,0:T(8,128)(2,1)}, bf16[2048,1536]{1,0:T(8,128)(2,1)}, bf16[1536,2816]{1,0:T(8,128)(2,1)}) custom-call(bf16[512,1536]{1,0:T(8,128)(2,1)} %f_ref.5, bf16[512,1536]{1,0:T(8,128)(2,1)} %go_ref.1, bf16[192,2816]{1,0:T(8,128)(2,1)} %concatenate.34.w_ref), custom_call_target="tpu_custom_call" | custom-call | flops 1 | bytes 146800640 | tf_op jit(solution)/shard_map/head_gather/pallas_call | solution.py:473
  116.0 1.0 slice-done
  117.3 1.2 pad_maximum_fusion.1
  118.6 0.7 copy-done.21
  119.4 0.6 reduce_sum.60
  120.7 0.6 multiply_reduce_fusion
  122.0 2.9 fusion.26
  125.9 0.7 pad_maximum_fusion.2.w_ref
  126.7 1.2 fusion.16
  127.9 0.6 copy-done.12
  128.5 0.6 fusion.31
  129.2 2.1 fusion.8
  131.2 0.6 fusion.32
  131.9 1.0 fusion.7.kv_ref
  132.9 16.5 %qkv_project.1 = (bf16[2048,1536]{1,0:T(8,128)(2,1)}, bf16[2048,384]{1,0:T(8,128)(2,1)}, bf16[2048,384]{1,0:T(8,128)(2,1)}, bf16[2048,384]{1,0:T(8,128)(2,1)}) custom-call(bf16[2048,1536]{1,0:T(8,128)(2,1)} %get-tuple-element.77.x_ref, f32[1,1536]{1,0:T(1,128)} %get-tuple-element.155.g_ref.g1_ref, ...), custom_call_target="tpu_custom_call" | custom-call | flops 7247757312 | bytes 25165824 | tf_op jit(solution)/shard_map/qkv_project/pallas_call | solution.py:910
  149.3 66.4 %attend.1 = (bf16[2048,384]{1,0:T(8,128)(2,1)}, bf16[2048,384]{1,0:T(8,128)(2,1)}, bf16[6144,768]{1,0:T(8,128)(2,1)}, bf16[1536,768]{1,0:T(8,128)(2,1)}) custom-call(bf16[2048,384]{1,0:T(8,128)(2,1)} %get-tuple-element.78.q_ref, bf16[2048,384]{1,0:T(8,128)(2,1)} %get-tuple-element.79.k_ref, bf16[2048,384]{1,0:T(8,128)(2,1)} %get-tuple-element.80.v_ref, ...), custom_call_target="tpu_custom_call" | custom-call | flops 25769803776 | bytes 7864320 | tf_op jit(solution)/shard_map/attend/pallas_call | solution.py:997
  215.8 44.7 %out_project.1 = (f32[512,1536]{1,0:T(8,128)}, bf16[512,768]{1,0:T(8,128)(2,1)}) custom-call(bf16[2048,384]{1,0:T(8,128)(2,1)} %get-tuple-element.84.m_ref.o_ref, bf16[1536,384]{1,0:T(8,128)(2,1)} %get-tuple-element.140.w_ref, bf16[128,768]{1,0:T(8,128)(2,1)} %fusion.7.kv_ref), custom_call_target="tpu_custom_call" | custom-call | flops 1 | bytes 146800640 | tf_op jit(solution)/shard_map/out_project/pallas_call | solution.py:680
  261.1 20.0 %cross_forward.1 = (f32[512,1536]{1,0:T(8,128)}, bf16[512,1536]{1,0:T(8,128)(2,1)}, bf16[512,1536]{1,0:T(8,128)(2,1)}, bf16[512,1536]{1,0:T(8,128)(2,1)}, f32[51...) custom-call(s32[1]{0:T(128)S(6)} %copy.56.len_ref, bf16[512,1536]{1,0:T(8,128)(2,1)} %f_ref.5, ...), custom_call_target="tpu_custom_call" | custom-call | flops 4831838208 | bytes 25165824 | tf_op jit(solution)/shard_map/cross_forward/pallas_call | solution.py:1178
  281.1 38.5 %plain_gather_2.1.refs_1_.refs_0_ = bf16[2048,1536]{1,0:T(8,128)(2,1)} custom-call(bf16[512,1536]{1,0:T(8,128)(2,1)} %get-tuple-element.88.x_ref), custom_call_target="tpu_custom_call" | custom-call | flops 1 | bytes 146800640 | tf_op jit(solution)/shard_map/plain_gather_2/pallas_call | solution.py:437
  319.6 1.0 slice.102
  320.7 0.6 fusion.18
  322.0 11.9 %glu_block_256.1 = (bf16[2048,256]{1,0:T(8,128)(2,1)}, bf16[2048,512]{1,0:T(8,128)(2,1)}, bf16[2048,1536]{1,0:T(8,128)(2,1)}) custom-call(f32[1]{0:T(128)} %bitcast.2.refs_0_.w_ref, bf16[2048,1536]{1,0:T(8,128)(2,1)} %plain_gather_2.1.refs_1_.refs_0_, bf16[2048,1536]{1,0:T(8,128)(2,1)} %get-tuple-element.89.refs_2_, ...), custom_call_target="tpu_custom_call" | custom-call | flops 4831838208 | bytes 18874368 | tf_op jit(solution)/shard_map/glu_block_256/pallas_call | solution.py:1354
  333.9 11.2 %weight_grads_768.1 = bf16[1536,768]{1,0:T(8,128)(2,1)} custom-call(bf16[2048,1536]{1,0:T(8,128)(2,1)} %plain_gather_2.1.refs_1_.refs_0_, bf16[2048,1536]{1,0:T(8,128)(2,1)} %get-tuple-element.92.refs_1_, bf16[2048,512]{1,0:T(8,128)(2,1)} %get-tuple-element.97.refs_2_.d0_ref, bf16[2048,256]{1,0:T(8,128)(2,1)} %get-tuple-element.93.refs_3_.h0_ref), custom_call_target="tpu_custom_call" | custom-call | flops 4831838208 | bytes 15728640 | tf_op jit(solution)/shard_map/weight_grads_768/pallas_call | solution.py:1402
  345.1 33.1 %glu_block_1280.1 = (bf16[2048,1280]{1,0:T(8,128)(2,1)}, bf16[2048,2560]{1,0:T(8,128)(2,1)}) custom-call(bf16[2048,1536]{1,0:T(8,128)(2,1)} %plain_gather_2.1.refs_1_.refs_0_, bf16[2048,1536]{1,0:T(8,128)(2,1)} %get-tuple-element.92.refs_1_, bf16[1536,3840]{1,0:T(8,128)(2,1)} %all-gather.2.cloned.1.call-done.refs_2_.g1_ref.w1_ref), custom_call_target="tpu_custom_call" | custom-call | flops 24159191040 | bytes 18874368 | tf_op jit(solution)/shard_map/glu_block_1280/pallas_call | solution.py:1354
  378.2 33.2 %weight_grads_3840.1 = bf16[1536,3840]{1,0:T(8,128)(2,1)} custom-call(bf16[2048,1536]{1,0:T(8,128)(2,1)} %plain_gather_2.1.refs_1_.refs_0_, bf16[2048,1536]{1,0:T(8,128)(2,1)} %get-tuple-element.92.refs_1_, bf16[2048,2560]{1,0:T(8,128)(2,1)} %get-tuple-element.95.refs_2_.d1_ref, bf16[2048,1280]{1,0:T(8,128)(2,1)} %get-tuple-element.96.refs_3_.h1_ref), custom_call_target="tpu_custom_call" | custom-call | flops 24159191040 | bytes 28311552 | tf_op jit(solution)/shard_map/weight_grads_3840/pallas_call | solution.py:1402
  411.5 0.7 reduce-scatter.8.cloned.1.call-update
  412.2 56.1 %glu_back.1 = (f32[512,1536]{1,0:T(8,128)}, bf16[2048,1536]{1,0:T(8,128)(2,1)}) custom-call(bf16[2048,512]{1,0:T(8,128)(2,1)} %get-tuple-element.97.refs_2_.d0_ref, bf16[2048,2560]{1,0:T(8,128)(2,1)} %get-tuple-element.95.refs_2_.d1_ref, bf16[1536,768]{1,0:T(8,128)(2,1)} %get-tuple-element.90.refs_3_.g0_ref.w0_ref, ...), custom_call_target="tpu_custom_call" | custom-call | flops 1 | bytes 146800640 | tf_op jit(solution)/shard_map/glu_back/pallas_call | solution.py:742
  468.4 49.9 %cross_backward.1 = (bf16[512,1536]{1,0:T(8,128)(2,1)}, bf16[512,1536]{1,0:T(8,128)(2,1)}, f32[512,1536]{1,0:T(8,128)}, bf16[512,1536]{1,0:T(8,128)(2,1)}, bf16[...) custom-call(s32[1]{0:T(128)S(6)} %copy.56.len_ref, ...), custom_call_target="tpu_custom_call" | custom-call | flops 4831838208 | bytes 28311552 | tf_op jit(solution)/shard_map/cross_backward/pallas_call | solution.py:1282
  518.2 49.7 %mid_gather.1 = (bf16[6144,768]{1,0:T(8,128)(2,1)}, bf16[2048,384]{1,0:T(8,128)(2,1)}, bf16[1536,384]{1,0:T(8,128)(2,1)}, f32[128,768]{1,0:T(8,128)}) custom-call(bf16[512,1536]{1,0:T(8,128)(2,1)} %get-tuple-element.105.c_ref, bf16[512,768]{1,0:T(8,128)(2,1)} %bitcast.32, bf16[512,1536]{1,0:T(8,128)(2,1)} %get-tuple-element.107.n_ref, ...), custom_call_target="tpu_custom_call" | custom-call | flops 1 | bytes 146800640 | tf_op jit(solution)/shard_map/mid_gather/pallas_call | solution.py:851
  567.9 1.5 fusion.2
  569.4 0.6 copy.46
  570.5 2.9 pad_maximum_fusion
  573.4 90.9 %attend_back.1 = (bf16[2048,384]{1,0:T(8,128)(2,1)}, bf16[2048,384]{1,0:T(8,128)(2,1)}, bf16[2048,384]{1,0:T(8,128)(2,1)}, f32[16,384]{1,0:T(8,128)}, f32[16,384]{1,0:T(8,128)}, /*index=5*/bf16[1536,768]{1,0:T(8,128)(2,1)}) custom-call(bf16[2048,384]{1,0:T(8,128)(2,1)} %get-tuple-element.78.q_ref, bf16[2048,384]{1,0:T(8,128)(2,1)} %get-tuple-element.104.aug_ref, ...), custom_call_target="tpu_custom_call" | custom-call | flops 64424509440 | bytes 15728640 | tf_op jit(solution)/shard_map/attend_back/pallas_call | solution.py:1112
  664.4 0.6 copy-done.18
  665.0 0.6 pad.10.refs_4_
  665.6 0.6 pad_convert_fusion.mark_ref
  666.2 20.7 %reduce-scatter.8.cloned.1.call-done = bf16[192,768]{1,0:T(8,128)(2,1)} async-done(((bf16[1536,768]{1,0:T(8,128)(2,1)}), bf16[192,768]{1,0:T(8,128)(2,1)}) %reduce-scatter.8.cloned.1.call-update) | async-done | bytes 294928 | tf_op jit(solution)/shard_map/reduce_scatter | solution.py:1419
  686.9 1.0 fusion.28
  688.0 1.7 fusion.3
  689.7 1.7 fusion.5
  691.4 2.0 fusion.24
  694.7 0.6 subtract_multiply_fusion.1.cb_ref
  695.3 0.6 broadcast_in_dim.33.refs_5_
  695.9 16.0 %weight_grads_1152.1.a_ref = bf16[1536,1152]{1,0:T(8,128)(2,1)} custom-call(bf16[2048,1536]{1,0:T(8,128)(2,1)} %get-tuple-element.116.refs_0_, bf16[2048,384]{1,0:T(8,128)(2,1)} %get-tuple-element.113.refs_1_.q_ref, bf16[2048,384]{1,0:T(8,128)(2,1)} %get-tuple-element.114.refs_2_.k_ref, bf16[2048,384]{1,0:T(8,128)(2,1)} %get-tuple-element.115.refs_3_.v_ref, ...), custom_call_target="tpu_custom_call" | custom-call | flops 7247757312 | bytes 17301504 | tf_op jit(solution)/shard_map/weight_grads_1152/pallas_call | solution.py:1402
  712.0 96.0 %tail_sums.1 = (f32[512,1536]{1,0:T(8,128)}, f32[16,1536]{1,0:T(8,128)}, f32[192,384]{1,0:T(8,128)}, f32[192,384]{1,0:T(8,128)}, f32[192,384]{1,0:T(8,128)}, /*index=5*/f32[192,384]{1,0:T(8,128)}, f32[192,384]{1,0:T(8,128)}) custom-call(bf16[2048,384]{1,0:T(8,128)(2,1)} %get-tuple-element.113.refs_1_.q_ref, ...), custom_call_target="tpu_custom_call" | custom-call | flops 1 | bytes 146800640 | tf_op jit(solution)/shard_map/tail_sums/pallas_call | solution.py:624
  807.9 1.4 slice.121
  809.4 1.6 slice_reduce_fusion
  811.0 1.1 maximum_convert_fusion.2
  812.2 1.7 maximum_convert_fusion
  813.9 1.9 fusion.30
  815.8 0.7 fusion.29
  816.5 1.1 copy.57
  817.7 1.3 copy-done.2
  819.0 1.7 copy.58
  820.7 0.7 copy.59
  821.4 0.7 copy.60
  822.1 0.7 copy.61
  822.8 0.7 copy.62
  823.6 0.7 copy.63
  (76 shorter events, 2.7 us)
Async XLA Ops:
  7.2 124.7 %copy-start = (bf16[1,128,768]{2,1,0:T(8,128)(2,1)S(1)}, bf16[1,128,768]{2,1,0:T(8,128)(2,1)}, u32[]{:S(2)}) copy-start(bf16[1,128,768]{2,1,0:T(8,128)(2,1)} %param.26) | copy-start | bytes 589828
  7.2 337.9 %all-gather.2.cloned.1.call-start = ((), (), s32[]{:S(2)}) async-start(), calls=%async_computation.3 | async-start | bytes 13271040 | tf_op jit(solution)/shard_map/all_gather | solution.py:1415
  116.0 1.0 slice-start
  116.0 1.2 slice-start.2
  116.0 1.3 slice-start.4
  118.5 0.7 copy-start.21
  118.6 545.8 %reduce-scatter.4.cloned.1.call-start = ((), (), s32[]{:S(2)}) async-start(), calls=%async_computation.4 | async-start | bytes 13271040 | tf_op jit(solution)/shard_map/reduce_scatter | solution.py:1419
  119.4 7.3 copy-start.10
  124.9 0.9 slice-start.1
  124.9 1.0 slice-start.3
  124.9 1.1 slice-start.5
  126.7 6.2 copy-start.13
  127.9 0.6 copy-start.12
  129.2 3.7 copy-start.17
  411.5 275.5 %reduce-scatter.8.cloned.1.call-start = ((), (), s32[]{:S(2)}) async-start(), calls=%async_computation.6 | async-start | bytes 2654208 | tf_op jit(solution)/shard_map/reduce_scatter | solution.py:1419
  412.2 401.7 %reduce-scatter.6.cloned.1.call-start = ((), (), s32[]{:S(2)}) async-start(), calls=%async_computation.5 | async-start | bytes 2654208 | tf_op jit(solution)/shard_map/reduce_scatter | solution.py:1419
  664.3 0.7 copy-start.18
  664.3 23.6 %copy-start.20 = (f32[16,384]{1,0:T(8,128)S(1)}, f32[16,384]{1,0:T(8,128)}, u32[]{:S(2)}) copy-start(f32[16,384]{1,0:T(8,128)} %get-tuple-element.117) | copy-start | bytes 73732
  664.3 23.7 %copy-start.19 = (f32[16,384]{1,0:T(8,128)S(1)}, f32[16,384]{1,0:T(8,128)}, u32[]{:S(2)}) copy-start(f32[16,384]{1,0:T(8,128)} %get-tuple-element.118) | copy-start | bytes 73732
  666.2 25.1 %copy-start.14 = (f32[1536]{0:T(1024)S(1)}, f32[1536]{0:T(1024)}, u32[]{:S(2)}) copy-start(f32[1536]{0:T(1024)} %copy-done.13) | copy-start | bytes 18436
  666.2 28.5 %copy-start.11 = (f32[1536]{0:T(1024)S(1)}, f32[1536]{0:T(1024)}, u32[]{:S(2)}) copy-start(f32[1536]{0:T(1024)} %copy-done.10) | copy-start | bytes 18436
  687.9 8.0 copy-start.15
  688.0 7.9 copy-start.16
  712.0 99.0 %copy-start.4 = (bf16[192,3840]{1,0:T(8,128)(2,1)S(1)}, bf16[192,3840]{1,0:T(8,128)(2,1)}, u32[]{:S(2)}) copy-start(bf16[192,3840]{1,0:T(8,128)(2,1)} %reduce-scatter.4.cloned.1.call-done) | copy-start | bytes 4423684
  813.9 2.7 copy-start.3
  816.5 2.5 copy-start.2
  819.0 1.7 copy-start.9
  819.0 2.4 copy-start.8
  819.0 3.1 copy-start.7
  819.0 5.3 copy-start.1
  820.7 2.2 copy-start.6
  820.7 2.9 copy-start.5
Sparse Core Ops, SparseCore 0:
  118.7 182.7 all-gather.1
  411.6 203.2 reduce-scatter.3
  618.8 68.0 reduce-scatter.7
  691.2 76.8 reduce-scatter.5

commit v3 on v2

v3 whole, which is shorter than its diff:
```python
import functools

import jax
import jax.numpy as jnp
import numpy as np
from jax import lax
from jax.experimental import pallas as pl
from jax.experimental.pallas import tpu as pltpu
from jax.sharding import PartitionSpec as P

HD = 64
ROT = 32
LOG2E = 1.4426950408889634
EPS = 1e-05
MESH = pl.DeviceIdType.MESH
NT = (((1,), (1,)), ((), ()))
TN = (((0,), (0,)), ((), ()))
NN = (((1,), (0,)), ((), ()))
BF = jnp.bfloat16
F32 = jnp.float32
ANY = pl.BlockSpec(memory_space=pl.ANY)
VM = 58 << 20


def shape_of(dims, dtype):
    return jax.ShapeDtypeStruct(dims, dtype)


def dot(left, right, dims):
    return lax.dot_general(left, right, dims, preferred_element_type=F32)


def local_params(**extra):
    return pltpu.CompilerParams(vmem_limit_bytes=VM, **extra)


def cost(flops, nbytes, trans=0):
    return pl.CostEstimate(flops=int(flops), bytes_accessed=int(nbytes), transcendentals=int(trans))


def norm_rows(values):
    center = values - jnp.mean(values, -1, keepdims=True)
    spread = lax.rsqrt(jnp.mean(center * center, -1, keepdims=True) + EPS)
    return center * spread, spread


def norm_back(grad_rows, unit_rows, spread, gain_row):
    scaled = grad_rows * gain_row
    result = spread * (
        scaled
        - jnp.mean(scaled, -1, keepdims=True)
        - unit_rows * jnp.mean(scaled * unit_rows, -1, keepdims=True)
    )
    return result, jnp.sum(grad_rows * unit_rows, 0, keepdims=True)


def rope_tables(length, offset):
    lane = np.arange(2 * HD) % HD
    half = ROT // 2
    frequency = np.power(10000.0, -2.0 * (lane % half) / ROT)
    angles = (offset + np.arange(length))[:, None] * frequency[None, :]
    cosine = np.where(lane[None] < ROT, np.cos(angles), 1.0)
    sine = np.sin(angles)
    upper = np.where((lane[None] >= half) & (lane[None] < ROT), sine, 0.0)
    lower = np.where(lane[None] < half, -sine, 0.0)
    return [jnp.asarray(table.astype(np.float32)) for table in (cosine, upper, lower)]


def rope(values, cosine, upper, lower):
    half = ROT // 2
    return (
        values * cosine
        + pltpu.roll(values, half, 1) * upper
        + pltpu.roll(values, 2 * HD - half, 1) * lower
    )


def lanes(dims):
    return lax.broadcasted_iota(jnp.int32, dims, 1)


def half_mask(values, head):
    lane = lanes(values.shape)
    keep = (lane < HD) if head == 0 else (lane >= HD)
    return jnp.where(keep, values, jnp.zeros_like(values))


def pieces(column, dims, base):
    high = column.astype(BF).astype(F32)
    rest = column - high
    middle = rest.astype(BF).astype(F32)
    low = rest - middle
    lane = lanes(dims)
    return jnp.where(
        lane == base,
        high,
        jnp.where(lane == base + 1, middle, jnp.where(lane == base + 2, low, 0.0)),
    )


def mp_peers():
    me = lax.axis_index("mp")
    chip, core = me // 2, me % 2
    return me, chip * 2 + (1 - core), (1 - chip) * 2 + core, (1 - chip) * 2 + (1 - core)


def greet(devices):
    barrier = pltpu.get_barrier_semaphore()
    for device in devices:
        pl.semaphore_signal(barrier, inc=1, device_id=device, device_id_type=MESH)
    pl.semaphore_wait(barrier, len(devices))


def remote(source, target, send, recv, device):
    return pltpu.make_async_remote_copy(
        source, target, send, recv, device_id=device, device_id_type=MESH
    )


CHUNKS = 4
CUTS = 2


def column_cuts(width):
    first = 128 * ((width // 128 + 1) // 2)
    return [pl.ds(0, first), pl.ds(first, width - first)]


BUSY = cost(1, 140 << 20)


def gather_scratch(rows, width):
    return [
        pltpu.VMEM((rows, width), BF),
        pltpu.SemaphoreType.DMA((2,)),
        pltpu.SemaphoreType.DMA((3, CHUNKS)),
        pltpu.SemaphoreType.DMA((3, CHUNKS)),
    ]


class Gather:
    def __init__(self, x_ref, o_ref, sems, columns=None, here=False):
        bounce, lsem, ssem, rsem = sems
        if here:
            bounce = x_ref
        self.me, self.sib, self.far, _ = mp_peers()
        dp = lax.axis_index("dp")
        self.to_sib = {"dp": dp, "mp": self.sib}
        self.to_far = {"dp": dp, "mp": self.far}
        rows = x_ref.shape[0]
        part = rows // CHUNKS

        def slot(i, k):
            return o_ref.at[pl.ds(pl.multiple_of(i * rows + k * part, part), part)]

        def source(first, size):
            if columns is None:
                return x_ref.at[pl.ds(first, size)]
            return x_ref.at[pl.ds(first, size), columns]

        self.load = None if here else pltpu.make_async_copy(source(0, rows), bounce, lsem.at[0])
        self.store = pltpu.make_async_copy(
            bounce, o_ref.at[pl.ds(pl.multiple_of(self.me * rows, rows), rows)], lsem.at[1]
        )
        self.across = []
        self.beside = []
        self.onward = []
        for k in range(CHUNKS):
            mine = source(k * part, part)
            self.across.append(
                remote(mine, slot(self.me, k), ssem.at[0, k], rsem.at[0, k], self.to_far)
            )
            self.beside.append(
                remote(mine, slot(self.me, k), ssem.at[1, k], rsem.at[1, k], self.to_sib)
            )
            self.onward.append(
                remote(
                    slot(self.far, k), slot(self.far, k), ssem.at[2, k], rsem.at[2, k], self.to_sib
                )
            )

    def start(self):
        for copy in self.across:
            copy.start()
        if self.load is not None:
            self.load.start()
        for copy in self.beside:
            copy.start()
        if self.load is not None:
            self.load.wait()
        self.store.start()

    def forward(self, k):
        self.across[k].wait_recv()
        self.onward[k].start()

    def finish(self):
        for k in range(CHUNKS):
            self.beside[k].wait_recv()
            self.onward[k].wait_recv()
        for k in range(CHUNKS):
            self.across[k].wait_send()
            self.beside[k].wait_send()
            self.onward[k].wait_send()
        self.store.wait()


def scatter_scratch(rows, width):
    return [pltpu.VMEM((2, rows, width), BF)] + [pltpu.VMEM((rows, width), BF)] * 4 + [
        pltpu.SemaphoreType.DMA((2,)),
        pltpu.SemaphoreType.DMA((3, CHUNKS)),
        pltpu.SemaphoreType.DMA((3, CHUNKS)),
    ]


class Scatter:
    def __init__(self, x_ref, o_ref, scratch):
        mine, ra, rb, rc, sb, lsem, ssem, rsem = scratch
        me, sib, far, diag = mp_peers()
        dp = lax.axis_index("dp")
        self.to_sib = {"dp": dp, "mp": sib}
        self.to_far = {"dp": dp, "mp": far}
        self.o_ref, self.mine, self.ra, self.rb, self.rc, self.sb = o_ref, mine, ra, rb, rc, sb
        rows = ra.shape[0]
        part = rows // CHUNKS
        self.spans = [pl.ds(k * part, part) for k in range(CHUNKS)]

        def slot(i, k):
            return x_ref.at[pl.ds(pl.multiple_of(i * rows + k * part, part), part)]

        def whole(i):
            return x_ref.at[pl.ds(pl.multiple_of(i * rows, rows), rows)]

        self.first, self.second, self.third = [], [], []
        for k, span in enumerate(self.spans):
            self.first.append(
                remote(slot(diag, k), ra.at[span], ssem.at[0, k], rsem.at[0, k], self.to_sib)
            )
            self.second.append(
                remote(slot(sib, k), rb.at[span], ssem.at[1, k], rsem.at[1, k], self.to_sib)
            )
            self.third.append(
                remote(sb.at[span], rc.at[span], ssem.at[2, k], rsem.at[2, k], self.to_far)
            )
        self.load0 = pltpu.make_async_copy(whole(far), mine.at[0], lsem.at[0])
        self.load1 = pltpu.make_async_copy(whole(me), mine.at[1], lsem.at[1])

    def start(self):
        self.load0.start()
        for copy in self.first:
            copy.start()
        self.load1.start()
        for copy in self.second:
            copy.start()

    def fold(self):
        self.load0.wait()
        for k, span in enumerate(self.spans):
            self.first[k].wait_recv()
            total = self.mine[0, span, :].astype(F32) + self.ra[span, :].astype(F32)
            self.sb[span, :] = total.astype(BF)
            self.third[k].start()

    def local(self):
        self.load1.wait()
        for k in range(CHUNKS):
            self.second[k].wait_recv()

    def land(self, addend=None):
        for k, span in enumerate(self.spans):
            self.third[k].wait_recv()
            total = self.mine[1, span, :].astype(F32) + self.rb[span, :].astype(F32)
            if addend is not None:
                total = total + addend[span, :]
            self.o_ref[span, :] = (total + self.rc[span, :].astype(F32)).astype(self.o_ref.dtype)

    def finish(self):
        for k in range(CHUNKS):
            self.first[k].wait_send()
            self.second[k].wait_send()
            self.third[k].wait_send()


def sum_scratch(rows, width):
    return [pltpu.VMEM((4, rows, width), BF)] + [pltpu.VMEM((rows, width), BF)] * 4 + [
        pltpu.SemaphoreType.DMA((3, CHUNKS)),
        pltpu.SemaphoreType.DMA((3, CHUNKS)),
    ]


class LocalSum:
    def __init__(self, o_ref, scratch):
        terms, ra, rb, rc, sb, ssem, rsem = scratch
        _, sib, far, _ = mp_peers()
        dp = lax.axis_index("dp")
        self.to_sib = {"dp": dp, "mp": sib}
        self.to_far = {"dp": dp, "mp": far}
        self.o_ref, self.terms, self.ra, self.rb, self.rc, self.sb = o_ref, terms, ra, rb, rc, sb
        rows = ra.shape[0]
        part = rows // CHUNKS
        self.spans = [pl.ds(k * part, part) for k in range(CHUNKS)]
        self.first, self.second, self.third = [], [], []
        for k, span in enumerate(self.spans):
            self.first.append(
                remote(terms.at[0, span], ra.at[span], ssem.at[0, k], rsem.at[0, k], self.to_sib)
            )
            self.second.append(
                remote(terms.at[2, span], rb.at[span], ssem.at[1, k], rsem.at[1, k], self.to_sib)
            )
            self.third.append(
                remote(sb.at[span], rc.at[span], ssem.at[2, k], rsem.at[2, k], self.to_far)
            )

    def put(self, step, value):
        half = value.shape[0]
        late = step // 4
        slot = (1 - late) * (step % 2) + late * (step // 2)
        row = (1 - late) * ((step // 2) % 2) + late * (step % 2)
        self.terms[slot, pl.ds(pl.multiple_of(row * half, half), half), :] = value

    def after_step(self, step):
        half = CHUNKS // 2
        for turn in range(2):
            chunks = range(turn * half, turn * half + half)

            @pl.when(step == 2 * turn)
            def _(chunks=chunks):
                for k in chunks:
                    self.first[k].start()

            @pl.when(step == 2 * turn + 1)
            def _(chunks=chunks):
                for k in chunks:
                    span = self.spans[k]
                    self.first[k].wait_recv()
                    total = self.terms[1, span, :].astype(F32) + self.ra[span, :].astype(F32)
                    self.sb[span, :] = total.astype(BF)
                    self.third[k].start()

        @pl.when(step == 5)
        def _():
            for copy in self.second:
                copy.start()

    def land(self):
        for k, span in enumerate(self.spans):
            self.second[k].wait_recv()
            self.third[k].wait_recv()
            total = self.terms[3, span, :].astype(F32) + self.rb[span, :].astype(F32)
            self.o_ref[span, :] = (total + self.rc[span, :].astype(F32)).astype(self.o_ref.dtype)

    def finish(self):
        for copy in self.first + self.second + self.third:
            copy.wait_send()


def order_block(step):
    me = lax.axis_index("mp")
    chip, core = me // 2, me % 2
    late = step // 4
    other = 1 - late
    cross = 1 - ((1 - late) * (step % 2) + late * ((step // 2) % 2))
    quarter = (chip + other - 2 * chip * other) * 2 + (core + cross - 2 * core * cross)
    return quarter * 2 + (1 - late) * ((step // 2) % 2) + late * (step % 2)


def arrival_quarter(turn):
    me = lax.axis_index("mp")
    chip, core = me // 2, me % 2
    other = turn // 2
    cross = turn % 2
    return (chip + other - 2 * chip * other) * 2 + (core + cross - 2 * core * cross)


class Ring:
    def __init__(self, count):
        self.count = count
        self.half = count // 2
        me = lax.axis_index("dp")
        mp = lax.axis_index("mp")
        odd = me % 2
        self.me = me
        self.spot = (1 - odd) * (me // 2) + odd * (count - 1 - me // 2)
        self.ahead = {"dp": self.at(1), "mp": mp}
        self.behind = {"dp": self.at(-1), "mp": mp}

    def at(self, distance):
        spot = (self.spot + distance + self.count) % self.count
        late = spot // self.half
        return (1 - late) * 2 * spot + late * (2 * (self.count - 1 - spot) + 1)


def ring_scratch(rows, width, half):
    return [pltpu.VMEM((rows, width), BF), pltpu.SemaphoreType.DMA((2,))] + [
        pltpu.SemaphoreType.DMA((half, CUTS))
    ] * 4


class RingGather:
    def __init__(self, count, w_ref, o_ref, scratch):
        bounce, lsem, fs, fr, bs, br = scratch
        ring = Ring(count)
        self.ahead, self.behind, self.half = ring.ahead, ring.behind, ring.half
        rows = w_ref.shape[0]

        spans = column_cuts(w_ref.shape[1])

        def slot(i):
            return o_ref.at[pl.ds(pl.multiple_of(i * rows, rows), rows)]

        last = self.half - 1

        def copies(block, hop, send, recv, device, only):
            result = {}
            for c, columns in enumerate(spans):
                if hop < last or c == only:
                    place = o_ref.at[pl.ds(pl.multiple_of(block * rows, rows), rows), columns]
                    source = w_ref.at[:, columns] if hop == 0 else place
                    result[c] = remote(source, place, send.at[hop, c], recv.at[hop, c], device)
            return result

        self.forward = []
        self.backward = []
        for hop in range(self.half):
            self.forward.append(copies(ring.at(-hop), hop, fs, fr, ring.ahead, 0))
            self.backward.append(copies(ring.at(hop), hop, bs, br, ring.behind, 1))
        self.load = pltpu.make_async_copy(w_ref, bounce, lsem.at[0])
        self.store = pltpu.make_async_copy(bounce, slot(ring.me), lsem.at[1])

    def start(self):
        for c in range(CUTS):
            self.forward[0][c].start()
            self.backward[0][c].start()
        self.load.start()

    def place(self):
        self.load.wait()
        self.store.start()

    def hop(self, hop):
        for c in range(CUTS):
            for way in (self.forward, self.backward):
                way[hop - 1][c].wait_recv()
                if c in way[hop]:
                    way[hop][c].start()

    def finish(self):
        self.forward[-1][0].wait_recv()
        self.backward[-1][1].wait_recv()
        self.store.wait()
        for copies in self.forward + self.backward:
            for copy in copies.values():
                copy.wait_send()


def ring_sum_scratch(rows, wide, half, sources):
    slots = pltpu.VMEM((half, rows, wide), BF)
    hops = pltpu.SemaphoreType.DMA((half, CUTS))
    return (
        [slots] * 4
        + [pltpu.VMEM((rows, wide), BF), pltpu.SemaphoreType.DMA((2 * half + 1, sources))]
        + [hops] * 4
    )


class RingSum:
    def __init__(self, count, sources, scratch):
        self.lf, self.lb, self.rf, self.rb, self.own, lsem, fs, fr, bs, br = scratch
        ring = Ring(count)
        self.ahead, self.behind, self.half = ring.ahead, ring.behind, ring.half
        rows = self.own.shape[0]
        self.spans = column_cuts(self.own.shape[1])

        def sends(source, target, hop, send, recv, device, only):
            return {
                c: remote(
                    source.at[hop, :, span],
                    target.at[hop, :, span],
                    send.at[hop, c],
                    recv.at[hop, c],
                    device,
                )
                for c, span in enumerate(self.spans)
                if hop > 0 or c == only
            }

        def loads(block, target, at):
            span = pl.ds(pl.multiple_of(block * rows, rows), rows)
            base, copies = 0, []
            for i, source in enumerate(sources):
                wide = source.shape[1]
                copies.append(
                    pltpu.make_async_copy(
                        source.at[span], target.at[:, pl.ds(base, wide)], lsem.at[at, i]
                    )
                )
                base += wide
            return copies

        self.forward, self.backward, self.local = [], [], []
        for hop in range(self.half):
            self.local.append(
                loads(ring.at(self.half - hop), self.lf.at[hop], 2 * hop)
                + loads(ring.at(hop - self.half), self.lb.at[hop], 2 * hop + 1)
            )
            self.forward.append(sends(self.lf, self.rf, hop, fs, fr, ring.ahead, 0))
            self.backward.append(sends(self.lb, self.rb, hop, bs, br, ring.behind, 1))
        self.local.append(loads(ring.me, self.own, 2 * self.half))

    def start(self):
        for copies in self.local:
            for copy in copies:
                copy.start()
        for copy in self.local[0]:
            copy.wait()
        self.forward[0][0].start()
        self.backward[0][1].start()
        for copy in self.local[1]:
            copy.wait()
        self.forward[1][1].start()
        self.backward[1][0].start()

    def hop(self, hop):
        if hop > 1:
            for copy in self.local[hop]:
                copy.wait()
        for c, span in enumerate(self.spans):
            for way, mine, came in (
                (self.forward, self.lf, self.rf),
                (self.backward, self.lb, self.rb),
            ):
                if c in way[hop - 1]:
                    way[hop - 1][c].wait_recv()
                    total = mine[hop, :, span].astype(F32) + came[hop - 1, :, span].astype(F32)
                    mine[hop, :, span] = total.astype(BF)
                    way[hop][c].start()

    def finish(self, outs):
        last = self.half - 1
        for copy in self.local[self.half]:
            copy.wait()
        for c in range(CUTS):
            self.forward[last][c].wait_recv()
            self.backward[last][c].wait_recv()
        base = 0
        for out in outs:
            span = slice(base, base + out.shape[1])
            base += out.shape[1]
            out[...] = (
                self.own[:, span].astype(F32)
                + self.rf[last, :, span].astype(F32)
                + self.rb[last, :, span].astype(F32)
            )
        for copies in self.forward + self.backward:
            for copy in copies.values():
                copy.wait_send()


def head_kernel(count, f_ref, g_ref, w_ref, fo_ref, go_ref, wo_ref, *scratch):
    job = Gather(f_ref, fo_ref, scratch[0:4])
    late = Gather(g_ref, go_ref, scratch[4:8])
    ring = RingGather(count, w_ref, wo_ref, scratch[8:])
    greet([job.to_sib, job.to_far, ring.ahead, ring.behind])
    ring.start()
    job.start()
    ring.place()
    ring.hop(1)
    for k in range(CHUNKS):
        job.forward(k)
    late.start()
    for hop in range(2, ring.half):
        ring.hop(hop)
    for k in range(CHUNKS):
        late.forward(k)
    job.finish()
    late.finish()
    ring.finish()


def head_gather(frames, grads, packed, count):
    rows, width = frames.shape
    wide = shape_of((4 * rows, width), BF)
    return pl.pallas_call(
        functools.partial(head_kernel, count),
        out_shape=(wide, wide, shape_of((count * packed.shape[0], packed.shape[1]), BF)),
        in_specs=[ANY] * 3,
        out_specs=(ANY,) * 3,
        scratch_shapes=gather_scratch(rows, width) * 2 + ring_scratch(*packed.shape, count // 2),
        compiler_params=local_params(collective_id=0, has_side_effects=True),
        cost_estimate=BUSY,
        name="head_gather",
    )(frames, grads, packed)


SMALL = 16


def tail_kernel(
    count, buckets, q_ref, k_ref, v_ref, wq_ref, wk_ref, wv_ref,
    a_ref, f_ref, c_ref, g_ref, dg_ref, mark_ref, r_ref, k0_ref, v0_ref, o_ref, s_ref, *scratch,
):
    outs = scratch[:3]
    scratch = scratch[3:]
    total, held = scratch[0:2]
    job = LocalSum(total, scratch[2:9])
    ring = RingSum(count, [a_ref], scratch[9:19])
    sent, got, ss, rs = scratch[19:]
    step = pl.program_id(0)
    me = lax.axis_index("dp")
    mp = lax.axis_index("mp")
    partners = [job.to_sib, job.to_far]
    bit = 1
    while bit < count:
        partners.append({"dp": me + bit * (1 - 2 * ((me // bit) % 2)), "mp": mp})
        bit *= 2

    @pl.when(step == 0)
    def _():
        greet(partners + [ring.ahead, ring.behind])
        ring.start()

    @pl.when(step < 8)
    def _():
        term = (
            dot(q_ref[...], wq_ref[...], NT)
            + dot(k_ref[...], wk_ref[...], NT)
            + dot(v_ref[...], wv_ref[...], NT)
        )
        job.put(step, term.astype(BF))

    job.after_step(step)

    @pl.when(step == 8)
    def _():
        for hop in range(1, ring.half - 1):
            ring.hop(hop)
        job.land()
        unit, spread = norm_rows(f_ref[...].astype(F32))
        back, part = norm_back(total[...], unit, spread, g_ref[0:1, :])
        o_ref[...] = c_ref[...] + back
        edge = dot(k0_ref[...].astype(BF), wk_ref[...], NT) + dot(
            v0_ref[...].astype(BF), wv_ref[...], NT
        )
        unit, spread = norm_rows(r_ref[...])
        edge_back, edge_part = norm_back(edge[0:1, :], unit[0:1, :], spread[0:1, :], g_ref[0:1, :])
        row = lax.broadcasted_iota(jnp.int32, held.shape, 0)
        held[...] = (
            mark_ref[:, 0:1] * edge_back
            + jnp.where(row == buckets, part + edge_part, 0.0)
            + jnp.where(row == buckets + 1, dg_ref[1:2, :], 0.0)
            + jnp.where(row == buckets + 2, dg_ref[2:3, :], 0.0)
        )
        ring.hop(ring.half - 1)
        for i, partner in enumerate(partners):
            sent[i] = held[...]
            copy = remote(sent.at[i], got.at[i], ss.at[i], rs.at[i], partner)
            copy.start()
            copy.wait_recv()
            held[...] += got[i]
            copy.wait_send()
        s_ref[...] = held[...]
        ring.finish(outs)
        job.finish()


def tail_sums(
    count, buckets, grads_qkv, weights, grads, frames, carried, gains, grad_gains, mark, cond_row,
    dk0, dv0,
):
    share, model = frames.shape
    width = grads_qkv[0].shape[1]
    block = 2 * share // 4
    rows = grads.shape[0] // count
    wide = grads.shape[1]
    half = count // 2
    steps = 2 + (count - 1).bit_length()
    once = pl.Buffered(1)

    def full(array):
        return pl.BlockSpec(array.shape, lambda i: (0,) * array.ndim, pipeline_mode=once)

    small = pltpu.VMEM((steps, SMALL, model), F32)
    out_shape = (shape_of((share, model), F32), shape_of((SMALL, model), F32)) + (
        shape_of((rows, wide // 3), F32),
    ) * 3
    whole = [frames, carried, gains, grad_gains, mark, cond_row, dk0, dv0]
    return pl.pallas_call(
        functools.partial(tail_kernel, count, buckets),
        grid=(9,),
        out_shape=out_shape,
        in_specs=[
            pl.BlockSpec((block, width), lambda i: (order_block(jnp.minimum(i, 7)), 0))
            for _ in range(3)
        ]
        + [
            pl.BlockSpec(
                (model, width), functools.partial(lambda at, i: (0, at), at), pipeline_mode=once
            )
            for at in range(3)
        ]
        + [ANY]
        + [full(array) for array in whole],
        out_specs=tuple(pl.BlockSpec(out.shape, lambda i: (0, 0)) for out in out_shape),
        scratch_shapes=[pltpu.VMEM((share, model), F32), pltpu.VMEM((SMALL, model), F32)]
        + sum_scratch(share, model)
        + ring_sum_scratch(rows, wide, half, 1)
        + [small, small, pltpu.SemaphoreType.DMA((steps,)), pltpu.SemaphoreType.DMA((steps,))],
        compiler_params=local_params(collective_id=6, has_side_effects=True),
        cost_estimate=BUSY,
        name="tail_sums",
    )(*grads_qkv, weights, weights, weights, grads, *whole)


def out_kernel(
    count, m_ref, w_ref, p_ref, wp_ref, share_ref, o_ref, kvo_ref, full_ref, mine, *scratch
):
    side = Gather(mine, kvo_ref, scratch[:4], here=True)
    job = LocalSum(o_ref, scratch[4:11])
    ring = RingGather(count, share_ref, full_ref, scratch[11:])
    step = pl.program_id(0)

    @pl.when(step == 0)
    def _():
        greet([job.to_sib, job.to_far, ring.ahead, ring.behind])
        ring.start()

    job.put(step, dot(m_ref[...], w_ref[...], NT).astype(BF))
    job.after_step(step)

    @pl.when(step == 1)
    def _():
        mine[...] = dot(p_ref[...], wp_ref[...], NN).astype(BF)
        side.start()
        ring.place()

    @pl.when(step == 7)
    def _():
        for hop in range(1, ring.half):
            ring.hop(hop)
        for k in range(CHUNKS):
            side.forward(k)
        job.land()
        side.finish()
        job.finish()
        ring.finish()


def out_project(mixed, weights, column, prompts, prompt_weights, weight_share, count):
    length, width = mixed.shape
    model = weights.shape[0]
    rows = length // 8
    share = length // 4
    short = prompts.shape[0]
    once = pl.Buffered(1)
    return pl.pallas_call(
        functools.partial(out_kernel, count),
        grid=(8,),
        out_shape=(
            shape_of((share, model), F32),
            shape_of((4 * short, width), BF),
            shape_of((count * weight_share.shape[0], weight_share.shape[1]), BF),
        ),
        in_specs=[
            pl.BlockSpec((rows, width), lambda i: (order_block(i), 0)),
            pl.BlockSpec((model, width), lambda i: (0, column), pipeline_mode=once),
            pl.BlockSpec(prompts.shape, lambda i: (0, 0), pipeline_mode=once),
            pl.BlockSpec((model, width), lambda i: (0, 0), pipeline_mode=once),
            ANY,
        ],
        out_specs=(pl.BlockSpec((share, model), lambda i: (0, 0)), ANY, ANY),
        scratch_shapes=[pltpu.VMEM((short, width), BF)]
        + gather_scratch(16, 128)
        + sum_scratch(share, model)
        + ring_scratch(*weight_share.shape, count // 2),
        compiler_params=local_params(collective_id=1, has_side_effects=True),
        cost_estimate=BUSY,
        name="out_project",
    )(mixed, weights, prompts, prompt_weights, weight_share)


def glu_back_kernel(parts, count, d0_ref, d1_ref, h0_ref, h1_ref, *refs):
    weights = refs[:count]
    o_ref, t0_ref, t1_ref = refs[count : count + 3]
    job = LocalSum(o_ref, refs[count + 3 :])
    step = pl.program_id(0)

    def gate_up():
        term = None
        for left, group in zip((d0_ref, d1_ref), parts):
            base = 0
            for index, low, size in group:
                w_ref = weights[index]
                width = w_ref.shape[1] // 3
                if size == width:
                    part = dot(left[:, base : base + 2 * size], w_ref[:, : 2 * size], NT)
                else:
                    high = low + size
                    part = dot(left[:, base : base + size], w_ref[:, low:high], NT) + dot(
                        left[:, base + size : base + 2 * size],
                        w_ref[:, width + low : width + high],
                        NT,
                    )
                term = part if term is None else term + part
                base += 2 * size
        return term.astype(BF)

    def down():
        term = None
        for left, group in zip((h0_ref, h1_ref), parts):
            base = 0
            for index, low, size in group:
                w_ref = weights[index]
                start = 2 * w_ref.shape[1] // 3 + low
                part = dot(left[:, base : base + size], w_ref[:, start : start + size], NT)
                term = part if term is None else term + part
                base += size
        return term.astype(BF)

    @pl.when(step == 0)
    def _():
        greet([job.to_sib, job.to_far])

    @pl.when(step < 8)
    def _():
        job.put(step, gate_up())

    job.after_step(step)

    @pl.when(step >= 8)
    def _():
        term = down()
        half = t0_ref.shape[1]
        t0_ref[...] = term[:, :half]
        t1_ref[...] = term[:, half:]

    @pl.when(step == 15)
    def _():
        job.land()
        job.finish()


def glu_back(dgus, hiddens, weights, parts):
    length = dgus[0].shape[0]
    model = weights[0].shape[0]
    rows = length // 8
    share = length // 4
    once = pl.Buffered(1)
    early = lambda i: (order_block(jnp.minimum(i, 7)), 0)
    late = lambda i: (jnp.maximum(i - 8, 0), 0)
    in_specs = [pl.BlockSpec((rows, d.shape[1]), early) for d in dgus]
    in_specs += [pl.BlockSpec((rows, h.shape[1]), late) for h in hiddens]
    for weight in weights:
        in_specs.append(pl.BlockSpec(weight.shape, lambda i: (0, 0), pipeline_mode=once))
    half = pl.BlockSpec((rows, model // 2), late)
    return pl.pallas_call(
        functools.partial(glu_back_kernel, parts, len(weights)),
        grid=(16,),
        out_shape=(
            shape_of((share, model), F32),
            shape_of((length, model // 2), BF),
            shape_of((length, model // 2), BF),
        ),
        in_specs=in_specs,
        out_specs=(
            pl.BlockSpec((share, model), lambda i: (0, 0)),
            half,
            half,
        ),
        scratch_shapes=sum_scratch(share, model),
        compiler_params=local_params(collective_id=3, has_side_effects=True),
        cost_estimate=BUSY,
        name="glu_back",
    )(*dgus, *hiddens, *weights)


def mid_kernel(
    count, c_ref, t_ref, n_ref, cb_ref, q_ref, cm_ref, w_ref, m_ref, p_ref, y_ref,
    x_ref, g_ref, dw_ref, yo_ref, s_ref, slots, total, ssem, rsem, *scratch,
):
    small = Scatter(t_ref, s_ref, scratch[:8])
    ring = RingSum(count, [y_ref], scratch[8:])
    me, sib, far, diag = mp_peers()
    dp = lax.axis_index("dp")
    to_sib = {"dp": dp, "mp": sib}
    to_far = {"dp": dp, "mp": far}
    step = pl.program_id(0)
    rows = c_ref.shape[0]
    part = rows // CHUNKS
    spans = [pl.ds(k * part, part) for k in range(CHUNKS)]
    beside = remote(c_ref, slots.at[0], ssem.at[0], rsem.at[0], to_sib)
    across = [
        remote(c_ref.at[span], slots.at[1, span], ssem.at[1 + k], rsem.at[1 + k], to_far)
        for k, span in enumerate(spans)
    ]
    onward = [
        remote(
            slots.at[1, span],
            slots.at[2, span],
            ssem.at[1 + CHUNKS + k],
            rsem.at[1 + CHUNKS + k],
            to_sib,
        )
        for k, span in enumerate(spans)
    ]

    @pl.when(step == 0)
    def _():
        greet([to_sib, to_far, ring.ahead, ring.behind])
        for copy in across:
            copy.start()
        small.start()
        beside.start()
        ring.start()

    @pl.when(step == 6)
    def _():
        for hop in range(1, ring.half // 2):
            ring.hop(hop)

    @pl.when(step == 1)
    def _():
        small.fold()
        small.local()

    @pl.when(step < 8)
    def _():
        width = q_ref.shape[1]
        x_ref[:, :width] = dot(n_ref[...], q_ref[...], TN).astype(BF)
        x_ref[:, width:] = dot(cb_ref[...], cm_ref[...], TN).astype(BF)

    def use(grads):
        g_ref[...] = dot(grads, w_ref[...], NN).astype(BF)
        return dot(grads, m_ref[...], TN)

    @pl.when(step == 8)
    def _():
        total[...] = use(c_ref[...])

    @pl.when(step == 9)
    def _():
        beside.wait_recv()
        total[...] += use(slots[0])

    @pl.when(step == 10)
    def _():
        ring.hop(ring.half // 2)
        small.land()
        for k in range(CHUNKS):
            across[k].wait_recv()
            onward[k].start()
        for hop in range(ring.half // 2 + 1, ring.half):
            ring.hop(hop)
        total[...] += use(slots[1])

    @pl.when(step == 11)
    def _():
        for copy in onward:
            copy.wait_recv()
        width = m_ref.shape[1]
        dw_ref[:, :width] = (total[...] + use(slots[2])).astype(BF)
        dw_ref[:, width:] = dot(p_ref[...], s_ref[...].astype(BF), TN).astype(BF)
        small.finish()
        ring.finish([yo_ref])
        beside.wait_send()
        for copy in across + onward:
            copy.wait_send()


def mid_gather(
    carried, term, normed, cross_back, grad_cq, cross_mixed, weights, column, mixed, prompts,
    more, groups, count,
):
    share, model = carried.shape
    own = more.shape[0] // count
    length, width = mixed.shape
    short, narrow = term.shape[0] // 4, term.shape[1]
    tile = 2 * model // 4
    once = pl.Buffered(1)
    fixed = pl.BlockSpec((share, model), lambda i: (0, 0), pipeline_mode=once)
    left = pl.BlockSpec((share, tile), lambda i: (0, jnp.minimum(i, 7) % 2))
    right = pl.BlockSpec((share, width), lambda i: (0, jnp.minimum(i, 7) // 2))

    def turn(i):
        return (arrival_quarter(jnp.maximum(i - 8, 0)), 0)

    return pl.pallas_call(
        functools.partial(mid_kernel, count),
        grid=(12,),
        in_specs=[
            fixed,
            ANY,
            left,
            left,
            right,
            right,
            pl.BlockSpec((model, width), lambda i: (0, column), pipeline_mode=once),
            pl.BlockSpec((share, width), turn),
            pl.BlockSpec(prompts.shape, lambda i: (0, 0), pipeline_mode=once),
            ANY,
        ],
        out_specs=(
            pl.BlockSpec((tile, 2 * width), lambda i: (jnp.minimum(i, 7), 0)),
            pl.BlockSpec((share, width), turn),
            pl.BlockSpec((model, 2 * width), lambda i: (0, 0)),
            pl.BlockSpec((own, more.shape[1]), lambda i: (0, 0)),
        ),
        out_shape=(
            shape_of((groups * model, 2 * width), BF),
            shape_of((length, width), BF),
            shape_of((model, 2 * width), BF),
            shape_of((own, more.shape[1]), F32),
        ),
        scratch_shapes=[
            pltpu.VMEM((short, narrow), F32),
            pltpu.VMEM((3, share, model), BF),
            pltpu.VMEM((model, width), F32),
            pltpu.SemaphoreType.DMA((1 + 2 * CHUNKS,)),
            pltpu.SemaphoreType.DMA((1 + 2 * CHUNKS,)),
        ]
        + scatter_scratch(short, narrow)
        + ring_sum_scratch(own, more.shape[1], count // 2, 1),
        compiler_params=local_params(collective_id=4, has_side_effects=True),
        cost_estimate=BUSY,
        name="mid_gather",
    )(carried, term, normed, cross_back, grad_cq, cross_mixed, weights, mixed, prompts, more)


def qkv_kernel(
    scale, x_ref, s_ref, r_ref, hot_ref, w_ref, c_ref, u_ref, l_ref,
    n_ref, q_ref, k_ref, v_ref, g_ref, sw_ref, nc_ref, k0_ref, v0_ref,
):
    width = q_ref.shape[1]

    @pl.when(pl.program_id(0) == 0)
    def _():
        side = s_ref[...]
        dims = (8, side.shape[1])
        pick = lax.broadcasted_iota(jnp.int32, dims, 0) == lanes(dims)
        g_ref[...] = dot(jnp.where(pick, 1.0, 0.0).astype(BF), side, NT)
        totals = dot(jnp.ones((8, side.shape[0]), BF), side, NN)
        sw_ref[...] = jnp.broadcast_to(
            scale / jnp.sum(totals * hot_ref[...], axis=1, keepdims=True), sw_ref.shape
        )
        unit, _ = norm_rows(r_ref[...])
        normed = (unit * g_ref[0:1, :]).astype(BF)
        nc_ref[...] = normed
        out = dot(normed, w_ref[:, width:], NN).astype(BF)
        k0_ref[...] = out[:, :width]
        v0_ref[...] = out[:, width:]

    unit, _ = norm_rows(x_ref[...].astype(F32))
    normed = (unit * g_ref[0:1, :]).astype(BF)
    n_ref[...] = normed
    out = dot(normed, w_ref[...], NN)
    cosine, upper, lower = c_ref[...], u_ref[...], l_ref[...]
    for pair in range(width // 128):
        span = slice(128 * pair, 128 * pair + 128)
        q_ref[:, span] = (rope(out[:, span], cosine, upper, lower) * (LOG2E / 8.0)).astype(BF)
        keys = out[:, width + 128 * pair : width + 128 * pair + 128]
        k_ref[:, span] = rope(keys, cosine, upper, lower).astype(BF)
    v_ref[...] = out[:, 2 * width : 3 * width].astype(BF)


def qkv_project(frames, cond_row, hot, weights, tables, width, scale):
    length, model = frames.shape
    rows = 256
    block = pl.BlockSpec((rows, model), lambda i: (i, 0))
    table = pl.BlockSpec((rows, 128), lambda i: (i, 0))
    head = pl.BlockSpec((rows, width), lambda i: (i, 0))
    fixed = lambda i: (0, 0)
    extra = [
        shape_of((8, model), F32),
        shape_of((8, 128), F32),
        shape_of((16, model), BF),
        shape_of((16, width), BF),
        shape_of((16, width), BF),
    ]
    return pl.pallas_call(
        functools.partial(qkv_kernel, scale),
        grid=(length // rows,),
        in_specs=[
            block,
            pl.BlockSpec((model, 128), lambda i: (0, 3 * width // 128)),
            pl.BlockSpec(cond_row.shape, fixed),
            pl.BlockSpec(hot.shape, fixed),
            pl.BlockSpec((model, 3 * width), fixed),
            table,
            table,
            table,
        ],
        out_specs=[block, head, head, head] + [pl.BlockSpec(e.shape, fixed) for e in extra],
        out_shape=[shape_of((length, model), BF)] + [shape_of((length, width), BF)] * 3 + extra,
        compiler_params=local_params(),
        cost_estimate=cost(6 * length * model * width, 8 * length * model),
        name="qkv_project",
    )(frames, weights, cond_row, hot, weights, *tables)


def attend_kernel(
    bk, first, count, q_ref, k_ref, v_ref, k0_ref, v0_ref, x_ref, w_ref, y_ref,
    o_ref, aug_ref, xo_ref, wo_ref, yo_ref, vaug, *scratch,
):
    length = k_ref.shape[0]
    bq = q_ref.shape[0]
    step = pl.program_id(0) * pl.num_programs(1) + pl.program_id(1)
    wide = xo_ref.shape[1]
    job = Gather(x_ref, xo_ref, scratch[:4], pl.ds(first, wide))
    ring = RingGather(count, w_ref, wo_ref, scratch[4:10])
    wide_ring = RingGather(count, y_ref, yo_ref, scratch[10:])
    last = pl.num_programs(0) * pl.num_programs(1) - 1

    @pl.when(step == 0)
    def _():
        greet([job.to_sib, job.to_far, ring.ahead, ring.behind])
        ring.start()
        wide_ring.start()
        job.start()
        ring.place()
        wide_ring.place()

    for hop in range(1, ring.half):

        @pl.when(step == min(3 * hop, 11))
        def _(hop=hop):
            ring.hop(hop)

        @pl.when(step == min(1 + 3 * hop, 11))
        def _(hop=hop):
            wide_ring.hop(hop)

    @pl.when(pl.program_id(1) == 0)
    def _():
        vaug[:, :128] = v_ref[...]
        vaug[:, 128:] = jnp.ones((length, 128), BF)

    queries = q_ref[...]
    key0 = k0_ref[0:1, :].astype(F32)
    value0 = v0_ref[0:1, :].astype(F32)
    outs = []
    logs = []
    for head in range(2):
        masked = half_mask(queries, head)
        peak = jnp.sum(masked.astype(F32) * key0, axis=1, keepdims=True)
        total = jnp.concatenate(
            [jnp.broadcast_to(value0, (bq, 128)), jnp.ones((bq, 128), F32)], 1
        )
        for block in range(length // bk):
            span = slice(block * bk, (block + 1) * bk)
            scores = dot(masked, k_ref[span, :], NT)
            higher = jnp.maximum(peak, jnp.max(scores, axis=1, keepdims=True))
            exponent = jnp.exp2(scores - higher).astype(BF)
            total = total * jnp.exp2(peak - higher) + dot(exponent, vaug[span, :], NN)
            peak = higher
        weight = total[:, 128:129]
        outs.append(total[:, :128] * (1.0 / weight))
        logs.append(-(peak + jnp.log2(weight)))
    lane = lanes((bq, 128))
    o_ref[...] = jnp.where(lane < HD, outs[0], outs[1]).astype(BF)
    aug_ref[...] = (pieces(logs[0], (bq, 128), 0) + pieces(logs[1], (bq, 128), HD)).astype(BF)

    @pl.when(step == last)
    def _():
        for k in range(CHUNKS):
            job.forward(k)
        job.finish()
        ring.finish()
        wide_ring.finish()


def attend(
    queries, keys, values, key0, value0, packed, first, share, more, count, bq=512, bk=1024
):
    length, width = queries.shape
    row = pl.BlockSpec((bq, 128), lambda p, i: (i, p))
    full = pl.BlockSpec((length, 128), lambda p, i: (0, p))
    zero = pl.BlockSpec((16, 128), lambda p, i: (0, p))
    return pl.pallas_call(
        functools.partial(attend_kernel, bk, first, count),
        grid=(width // 128, length // bq),
        in_specs=[row, full, full, zero, zero, ANY, ANY, ANY],
        out_specs=[row, row, ANY, ANY, ANY],
        out_shape=[shape_of((length, width), BF)] * 2
        + [
            shape_of((4 * packed.shape[0], 2 * width), BF),
            shape_of((count * share.shape[0], share.shape[1]), BF),
            shape_of((count * more.shape[0], more.shape[1]), BF),
        ],
        scratch_shapes=[pltpu.VMEM((length, 256), BF)]
        + gather_scratch(packed.shape[0], 2 * width)
        + ring_scratch(*share.shape, count // 2)
        + ring_scratch(*more.shape, count // 2),
        compiler_params=local_params(collective_id=7, has_side_effects=True),
        cost_estimate=cost(16 * length * length * width, 10 * length * width),
        name="attend",
    )(queries, keys, values, key0, value0, packed, share, more)


def attend_back_kernel(
    bk, count, q_ref, aug_ref, o_ref, do_ref, k_ref, v_ref, k0_ref, v0_ref,
    cq_ref, uq_ref, lq_ref, ck_ref, uk_ref, lk_ref,
    x_ref, y_ref, t_ref, ac_ref, dq_ref, dk_ref, dv_ref, dk0_ref, dv0_ref, xh_ref,
    yo_ref, zo_ref,
    to_ref, xo0_ref, xo1_ref, kaug, vaug, kt, dka, dva, xs, xsem, *scratch,
):
    length = k_ref.shape[0]
    bq = q_ref.shape[0]
    step = pl.program_id(1)
    turn = pl.program_id(0) * pl.num_programs(1) + step
    job = Scatter(x_ref, xs, scratch[:8])
    late = Scatter(t_ref, to_ref, scratch[8:16])
    ring = RingSum(count, [y_ref], scratch[16:26])
    next_ring = RingSum(count, [xh_ref], scratch[26:])
    keep = pltpu.make_async_copy(xs, xh_ref, xsem)

    @pl.when(turn == 0)
    def _():
        greet([job.to_sib, job.to_far, ring.ahead, ring.behind])
        job.start()
        ring.start()

    @pl.when(turn == 1)
    def _():
        job.fold()
        job.local()
        late.start()

    for hop in range(1, ring.half):

        @pl.when(turn == min(1 + 2 * hop, 7))
        def _(hop=hop):
            ring.hop(hop)

        @pl.when(turn == min(8 + hop, 11))
        def _(hop=hop):
            next_ring.hop(hop)

    @pl.when(turn == 8)
    def _():
        job.land()
        keep.start()
        late.fold()
        late.local()
        keep.wait()
        next_ring.start()
        job.finish()
        ring.finish([yo_ref, zo_ref])

    @pl.when(step == 0)
    def _():
        lane = lanes((length, 128))
        ones = jnp.where((lane % HD) < 3, 1.0, 0.0).astype(BF)
        kaug[:, :128] = k_ref[...]
        kaug[:, 128:] = ones
        vaug[:, :128] = v_ref[...]
        vaug[:, 128:] = ones
        kt[...] = k_ref[...].astype(F32).T.astype(BF)
        dka[...] = jnp.zeros_like(dka)
        dva[...] = jnp.zeros_like(dva)
        dk0_ref[...] = jnp.zeros_like(dk0_ref)
        dv0_ref[...] = jnp.zeros_like(dv0_ref)

    queries = q_ref[...]
    grads = do_ref[...]
    aug = aug_ref[...]
    product = grads.astype(F32) * o_ref[...].astype(F32)
    lane = lanes((bq, 128))
    ones0 = jnp.where((lanes((16, 128)) % HD) < 3, 1.0, 0.0).astype(BF)
    key0 = jnp.concatenate([k0_ref[...], ones0], 1)
    value0 = jnp.concatenate([v0_ref[...], ones0], 1)
    row0 = lax.broadcasted_iota(jnp.int32, (16, bq), 0) == 0
    qa, da, qm, dm, dq = [], [], [], [], []
    for head in range(2):
        qm.append(half_mask(queries, head))
        dm.append(half_mask(grads, head))
        mine = (lane < HD) if head == 0 else (lane >= HD)
        inner = jnp.sum(jnp.where(mine, product, 0.0), axis=1, keepdims=True)
        qa.append(jnp.concatenate([qm[head], half_mask(aug, head)], 1))
        da.append(
            jnp.concatenate([dm[head], pieces(-inner, (bq, 128), HD * head).astype(BF)], 1)
        )
        prob0 = jnp.where(row0, jnp.exp2(dot(key0, qa[head], NT)), 0.0)
        ds0 = (prob0 * dot(value0, da[head], NT)).astype(BF)
        dv0_ref[...] += dot(prob0.astype(BF), dm[head], NN)
        dk0_ref[...] += dot(ds0, qm[head], NN)
        dq.append(dot(k0_ref[:, HD * head : HD * head + HD], ds0, TN))
    for block in range(length // bk):
        span = slice(block * bk, (block + 1) * bk)
        for head in range(2):
            probs = jnp.exp2(dot(kaug[span, :], qa[head], NT))
            ds = (probs * dot(vaug[span, :], da[head], NT)).astype(BF)
            dva[span, :] += dot(probs.astype(BF), dm[head], NN)
            dka[span, :] += dot(ds, qm[head], NN)
            dq[head] = dq[head] + dot(kt[HD * head : HD * head + HD, span], ds, NN)
    grad_q = jnp.concatenate(dq, 0).T * 0.125
    dq_ref[...] = rope(grad_q, cq_ref[...], -uq_ref[...], -lq_ref[...]).astype(BF)

    @pl.when(turn == pl.num_programs(0) * pl.num_programs(1) - 1)
    def _():
        late.land(ac_ref)
        late.finish()
        next_ring.finish([xo0_ref, xo1_ref])

    @pl.when(step == pl.num_programs(1) - 1)
    def _():
        grad_k = dka[...] * (1.0 / LOG2E)
        dk_ref[...] = rope(grad_k, ck_ref[...], -uk_ref[...], -lk_ref[...]).astype(BF)
        dv_ref[...] = dva[...].astype(BF)
        dk0_ref[...] = dk0_ref[...] * (1.0 / LOG2E)


def attend_back(
    queries, aug, mixed, grads, keys, values, key0, value0, tables, extra, more, term, after_cross, count,
    bq=512, bk=512,
):
    length, width = queries.shape
    row = pl.BlockSpec((bq, 128), lambda p, i: (i, p))
    full = pl.BlockSpec((length, 128), lambda p, i: (0, p))
    zero = pl.BlockSpec((16, 128), lambda p, i: (0, p))
    tq = pl.BlockSpec((bq, 128), lambda p, i: (i, 0))
    tk = pl.BlockSpec((length, 128), lambda p, i: (0, 0), pipeline_mode=pl.Buffered(1))
    own = more.shape[0] // count
    owned = pl.BlockSpec((own, more.shape[1] // 2), lambda p, i: (0, 0))
    wide, narrow = extra.shape[0] // 4, extra.shape[1]
    half_shape = (after_cross.shape[0], term.shape[1])
    share_spec = pl.BlockSpec(half_shape, lambda p, i: (0, 0))
    part = pl.BlockSpec((own, narrow // 2), lambda p, i: (0, 0))
    big = shape_of((length, width), BF)
    small = shape_of((16, width), F32)
    return pl.pallas_call(
        functools.partial(attend_back_kernel, bk, count),
        grid=(width // 128, length // bq),
        in_specs=[row, row, row, row, full, full, zero, zero, tq, tq, tq, tk, tk, tk, ANY, ANY, ANY,
            pl.BlockSpec(half_shape, lambda p, i: (0, 1), pipeline_mode=pl.Buffered(1)),
        ],
        out_specs=[row, full, full, zero, zero, ANY, owned, owned, share_spec, part, part],
        out_shape=[big, big, big, small, small]
        + [
            shape_of((wide, narrow), BF),
            shape_of((own, more.shape[1] // 2), F32),
            shape_of((own, more.shape[1] // 2), F32),
            shape_of(half_shape, BF),
            shape_of((own, narrow // 2), F32),
            shape_of((own, narrow // 2), F32),
        ],
        scratch_shapes=[pltpu.VMEM((length, 256), BF)] * 2
        + [pltpu.VMEM((128, length), BF)]
        + [pltpu.VMEM((length, 128), F32)] * 2
        + [
            pltpu.VMEM((wide, narrow), BF),
            pltpu.SemaphoreType.DMA(()),
        ]
        + scatter_scratch(wide, narrow)
        + scatter_scratch(*half_shape)
        + ring_sum_scratch(own, more.shape[1], count // 2, 1)
        + ring_sum_scratch(own, narrow, count // 2, 1),
        compiler_params=local_params(collective_id=8, has_side_effects=True),
        cost_estimate=cost(40 * length * length * width, 20 * length * width),
        name="attend_back",
    )(queries, aug, mixed, grads, keys, values, key0, value0, *tables, *tables, extra, more, term, after_cross)


def softmax_keys(scores, length):
    key = lax.broadcasted_iota(jnp.int32, scores.shape, 0)
    masked = jnp.where(key < length, scores, -1e9)
    exponent = jnp.exp2(masked - jnp.max(masked, axis=0, keepdims=True))
    return exponent * (1.0 / jnp.sum(exponent, axis=0, keepdims=True))


def two_heads(values):
    return jnp.concatenate([half_mask(values, 0), half_mask(values, 1)], 0)


def one_row(values):
    rows = values.shape[0] // 2
    lane = lanes((rows, 128))
    return jnp.where(lane < HD, values[:rows], values[rows:])


def cross_kernel(
    count, len_ref, f_ref, s_ref, g_ref, wq_ref, wo_ref, kv_ref, share_ref,
    as_ref, n2_ref, q_ref, m_ref, ac_ref, n3_ref, full_ref, mine, *scratch,
):
    job = Gather(mine, n3_ref, scratch[:4], here=True)
    ring = RingGather(count, share_ref, full_ref, scratch[4:])
    step = pl.program_id(0)
    groups, model, width = wq_ref.shape
    keys = kv_ref.shape[1] // 2

    @pl.when(step == 0)
    def _():
        greet([job.to_sib, job.to_far, ring.ahead, ring.behind])
        ring.start()

    after_self = f_ref[...].astype(F32) + s_ref[...]
    as_ref[...] = after_self
    unit, _ = norm_rows(after_self)
    normed = (unit * g_ref[1:2, :]).astype(BF)
    n2_ref[...] = normed
    rows = normed.shape[0]
    total = after_self
    for group in range(groups):
        queries = (dot(normed, wq_ref[group], NN) * (LOG2E / 8.0)).astype(BF)
        base = group * width
        q_ref[:, base : base + width] = queries
        for pair in range(width // 128):
            span = slice(128 * pair, 128 * pair + 128)
            scores = dot(kv_ref[group, :keys, span], two_heads(queries[:, span]), NT)
            probs = softmax_keys(scores, len_ref[0])
            m_ref[:, base + 128 * pair : base + 128 * pair + 128] = one_row(
                dot(probs.astype(BF), kv_ref[group, keys:, span], TN)
            ).astype(BF)
        total = total + dot(m_ref[:, base : base + width], wo_ref[group], NT)
    ac_ref[...] = total
    unit, _ = norm_rows(total)
    mine[pl.ds(pl.multiple_of(step * rows, rows), rows), :] = (unit * g_ref[2:3, :]).astype(BF)

    for turn in range(2):

        @pl.when(step == turn)
        def _(turn=turn):
            half = CHUNKS // 2
            for k in range(turn * half, turn * half + half):
                job.across[k].start()
                job.beside[k].start()
            if turn == 0:
                ring.place()
                ring.hop(1)

    @pl.when(step == 1)
    def _():
        job.store.start()
        for hop in range(2, ring.half):
            ring.hop(hop)
        for k in range(CHUNKS):
            job.forward(k)
        job.finish()
        ring.finish()


def cross_forward(plen, frames, summed, gains, weights, prompt_kv, share, count):
    own, model = frames.shape
    groups, _, both = weights.shape
    width = both // 2
    rows = own // 2
    block = pl.BlockSpec((rows, model), lambda i: (i, 0))
    gain = pl.BlockSpec(gains.shape, lambda i: (0, 0))
    once = pl.Buffered(1)
    return pl.pallas_call(
        functools.partial(cross_kernel, count),
        grid=(2,),
        in_specs=[
            pl.BlockSpec(memory_space=pltpu.SMEM),
            block,
            block,
            gain,
            pl.BlockSpec((groups, model, width), lambda i: (0, 0, 0), pipeline_mode=once),
            pl.BlockSpec((groups, model, width), lambda i: (0, 0, 1), pipeline_mode=once),
            pl.BlockSpec(prompt_kv.shape, lambda i: (0, 0, 0)),
            ANY,
        ],
        out_specs=[block] * 5 + [ANY, ANY],
        out_shape=[
            shape_of((own, model), F32),
            shape_of((own, model), BF),
            shape_of((own, model), BF),
            shape_of((own, model), BF),
            shape_of((own, model), F32),
            shape_of((4 * own, model), BF),
            shape_of((count * share.shape[0], share.shape[1]), BF),
        ],
        scratch_shapes=[pltpu.VMEM((own, model), BF)]
        + gather_scratch(16, 128)
        + ring_scratch(*share.shape, count // 2),
        compiler_params=local_params(collective_id=2, has_side_effects=True),
        cost_estimate=BUSY,
        name="cross_forward",
    )(plen, frames, summed, gains, weights, weights, prompt_kv, share)


def cross_back_kernel(
    len_ref, w_ref, go_ref, e_ref, ac_ref, as_ref, g_ref, q_ref, wq_ref, wo_ref, kv_ref, t_ref,
    cb_ref, dq_ref, c3_ref, c3b_ref, dkv_ref, dg_ref, bo_ref, dkv, hold, *scratch,
):
    groups, model, width = wq_ref.shape
    keys = kv_ref.shape[1] // 2
    job = Scatter(t_ref, bo_ref, scratch)
    step = pl.program_id(0)

    @pl.when(step == 0)
    def _():
        greet([job.to_sib, job.to_far])
        job.start()

    @pl.when(pl.program_id(0) == 0)
    def _():
        dkv[...] = jnp.zeros_like(dkv)
        dg_ref[...] = jnp.zeros_like(dg_ref)

    unit, spread = norm_rows(ac_ref[...])
    back, part = norm_back(e_ref[...], unit, spread, g_ref[2:3, :])
    dg_ref[2:3, :] += part
    carried = go_ref[...].astype(F32) * w_ref[0:1, 0:1] + back
    cross_back = carried.astype(BF)
    cb_ref[...] = cross_back
    rows = cross_back.shape[0]
    total = jnp.zeros((rows, model), F32)
    spot = pl.ds(pl.multiple_of(pl.program_id(0) * rows, rows), rows)
    hold[spot, :] = ac_ref[:, : hold.shape[1]]

    @pl.when(step == 0)
    def _():
        job.fold()
        job.local()

    for group in range(groups):
        grads = dot(cross_back, wo_ref[group], NN).astype(BF)
        base = group * width
        for pair in range(width // 128):
            span = slice(128 * pair, 128 * pair + 128)
            wide = slice(base + 128 * pair, base + 128 * pair + 128)
            queries = two_heads(q_ref[:, wide])
            masked = two_heads(grads[:, span])
            probs = softmax_keys(dot(kv_ref[group, :keys, span], queries, NT), len_ref[0])
            dprobs = dot(kv_ref[group, keys:, span], masked, NT)
            inner = jnp.sum(dprobs * probs, axis=0, keepdims=True)
            ds = (probs * (dprobs - inner)).astype(BF)
            dkv[group, :keys, span] += dot(ds, queries, NN) * (1.0 / LOG2E)
            dkv[group, keys:, span] += dot(probs.astype(BF), masked, NN)
            grad_q = one_row(dot(ds, kv_ref[group, :keys, span], TN))
            dq_ref[:, wide] = (grad_q * 0.125).astype(BF)
        total = total + dot(dq_ref[:, base : base + width], wq_ref[group], NT)
    unit, spread = norm_rows(as_ref[...])
    back, part = norm_back(total, unit, spread, g_ref[1:2, :])
    dg_ref[1:2, :] += part
    carried = carried + back
    c3_ref[...] = carried
    c3b_ref[...] = carried.astype(BF)

    @pl.when(pl.program_id(0) == pl.num_programs(0) - 1)
    def _():
        dkv_ref[...] = dkv[...].astype(BF)
        job.land(hold)
        job.finish()


def cross_backward(plen, weight, grad_out, summed, after_cross, after_self, gains, queries,
                   weights, prompt_kv, term):
    share, model = grad_out.shape
    groups, _, both = weights.shape
    width = both // 2
    rows = 256
    block = pl.BlockSpec((rows, model), lambda i: (i, 0))
    gain = pl.BlockSpec(gains.shape, lambda i: (0, 0))
    once = pl.Buffered(1)
    return pl.pallas_call(
        cross_back_kernel,
        grid=(share // rows,),
        in_specs=[
            pl.BlockSpec(memory_space=pltpu.SMEM),
            pl.BlockSpec(weight.shape, lambda i: (0, 0)),
            block,
            block,
            block,
            block,
            gain,
            block,
            pl.BlockSpec((groups, model, width), lambda i: (0, 0, 0), pipeline_mode=once),
            pl.BlockSpec((groups, model, width), lambda i: (0, 0, 1), pipeline_mode=once),
            pl.BlockSpec(prompt_kv.shape, lambda i: (0, 0, 0)),
            ANY,
        ],
        out_specs=[block] * 4
        + [pl.BlockSpec(prompt_kv.shape, lambda i: (0, 0, 0)), gain]
        + [pl.BlockSpec((share, term.shape[1]), lambda i: (0, 0))],
        out_shape=[
            shape_of((share, model), BF),
            shape_of((share, model), BF),
            shape_of((share, model), F32),
            shape_of((share, model), BF),
            shape_of(prompt_kv.shape, BF),
            shape_of(gains.shape, F32),
            shape_of((share, term.shape[1]), BF),
        ],
        scratch_shapes=[
            pltpu.VMEM(prompt_kv.shape, F32),
            pltpu.VMEM((share, term.shape[1]), F32),
        ]
        + scatter_scratch(share, term.shape[1]),
        compiler_params=local_params(collective_id=9, has_side_effects=True),
        cost_estimate=cost(4 * share * model * model, 4 * model * model + 24 * share * model),
        name="cross_backward",
    )(plen, weight, grad_out, summed, after_cross, after_self, gains, queries, weights, weights,
      prompt_kv, term)


def glu_kernel(scaled, parts, count, *refs):
    refs = list(refs)
    s_ref = None if scaled else refs.pop(0)
    n_ref, c_ref = refs[:2]
    weights, outs = refs[2 : 2 + count], refs[2 + count :]
    cot = c_ref[...]
    if not scaled:
        cot = (cot.astype(F32) * s_ref[0:1, 0:1]).astype(BF)
        outs[2][...] = cot
    h_ref, d_ref = outs[:2]
    normed = n_ref[...]
    piece = 256
    at = 0
    for index, low, size in parts:
        w_ref = weights[index]
        width = w_ref.shape[1] // 3
        for base in range(0, size, piece):
            spot = low + base
            gate = dot(normed, w_ref[:, spot : spot + piece], NN)
            up = dot(normed, w_ref[:, width + spot : width + spot + piece], NN)
            grads = dot(cot, w_ref[:, 2 * width + spot : 2 * width + spot + piece], NN)
            sig = 1.0 / (1.0 + jnp.exp(-gate))
            silu = gate * sig
            h_ref[:, at + base : at + base + piece] = (silu * up).astype(BF)
            grad_gate = grads * up * sig * (1.0 + gate * (1.0 - sig))
            spot = 2 * at + base
            d_ref[:, spot : spot + piece] = grad_gate.astype(BF)
            d_ref[:, size + spot : size + spot + piece] = (grads * silu).astype(BF)
        at += size


def glu_block(normed, cot, weights, parts, scale=None):
    length, model = normed.shape
    width = sum(size for _, _, size in parts)
    rows = 512
    block = pl.BlockSpec((rows, model), lambda i: (i, 0))
    first = scale is not None
    return pl.pallas_call(
        functools.partial(glu_kernel, not first, parts, len(weights)),
        grid=(length // rows,),
        in_specs=[pl.BlockSpec((8, 128), lambda i: (0, 0))] * first
        + [block, block]
        + [
            pl.BlockSpec(weight.shape, lambda i: (0, 0), pipeline_mode=pl.Buffered(1))
            for weight in weights
        ],
        out_specs=[
            pl.BlockSpec((rows, width), lambda i: (i, 0)),
            pl.BlockSpec((rows, 2 * width), lambda i: (i, 0)),
        ]
        + [block] * first,
        out_shape=[shape_of((length, width), BF), shape_of((length, 2 * width), BF)]
        + [shape_of((length, model), BF)] * first,
        compiler_params=local_params(),
        cost_estimate=cost(6 * length * model * width, 6 * length * model),
        name="glu_block_%d" % width,
    )(*([scale] if first else []), normed, cot, *weights)


def grads_kernel(plan, n_ref, c_ref, d_ref, h_ref, *outs):
    for out, spans in zip(outs, plan):
        base = 0
        for side, low, high in spans:
            left, right = (n_ref, d_ref) if side == 0 else (c_ref, h_ref)
            value = dot(left[...], right[:, low:high], TN)
            out[:, base : base + high - low] = value.astype(BF)
            base += high - low


def weight_grads(normed, cot, dgu, hidden, plan, tile=256):
    length, model = normed.shape
    widths = [sum(high - low for _, low, high in spans) for spans in plan]
    once = pl.Buffered(1)
    left = pl.BlockSpec((length, tile), lambda i: (0, i))
    return pl.pallas_call(
        functools.partial(grads_kernel, plan),
        grid=(model // tile,),
        in_specs=[left, left]
        + [pl.BlockSpec(right.shape, lambda i: (0, 0), pipeline_mode=once) for right in (dgu, hidden)],
        out_specs=[pl.BlockSpec((tile, wide), lambda i: (i, 0)) for wide in widths],
        out_shape=[shape_of((model, wide), BF) for wide in widths],
        compiler_params=local_params(),
        cost_estimate=cost(2 * length * model * sum(widths), 2 * length * (2 * model + sum(widths))),
        name="weight_grads_%d" % sum(widths),
    )(normed, cot, dgu, hidden)


def last_grads_kernel(plan, copies, count, n_ref, q_ref, k_ref, v_ref, nc_ref, k0_ref, v0_ref, *refs):
    sources, rest = refs[:count], refs[count:]
    passed, (o_ref, gate_ref, up_ref, down_ref), targets = (
        rest[: -4 - len(copies)],
        rest[-4 - len(copies) : len(rest) - len(copies)],
        rest[len(rest) - len(copies) :],
    )
    width = q_ref.shape[1]
    normed = n_ref[...]
    edge = nc_ref[...]
    o_ref[:, :width] = dot(normed, q_ref[...], TN).astype(BF)
    grad_k = dot(normed, k_ref[...], TN) + dot(edge, k0_ref[...].astype(BF), TN)
    o_ref[:, width : 2 * width] = grad_k.astype(BF)
    grad_v = dot(normed, v_ref[...], TN) + dot(edge, v0_ref[...].astype(BF), TN)
    o_ref[:, 2 * width :] = grad_v.astype(BF)

    @pl.when(pl.program_id(0) == 0)
    def _():
        for source, base, kind, low, size in plan:
            target = (gate_ref, up_ref, down_ref)[kind]
            target[:, low : low + size] = sources[source][:, base : base + size].astype(F32)

    @pl.when(pl.program_id(0) == 1)
    def _():
        for target, (dims, places) in zip(targets, copies):
            for index, from_row, rows, row, column in places:
                ref = passed[index]
                value = ref[from_row : from_row + rows, :]
                target[row : row + rows, column : column + ref.shape[1]] = value


def last_grads(normed, grads, edge, dk0, dv0, sources, plan, hidden, passed, copies, tile=256):
    length, model = normed.shape
    width = grads[0].shape[1]
    own = sources[0].shape[0]
    once = pl.Buffered(1)
    fixed = lambda i: (0, 0)

    def full(array):
        return pl.BlockSpec(array.shape, fixed, pipeline_mode=once)

    extra = [shape_of(dims, passed[places[0][0]].dtype) for dims, places in copies]
    return pl.pallas_call(
        functools.partial(last_grads_kernel, plan, copies, len(sources)),
        grid=(model // tile,),
        in_specs=[pl.BlockSpec((length, tile), lambda i: (0, i))]
        + [full(grad) for grad in grads]
        + [pl.BlockSpec((edge.shape[0], tile), lambda i: (0, i)), full(dk0), full(dv0)]
        + [full(source) for source in sources]
        + [full(array) for array in passed],
        out_specs=[pl.BlockSpec((tile, 3 * width), lambda i: (i, 0))]
        + [pl.BlockSpec((own, hidden), fixed)] * 3
        + [pl.BlockSpec(array.shape, fixed) for array in extra],
        out_shape=[shape_of((model, 3 * width), BF)]
        + [shape_of((own, hidden), F32)] * 3
        + extra,
        compiler_params=local_params(),
        cost_estimate=cost(6 * length * model * width, 2 * length * (model + 3 * width)),
        name="last_grads",
    )(normed, *grads, edge, dk0, dv0, *sources, *passed)


def owner_sum(term):
    return lax.psum_scatter(term, "dp", scatter_dimension=0, tiled=True)


def after(value, *others):
    return lax.optimization_barrier((value,) + others)[0]


GLU_PARTS = 3


def per_device(
    frames, cond_table, bucket_ids, prompt, prompt_len,
    attn_query, attn_key, attn_value, attn_out,
    cross_query, cross_key, cross_value, cross_out,
    glu_gate, glu_up, glu_down, first_gain, second_gain, third_gain, grad_out,
):
    groups = lax.axis_size("mp")
    count = lax.axis_size("dp")
    sequences = bucket_ids.shape[0]
    assert sequences == 1 and groups == 4
    share, model = frames.shape
    length = share * groups
    buckets = cond_table.shape[0]
    own_rows, width = attn_query.shape
    unit = glu_gate.shape[1] // GLU_PARTS
    context = prompt.shape[2]

    onehot = (bucket_ids[:, None] == jnp.arange(buckets)[None, :]).astype(F32)
    extra = jnp.concatenate(
        [
            first_gain[:, None],
            second_gain[:, None],
            third_gain[:, None],
            jnp.broadcast_to(onehot.astype(BF), (own_rows, buckets)),
            jnp.zeros((own_rows, 128 - 3 - buckets), BF),
        ],
        1,
    )
    packed = jnp.concatenate(
        [attn_query, attn_key, attn_value, extra, cross_query, cross_out, attn_out], 1
    )
    prompt_blocks = prompt.reshape(-1, count, context // count)
    blank = jnp.zeros_like(prompt_blocks)
    prompts = jnp.concatenate(
        [
            jnp.concatenate([prompt_blocks, blank], 2).reshape(-1, model),
            jnp.concatenate([blank, prompt_blocks], 2).reshape(-1, model),
        ],
        0,
    )
    prompt_share = jnp.concatenate([cross_key, cross_value], 0)
    glu_share = []
    for part in range(GLU_PARTS):
        span = slice(part * unit, (part + 1) * unit)
        glu_share.append(
            jnp.concatenate([glu_gate[:, span], glu_up[:, span], glu_down[:, span]], 1)
        )
    cond_row = jnp.pad(dot(onehot.astype(BF), cond_table, NN), ((0, 15), (0, 0)))
    hot = jnp.pad(onehot, ((0, 0), (3, 128 - 3 - buckets)))
    mark = jnp.pad(jnp.broadcast_to(onehot.T, (buckets, 128)), ((0, SMALL - buckets), (0, 0)))
    frames_all, grad_all, first = head_gather(frames, grad_out, packed, count)

    tables = rope_tables(length, 1.0)
    scale = sequences * count * own_rows / buckets
    (
        normed_one, queries, keys, values, gains, seq_weight, normed_cond, key0, value0,
    ) = qkv_project(frames_all, cond_row, hot, first, tables, width, scale)
    mixed, aug, cross_full, second, glu_first = attend(
        queries, keys, values, key0, value0, first, 3 * width + 128, prompt_share,
        glu_share[0], count,
    )
    cross_full = cross_full.reshape(groups, model, 2 * width)
    column = 5 * width + 128
    out_full = first[:, column : column + width]
    self_out, prompt_kv, glu_second = out_project(
        mixed, out_full, 0, prompts, second, glu_share[1], count
    )
    prompt_kv = prompt_kv.reshape(groups, prompts.shape[0], width)

    (
        after_self, normed_two, cross_q, cross_mixed, after_cross, normed_three, glu_third,
    ) = cross_forward(
        prompt_len, frames, self_out, gains, cross_full, prompt_kv, glu_share[2], count
    )
    glu_full = [glu_first, glu_second, glu_third]
    half = unit // 2
    parts = (((0, 0, half),), ((0, half, half), (1, 0, unit), (2, 0, unit)))
    h0, d0, cot_all = glu_block(normed_three, grad_all, glu_full[:1], parts[0], seq_weight)
    (pack0,) = weight_grads(normed_three, cot_all, d0, h0, (((0, 0, unit), (1, 0, half)),))
    h1, d1 = glu_block(after(normed_three, pack0), cot_all, glu_full, parts[1])
    wide = unit + 2 * unit
    pack1, pack2 = weight_grads(
        normed_three, cot_all, d1, h1,
        (
            (
                (0, 0, unit), (1, 0, half),
                (0, unit, wide), (1, half, half + unit),
                (0, wide, wide + half), (0, wide + unit, wide + unit + half),
                (1, half + unit, 2 * unit),
            ),
            (
                (0, wide + half, wide + unit), (0, wide + unit + half, wide + 2 * unit),
                (1, 2 * unit, 2 * unit + half),
            ),
        ),
    )
    glu_sum0 = owner_sum(pack0)
    pack1 = after(pack1, glu_sum0)
    glu_sum1 = owner_sum(pack1)
    back_term, out_term0, out_term1 = glu_back(
        [after(d0, pack1), d1], [h0, h1], glu_full, parts
    )

    cross_back, grad_cq, carried, carried_low, grad_kv, grad_gains, block0 = cross_backward(
        prompt_len, seq_weight, grad_out, back_term, after_cross, after_self, gains, cross_q,
        cross_full, prompt_kv, out_term0,
    )
    cross_term, grad_mixed, second_pack, glu_sum2 = mid_gather(
        carried_low, grad_kv.reshape(-1, width), normed_two, cross_back, grad_cq, cross_mixed,
        out_full, 0, mixed, prompts, pack2, groups, count,
    )
    (
        dq, dk, dv, dk0, dv0, _, grad_out_own, grad_prompt, block1, grad_cross_q, grad_cross_o,
    ) = attend_back(
        queries, aug, mixed, grad_mixed, keys, values, key0, value0, tables, cross_term,
        second_pack, out_term1, after_cross, count,
    )
    plan = []
    pieces_of = (
        (0, 0, 0, half), (1, 0, half, half), (1, 3 * half, unit, unit),
        (1, 9 * half, 2 * unit, half), (2, 0, 2 * unit + half, half),
    )
    for source, base, low, size in pieces_of:
        for kind in range(3):
            plan.append((source, base + kind * size, kind, low, size))
    short = context // count
    copies = (
        ((share, model), ((0, 0, share, 0, 0), (1, 0, share, 0, model // 2))),
        ((own_rows, width), ((2, 0, own_rows, 0, 0),)),
        ((own_rows, width), ((3, 0, own_rows, 0, 0),)),
        ((short, width), ((4, 0, short, 0, 0),)),
        ((short, width), ((4, short, short, 0, 0),)),
        ((own_rows, width), ((5, 0, own_rows, 0, 0),)),
    )
    (
        first_pack, *glu_out, block_out, grad_out_own, grad_cross_q, grad_cross_k, grad_cross_v,
        grad_cross_o,
    ) = last_grads(
        normed_one, [dq, dk, dv], normed_cond, dk0, dv0, [glu_sum0, glu_sum1, glu_sum2], plan,
        glu_gate.shape[1],
        [block0, block1, grad_out_own, grad_cross_q, grad_prompt, grad_cross_o], copies,
    )
    frames_grad, sums, *first_grads = tail_sums(
        count, buckets, [dq, dk, dv], first, first_pack, frames, carried, gains, grad_gains, mark,
        cond_row, dk0, dv0,
    )
    return (
        block_out,
        frames_grad,
        sums[:buckets],
        *first_grads,
        grad_out_own,
        grad_cross_q,
        grad_cross_k,
        grad_cross_v,
        grad_cross_o,
        *glu_out,
        sums[buckets],
        sums[buckets + 1],
        sums[buckets + 2],
    )


def solution(mesh):
    both = P(("dp", "mp"), None)
    weight = P("dp", "mp")
    return jax.shard_map(
        per_device,
        mesh=mesh,
        in_specs=(both, P(), P("dp"), P("dp", None, None), P("dp"))
        + (weight,) * 11
        + (P("dp"),) * 3
        + (both,),
        out_specs=(both, both, P()) + (weight,) * 11 + (P(),) * 3,
        check_vma=False,
    )
```

time: 841 us -> 750 us (0.89)
  Pallas kernels: 736 us -> 700 us
  waiting for transfers between devices: 21.4 us -> 0.33 us
  local copies, waits for them, and re-layouts: 31 us -> 20.4 us
  other arithmetic: 14.4 us -> 4.16 us
  matrix products: 9.3 us -> 0.12 us
    pallas_call x1, Pallas kernels: 102 us -> 77.4 us  [head_gather(): pl.pallas_call(functools.partial(head_kernel, count), out_shape=(wide, wi...]
    pallas_call x1, Pallas kernels: 96 us -> 75.2 us  [tail_sums(): pl.pallas_call(functools.partial(tail_kernel, count, buckets), grid=(9,),...]
    reduce_scatter x3 -> x2, waiting for transfers between devices: 20.7 us -> 0.3 us  [owner_sum(): return lax.psum_scatter(term, 'dp', scatter_dimension=0, tiled=True)]
    pallas_call x13 -> x12, Pallas kernels: 472 us -> 481 us  [the longest x1 101 us: attend_back(): pl.pallas_call(functools.partial(attend_back_kernel, bk, count), grid=(wi...]
    dot_general x7 -> x1, matrix products: 9.3 us -> 0.12 us  [dot(): return lax.dot_general(left, right, dims, preferred_element_type=F32)]
  transfers between devices with their start and end apart: 4 -> 2, of which waited for: 1 -> 1; matrix products, arithmetic and copies ran while one was open for 4% -> 0% of each run, Pallas kernels for 68% -> 42%
where the time goes in v3:
time: 750 us; the launch traced here: 741 us
  Pallas kernels  700 us (93%)
  local copies, waits for them, and re-layouts  20.4 us (3%)
  between operations  16.1 us (2%)
    pallas_call x1, Pallas kernels, attend_back(): pl.pallas_call(functools.partial(attend_back_kernel, bk, count), grid=(wi...  101 us
    pallas_call x1, Pallas kernels, head_gather(): pl.pallas_call(functools.partial(head_kernel, count), out_shape=(wide, wi...  77.4 us
    pallas_call x1, Pallas kernels, tail_sums(): pl.pallas_call(functools.partial(tail_kernel, count, buckets), grid=(9,),...  75.2 us
    pallas_call x1, Pallas kernels, attend(): pl.pallas_call(functools.partial(attend_kernel, bk, first, count), grid=(...  66 us
    pallas_call x1, Pallas kernels, mid_gather(): pl.pallas_call(functools.partial(mid_kernel, count), grid=(12,), in_specs...  57.9 us
    pallas_call x1, Pallas kernels, cross_forward(): pl.pallas_call(functools.partial(cross_kernel, count), grid=(2,), in_spec...  56.3 us
    pallas_call x1, Pallas kernels, out_project(): pl.pallas_call(functools.partial(out_kernel, count), grid=(8,), out_shape...  54.8 us
    pallas_call x1, Pallas kernels, glu_back(): pl.pallas_call(functools.partial(glu_back_kernel, parts, len(weights)), g...  50.3 us
  transfers between devices with their start and end apart: 2, of which 1 were waited for; matrix products, arithmetic and copies ran while one was open for 0% of the time, Pallas kernels for 42%

profile of v3, /device:TPU:0, one launch (start us, length us, event | category | flops | bytes accessed | tf_op | source)
XLA Modules:
  0.0 740.9 jit_solution(14064591993730393715)
XLA Ops:
  7.2 0.0 copy-start
  7.2 0.0 copy-start.2
  7.2 0.0 reduce-scatter.3.cloned.1.call-start
  8.6 0.6 pad_convert_fusion.hot_ref
  9.2 0.7 broadcast_in_dim.28
  10.0 0.7 broadcast_in_dim.29
  10.7 0.7 broadcast_in_dim.30
  11.5 1.1 copy.43
  12.6 0.0 copy-start.3
  12.6 1.2 fusion.4
  13.8 0.0 copy-done.2
  13.9 0.1 copy-done.3
  14.0 0.0 copy-start.7
  14.0 0.0 copy-start.8
  14.0 0.1 fusion.7
  14.1 0.2 copy.44
  14.3 0.2 copy.45
  14.5 0.3 copy-done.7
  14.9 0.1 copy-done.8
  14.9 2.0 concatenate.24.w_ref
  17.0 77.4 %head_gather.1 = (bf16[2048,1536]{1,0:T(8,128)(2,1)}, bf16[2048,1536]{1,0:T(8,128)(2,1)}, bf16[1536,2432]{1,0:T(8,128)(2,1)}) custom-call(bf16[512,1536]{1,0:T(8,128)(2,1)} %f_ref.5, bf16[512,1536]{1,0:T(8,128)(2,1)} %go_ref.1, bf16[192,2432]{1,0:T(8,128)(2,1)} %concatenate.24.w_ref), custom_call_target="tpu_custom_call" | custom-call | flops 1 | bytes 146800640 | tf_op jit(solution)/shard_map/head_gather/pallas_call | solution.py:583
  94.4 0.0 copy-start.9
  94.4 0.0 copy-start.10
  94.4 2.4 slice.45.w_ref
  96.8 0.0 copy-done
  96.8 0.1 fusion
  96.9 0.6 pad.18.r_ref
  97.6 0.0 copy-done.9
  97.6 0.0 copy-done.10
  97.6 0.7 pad_maximum_fusion.4.w_ref
  98.3 0.9 pad_maximum_fusion.p_ref
  99.2 0.9 pad_maximum_fusion.3.share_ref
  100.1 1.1 pad_maximum_fusion.1
  101.2 17.5 %qkv_project.1 = (bf16[2048,1536]{1,0:T(8,128)(2,1)}, bf16[2048,384]{1,0:T(8,128)(2,1)}, bf16[2048,384]{1,0:T(8,128)(2,1)}, bf16[2048,384]{1,0:T(8,128)(2,1)}, f...) custom-call(bf16[2048,1536]{1,0:T(8,128)(2,1)} %get-tuple-element.93, ...), custom_call_target="tpu_custom_call" | custom-call | flops 7247757312 | bytes 25165824 | tf_op jit(solution)/shard_map/qkv_project/pallas_call | solution.py:1078
  118.6 66.0 %attend.1 = (bf16[2048,384]{1,0:T(8,128)(2,1)}, bf16[2048,384]{1,0:T(8,128)(2,1)}, bf16[6144,768]{1,0:T(8,128)(2,1)}, bf16[1536,384]{1,0:T(8,128)(2,1)}, bf16[1536,1536]{1,0:T(8,128)(2,1)}) custom-call(bf16[2048,384]{1,0:T(8,128)(2,1)} %get-tuple-element.96.q_ref, bf16[2048,384]{1,0:T(8,128)(2,1)} %get-tuple-element.97.k_ref, ...), custom_call_target="tpu_custom_call" | custom-call | flops 25769803776 | bytes 7864320 | tf_op jit(solution)/shard_map/attend/pallas_call | solution.py:1177
  184.6 54.8 %out_project.1 = (f32[512,1536]{1,0:T(8,128)}, bf16[1024,384]{1,0:T(8,128)(2,1)}, bf16[1536,1536]{1,0:T(8,128)(2,1)}) custom-call(bf16[2048,384]{1,0:T(8,128)(2,1)} %get-tuple-element.102.m_ref.o_ref, bf16[1536,384]{1,0:T(8,128)(2,1)} %slice.45.w_ref, bf16[256,1536]{1,0:T(8,128)(2,1)} %pad_maximum_fusion.p_ref, bf16[1536,384]{1,0:T(8,128)(2,1)} %get-tuple-element.104.wp_ref, ...), custom_call_target="tpu_custom_call" | custom-call | flops 1 | bytes 146800640 | tf_op jit(solution)/shard_map/out_project/pallas_call | solution.py:755
  239.4 56.3 %cross_forward.1 = (f32[512,1536]{1,0:T(8,128)}, bf16[512,1536]{1,0:T(8,128)(2,1)}, bf16[512,1536]{1,0:T(8,128)(2,1)}, bf16[512,1536]{1,0:T(8,128)(2,1)}, f32[51...) custom-call(s32[1]{0:T(128)S(6)} %copy.51.len_ref, bf16[512,1536]{1,0:T(8,128)(2,1)} %f_ref.5, ...), custom_call_target="tpu_custom_call" | custom-call | flops 1 | bytes 146800640 | tf_op jit(solution)/shard_map/cross_forward/pallas_call | solution.py:1448
  295.7 12.6 %glu_block_256.1 = (bf16[2048,256]{1,0:T(8,128)(2,1)}, bf16[2048,512]{1,0:T(8,128)(2,1)}, bf16[2048,1536]{1,0:T(8,128)(2,1)}) custom-call(f32[8,128]{1,0:T(8,128)} %get-tuple-element.103.refs_0_.w_ref, bf16[2048,1536]{1,0:T(8,128)(2,1)} %get-tuple-element.115.refs_1_.n_ref.refs_0_, bf16[2048,1536]{1,0:T(8,128)(2,1)} %get-tuple-element.110.refs_2_, ...), custom_call_target="tpu_custom_call" | custom-call | flops 4831838208 | bytes 18874368 | tf_op jit(solution)/shard_map/glu_block_256/pallas_call | solution.py:1633
  308.3 11.2 %weight_grads_768.1 = bf16[1536,768]{1,0:T(8,128)(2,1)} custom-call(bf16[2048,1536]{1,0:T(8,128)(2,1)} %get-tuple-element.115.refs_1_.n_ref.refs_0_, bf16[2048,1536]{1,0:T(8,128)(2,1)} %get-tuple-element.113.c_ref.refs_1_, bf16[2048,512]{1,0:T(8,128)(2,1)} %get-tuple-element.122.d_ref.d0_ref, bf16[2048,256]{1,0:T(8,128)(2,1)} %get-tuple-element.114.h_ref.h0_ref), custom_call_target="tpu_custom_call" | custom-call | flops 4831838208 | bytes 15728640 | tf_op jit(solution)/shard_map/weight_grads_768/pallas_call | solution.py:1670
  319.5 0.0 reduce-scatter.3.cloned.1.call-update
  319.5 0.0 reduce-scatter.5.cloned.1.call-start
  319.5 34.1 %glu_block_1280.1 = (bf16[2048,1280]{1,0:T(8,128)(2,1)}, bf16[2048,2560]{1,0:T(8,128)(2,1)}) custom-call(bf16[2048,1536]{1,0:T(8,128)(2,1)} %get-tuple-element.115.refs_1_.n_ref.refs_0_, bf16[2048,1536]{1,0:T(8,128)(2,1)} %get-tuple-element.113.c_ref.refs_1_, bf16[1536,1536]{1,0:T(8,128)(2,1)} %get-tuple-element.111.refs_3_.refs_2_.refs_0_, ...), custom_call_target="tpu_custom_call" | custom-call | flops 24159191040 | bytes 18874368 | tf_op jit(solution)/shard_map/glu_block_1280/pallas_call | solution.py:1633
  353.7 32.8 %weight_grads_3840.1 = (bf16[1536,3072]{1,0:T(8,128)(2,1)}, bf16[1536,768]{1,0:T(8,128)(2,1)}) custom-call(bf16[2048,1536]{1,0:T(8,128)(2,1)} %get-tuple-element.115.refs_1_.n_ref.refs_0_, bf16[2048,1536]{1,0:T(8,128)(2,1)} %get-tuple-element.113.c_ref.refs_1_, bf16[2048,2560]{1,0:T(8,128)(2,1)} %get-tuple-element.118.d_ref.d1_ref, ...), custom_call_target="tpu_custom_call" | custom-call | flops 24159191040 | bytes 28311552 | tf_op jit(solution)/shard_map/weight_grads_3840/pallas_call | solution.py:1670
  386.5 0.3 reduce-scatter.3.cloned.1.call-done.refs_0_
  386.8 0.0 reduce-scatter.5.cloned.1.call-update
  386.8 50.3 %glu_back.1 = (f32[512,1536]{1,0:T(8,128)}, bf16[2048,768]{1,0:T(8,128)(2,1)}, bf16[2048,768]{1,0:T(8,128)(2,1)}) custom-call(bf16[2048,512]{1,0:T(8,128)(2,1)} %get-tuple-element.122.d_ref.d0_ref, bf16[2048,2560]{1,0:T(8,128)(2,1)} %get-tuple-element.118.d_ref.d1_ref, bf16[2048,256]{1,0:T(8,128)(2,1)} %get-tuple-element.114.h_ref.h0_ref, ...), custom_call_target="tpu_custom_call" | custom-call | flops 1 | bytes 146800640 | tf_op jit(solution)/shard_map/glu_back/pallas_call | solution.py:855
  437.1 32.8 %cross_backward.1 = (bf16[512,1536]{1,0:T(8,128)(2,1)}, bf16[512,1536]{1,0:T(8,128)(2,1)}, f32[512,1536]{1,0:T(8,128)}, bf16[512,1536]{1,0:T(8,128)(2,1)}, bf16[...) custom-call(s32[1]{0:T(128)S(6)} %copy.51.len_ref, ...), custom_call_target="tpu_custom_call" | custom-call | flops 4831838208 | bytes 28311552 | tf_op jit(solution)/shard_map/cross_backward/pallas_call | solution.py:1555
  469.9 57.9 %mid_gather.1 = (bf16[6144,768]{1,0:T(8,128)(2,1)}, bf16[2048,384]{1,0:T(8,128)(2,1)}, bf16[1536,768]{1,0:T(8,128)(2,1)}, f32[192,768]{1,0:T(8,128)}) custom-call(bf16[512,1536]{1,0:T(8,128)(2,1)} %get-tuple-element.128.c_ref, bf16[1024,384]{1,0:T(8,128)(2,1)} %bitcast.22, bf16[512,1536]{1,0:T(8,128)(2,1)} %get-tuple-element.130.n_ref, ...), custom_call_target="tpu_custom_call" | custom-call | flops 1 | bytes 146800640 | tf_op jit(solution)/shard_map/mid_gather/pallas_call | solution.py:986
  527.8 101.4 %attend_back.1 = (bf16[2048,384]{1,0:T(8,128)(2,1)}, bf16[2048,384]{1,0:T(8,128)(2,1)}, bf16[2048,384]{1,0:T(8,128)(2,1)}, f32[16,384]{1,0:T(8,128)}, f32[16,384...) custom-call(bf16[2048,384]{1,0:T(8,128)(2,1)} %get-tuple-element.96., ...), custom_call_target="tpu_custom_call" | custom-call | flops 64424509440 | bytes 15728640 | tf_op jit(solution)/shard_map/attend_back/pallas_call | solution.py:1329
  629.1 0.0 reduce-scatter.5.cloned.1.call-done.refs_1_
  629.2 19.7 %last_grads.1 = (bf16[1536,1152]{1,0:T(8,128)(2,1)}, f32[192,1536]{1,0:T(8,128)}, f32[192,1536]{1,0:T(8,128)}, f32[192,1536]{1,0:T(8,128)}, bf16[512,1536]{1,0:T...) custom-call(bf16[2048,1536]{1,0:T(8,128)(2,1)} %get-tuple-element.95, ...), custom_call_target="tpu_custom_call" | custom-call | flops 7247757312 | bytes 11010048 | tf_op jit(solution)/shard_map/last_grads/pallas_call | solution.py:1725
  648.8 0.7 pad.22.mark_ref
  649.5 75.2 %tail_sums.1 = (f32[512,1536]{1,0:T(8,128)}, f32[16,1536]{1,0:T(8,128)}, f32[192,384]{1,0:T(8,128)}, f32[192,384]{1,0:T(8,128)}, f32[192,384]{1,0:T(8,128)}) custom-call(bf16[2048,384]{1,0:T(8,128)(2,1)} %get-tuple-element.139.q_ref, bf16[2048,384]{1,0:T(8,128)(2,1)} %get-tuple-element.140.k_ref, bf16[2048,384]{1,0:T(8,128)(2,1)} %get-tuple-element.141.v_ref, ...), custom_call_target="tpu_custom_call" | custom-call | flops 1 | bytes 146800640 | tf_op jit(solution)/shard_map/tail_sums/pallas_call | solution.py:687
  724.7 1.6 slice_reduce_fusion
  726.2 1.4 slice.52
  727.7 0.0 copy-start.6
  727.7 3.8 copy.52
  731.5 0.0 copy-done.6
  731.5 0.7 copy.53
  732.2 0.0 copy-done.5
  732.2 0.7 copy.54
  732.9 0.0 copy-done.4
  732.9 0.7 copy.55
  733.7 0.0 copy-done.1
  (10 shorter events, 0.1 us)
Async XLA Ops:
  7.2 89.6 %copy-start = (bf16[8,1536]{1,0:T(8,128)(2,1)S(1)}, bf16[8,1536]{1,0:T(8,128)(2,1)}, u32[]{:S(2)}) copy-start(bf16[8,1536]{1,0:T(8,128)(2,1)} %param.24) | copy-start | bytes 73732
  7.2 6.6 copy-start.2
  7.2 379.6 %reduce-scatter.3.cloned.1.call-start = ((), (), s32[]{:S(2)}) async-start(), calls=%async_computation.2 | async-start | bytes 2654208 | tf_op jit(solution)/shard_map/reduce_scatter | solution.py:1746
  12.6 1.4 copy-start.3
  14.0 0.9 copy-start.7
  14.0 1.0 copy-start.8
  94.4 3.2 copy-start.9
  94.4 3.2 copy-start.10
  319.5 309.7 %reduce-scatter.5.cloned.1.call-start = ((), (), s32[]{:S(2)}) async-start(), calls=%async_computation.3 | async-start | bytes 10616832 | tf_op jit(solution)/shard_map/reduce_scatter | solution.py:1746
  727.7 3.8 copy-start.6
  727.7 4.6 copy-start.5
  727.7 5.3 copy-start.4
  727.7 6.0 copy-start.1
Sparse Core Ops, SparseCore 0:
  319.6 67.1 reduce-scatter.2
  390.4 182.0 reduce-scatter.4

commit v4 on v3

--- a/solution.py
+++ b/solution.py
@@ -73,6 +73,18 @@
         + pltpu.roll(values, half, 1) * upper
         + pltpu.roll(values, 2 * HD - half, 1) * lower
     )
+
+
+def bucket_column(hot, rows):
+    dims = (rows, 128)
+    pick = lax.broadcasted_iota(jnp.int32, dims, 0) + 3 == lanes(dims)
+    marks = jnp.broadcast_to(hot, (8, 128)).astype(BF)
+    return dot(jnp.where(pick, 1.0, 0.0).astype(BF), marks, NT)[:, 0:1]
+
+
+def bucket_row(hot, table):
+    rows = table.shape[0]
+    return jnp.sum(table.astype(F32) * bucket_column(hot, rows), axis=0, keepdims=True)
 
 
 def lanes(dims):
@@ -397,8 +409,10 @@
 
 
 class RingGather:
-    def __init__(self, count, w_ref, o_ref, scratch):
+    def __init__(self, count, w_ref, o_ref, scratch, here=False):
         bounce, lsem, fs, fr, bs, br = scratch
+        if here:
+            bounce = w_ref
         ring = Ring(count)
         self.ahead, self.behind, self.half = ring.ahead, ring.behind, ring.half
         rows = w_ref.shape[0]
@@ -424,17 +438,19 @@
         for hop in range(self.half):
             self.forward.append(copies(ring.at(-hop), hop, fs, fr, ring.ahead, 0))
             self.backward.append(copies(ring.at(hop), hop, bs, br, ring.behind, 1))
-        self.load = pltpu.make_async_copy(w_ref, bounce, lsem.at[0])
+        self.load = None if here else pltpu.make_async_copy(w_ref, bounce, lsem.at[0])
         self.store = pltpu.make_async_copy(bounce, slot(ring.me), lsem.at[1])
 
     def start(self):
         for c in range(CUTS):
             self.forward[0][c].start()
             self.backward[0][c].start()
-        self.load.start()
+        if self.load is not None:
+            self.load.start()
 
     def place(self):
-        self.load.wait()
+        if self.load is not None:
+            self.load.wait()
         self.store.start()
 
     def hop(self, hop):
@@ -556,14 +572,52 @@
                 copy.wait_send()
 
 
-def head_kernel(count, f_ref, g_ref, w_ref, fo_ref, go_ref, wo_ref, *scratch):
-    job = Gather(f_ref, fo_ref, scratch[0:4])
-    late = Gather(g_ref, go_ref, scratch[4:8])
-    ring = RingGather(count, w_ref, wo_ref, scratch[8:])
+HEAD = 6
+
+
+def head_kernel(count, f_ref, g_ref, gains_ref, hot_ref, *refs):
+    mats, glu = refs[:HEAD], refs[HEAD : HEAD + 3]
+    fo_ref, go_ref, wo_ref = refs[HEAD + 3 : HEAD + 6]
+    shares = refs[HEAD + 6 : HEAD + 9]
+    scratch = refs[HEAD + 9 :]
+    pack, held, psem, hsem, osem = scratch[:5]
+    job = Gather(f_ref, fo_ref, scratch[5:9])
+    late = Gather(g_ref, go_ref, scratch[9:13])
+    ring = RingGather(count, pack, wo_ref, scratch[13:], here=True)
+    width = mats[0].shape[1]
+    side = 4 * width
+    loads = []
+    for i, mat in enumerate(mats):
+        base = i * width if i < 4 else i * width + 128
+        loads.append(pltpu.make_async_copy(mat, pack.at[:, pl.ds(base, width)], psem.at[i]))
+    fetch = [pltpu.make_async_copy(mat, held.at[i], hsem.at[i]) for i, mat in enumerate(glu)]
+    unit = held.shape[2] // len(shares)
+    stores = []
+    for at, share in enumerate(shares):
+        for i in range(3):
+            stores.append(
+                pltpu.make_async_copy(
+                    held.at[i, :, pl.ds(at * unit, unit)],
+                    share.at[:, pl.ds(i * unit, unit)],
+                    osem.at[at, i],
+                )
+            )
+    for copy in loads + fetch:
+        copy.start()
     greet([job.to_sib, job.to_far, ring.ahead, ring.behind])
+    job.start()
+    dims = (8, 128)
+    pick = lax.broadcasted_iota(jnp.int32, dims, 0) == lanes(dims)
+    columns = dot(gains_ref[...], jnp.where(pick, 1.0, 0.0).astype(BF), TN)
+    pack[:, side : side + 128] = (columns + hot_ref[...]).astype(BF)
+    for copy in loads:
+        copy.wait()
     ring.start()
-    job.start()
     ring.place()
+    for copy in fetch:
+        copy.wait()
+    for copy in stores:
+        copy.start()
     ring.hop(1)
     for k in range(CHUNKS):
         job.forward(k)
@@ -575,21 +629,36 @@
     job.finish()
     late.finish()
     ring.finish()
-
-
-def head_gather(frames, grads, packed, count):
+    for copy in stores:
+        copy.wait()
+
+
+def head_gather(frames, grads, gains, hot, mats, glu, parts, count):
     rows, width = frames.shape
+    own = mats[0].shape[0]
+    columns = len(mats) * mats[0].shape[1] + 128
+    hidden = glu[0].shape[1]
     wide = shape_of((4 * rows, width), BF)
+    vmem = pl.BlockSpec(memory_space=pltpu.VMEM)
     return pl.pallas_call(
         functools.partial(head_kernel, count),
-        out_shape=(wide, wide, shape_of((count * packed.shape[0], packed.shape[1]), BF)),
-        in_specs=[ANY] * 3,
-        out_specs=(ANY,) * 3,
-        scratch_shapes=gather_scratch(rows, width) * 2 + ring_scratch(*packed.shape, count // 2),
+        out_shape=(wide, wide, shape_of((count * own, columns), BF))
+        + (shape_of((own, 3 * hidden // parts), BF),) * parts,
+        in_specs=[ANY, ANY, vmem, vmem] + [ANY] * (len(mats) + 3),
+        out_specs=(ANY,) * (3 + parts),
+        scratch_shapes=[
+            pltpu.VMEM((own, columns), BF),
+            pltpu.VMEM((3, own, hidden), BF),
+            pltpu.SemaphoreType.DMA((len(mats),)),
+            pltpu.SemaphoreType.DMA((3,)),
+            pltpu.SemaphoreType.DMA((parts, 3)),
+        ]
+        + gather_scratch(rows, width) * 2
+        + ring_scratch(16, 128, count // 2),
         compiler_params=local_params(collective_id=0, has_side_effects=True),
         cost_estimate=BUSY,
         name="head_gather",
-    )(frames, grads, packed)
+    )(frames, grads, gains, hot, *mats, *glu)
 
 
 SMALL = 16
@@ -597,10 +666,9 @@
 
 def tail_kernel(
     count, buckets, q_ref, k_ref, v_ref, wq_ref, wk_ref, wv_ref,
-    a_ref, f_ref, c_ref, g_ref, dg_ref, mark_ref, r_ref, k0_ref, v0_ref, o_ref, s_ref, *scratch,
+    a_ref, f_ref, c_ref, g_ref, dg_ref, hot_ref, r_ref, k0_ref, v0_ref,
+    o_ref, s_ref, w_ref, *scratch,
 ):
-    outs = scratch[:3]
-    scratch = scratch[3:]
     total, held = scratch[0:2]
     job = LocalSum(total, scratch[2:9])
     ring = RingSum(count, [a_ref], scratch[9:19])
@@ -613,7 +681,6 @@
     while bit < count:
         partners.append({"dp": me + bit * (1 - 2 * ((me // bit) % 2)), "mp": mp})
         bit *= 2
-
     @pl.when(step == 0)
     def _():
         greet(partners + [ring.ahead, ring.behind])
@@ -632,40 +699,48 @@
 
     @pl.when(step == 8)
     def _():
+        edge = dot(k0_ref[...].astype(BF), wk_ref[...], NT) + dot(
+            v0_ref[...].astype(BF), wv_ref[...], NT
+        )
+        unit, spread = norm_rows(bucket_row(hot_ref[...], r_ref[...]))
+        edge_back, edge_part = norm_back(edge[0:1, :], unit, spread, g_ref[0:1, :])
+        place = lax.broadcasted_iota(jnp.int32, held.shape, 0)
+        held[...] = (
+            bucket_column(hot_ref[...], SMALL) * edge_back
+            + jnp.where(place == buckets, edge_part, 0.0)
+            + jnp.where(place == buckets + 1, dg_ref[1:2, :], 0.0)
+            + jnp.where(place == buckets + 2, dg_ref[2:3, :], 0.0)
+        )
         for hop in range(1, ring.half - 1):
             ring.hop(hop)
         job.land()
         unit, spread = norm_rows(f_ref[...].astype(F32))
         back, part = norm_back(total[...], unit, spread, g_ref[0:1, :])
+        held[buckets : buckets + 1, :] += part
+        copies = [
+            remote(sent.at[i], got.at[i], ss.at[i], rs.at[i], partner)
+            for i, partner in enumerate(partners)
+        ]
+        sent[0] = held[...]
+        copies[0].start()
+        ring.hop(ring.half - 1)
         o_ref[...] = c_ref[...] + back
-        edge = dot(k0_ref[...].astype(BF), wk_ref[...], NT) + dot(
-            v0_ref[...].astype(BF), wv_ref[...], NT
-        )
-        unit, spread = norm_rows(r_ref[...])
-        edge_back, edge_part = norm_back(edge[0:1, :], unit[0:1, :], spread[0:1, :], g_ref[0:1, :])
-        row = lax.broadcasted_iota(jnp.int32, held.shape, 0)
-        held[...] = (
-            mark_ref[:, 0:1] * edge_back
-            + jnp.where(row == buckets, part + edge_part, 0.0)
-            + jnp.where(row == buckets + 1, dg_ref[1:2, :], 0.0)
-            + jnp.where(row == buckets + 2, dg_ref[2:3, :], 0.0)
-        )
-        ring.hop(ring.half - 1)
-        for i, partner in enumerate(partners):
-            sent[i] = held[...]
-            copy = remote(sent.at[i], got.at[i], ss.at[i], rs.at[i], partner)
-            copy.start()
+        for i, copy in enumerate(copies):
             copy.wait_recv()
             held[...] += got[i]
+            if i + 1 < len(copies):
+                sent[i + 1] = held[...]
+                copies[i + 1].start()
+        for copy in copies:
             copy.wait_send()
         s_ref[...] = held[...]
-        ring.finish(outs)
+        ring.finish([w_ref])
         job.finish()
 
 
 def tail_sums(
-    count, buckets, grads_qkv, weights, grads, frames, carried, gains, grad_gains, mark, cond_row,
-    dk0, dv0,
+    count, buckets, grads_qkv, weights, grads, frames, carried, gains, grad_gains, hot,
+    table_rows, dk0, dv0,
 ):
     share, model = frames.shape
     width = grads_qkv[0].shape[1]
@@ -680,10 +755,12 @@
         return pl.BlockSpec(array.shape, lambda i: (0,) * array.ndim, pipeline_mode=once)
 
     small = pltpu.VMEM((steps, SMALL, model), F32)
-    out_shape = (shape_of((share, model), F32), shape_of((SMALL, model), F32)) + (
-        shape_of((rows, wide // 3), F32),
-    ) * 3
-    whole = [frames, carried, gains, grad_gains, mark, cond_row, dk0, dv0]
+    out_shape = (
+        shape_of((share, model), F32),
+        shape_of((SMALL, model), F32),
+        shape_of((rows, wide), F32),
+    )
+    whole = [frames, carried, gains, grad_gains, hot, table_rows, dk0, dv0]
     return pl.pallas_call(
         functools.partial(tail_kernel, count, buckets),
         grid=(9,),
@@ -1041,8 +1118,8 @@
         sw_ref[...] = jnp.broadcast_to(
             scale / jnp.sum(totals * hot_ref[...], axis=1, keepdims=True), sw_ref.shape
         )
-        unit, _ = norm_rows(r_ref[...])
-        normed = (unit * g_ref[0:1, :]).astype(BF)
+        unit, _ = norm_rows(bucket_row(hot_ref[...], r_ref[...]))
+        normed = jnp.broadcast_to(unit * g_ref[0:1, :], nc_ref.shape).astype(BF)
         nc_ref[...] = normed
         out = dot(normed, w_ref[:, width:], NN).astype(BF)
         k0_ref[...] = out[:, :width]
@@ -1061,7 +1138,7 @@
     v_ref[...] = out[:, 2 * width : 3 * width].astype(BF)
 
 
-def qkv_project(frames, cond_row, hot, weights, tables, width, scale):
+def qkv_project(frames, table_rows, hot, weights, tables, width, scale):
     length, model = frames.shape
     rows = 256
     block = pl.BlockSpec((rows, model), lambda i: (i, 0))
@@ -1080,8 +1157,8 @@
         grid=(length // rows,),
         in_specs=[
             block,
-            pl.BlockSpec((model, 128), lambda i: (0, 3 * width // 128)),
-            pl.BlockSpec(cond_row.shape, fixed),
+            pl.BlockSpec((model, 128), lambda i: (0, 4 * width // 128)),
+            pl.BlockSpec(table_rows.shape, fixed),
             pl.BlockSpec(hot.shape, fixed),
             pl.BlockSpec((model, 3 * width), fixed),
             table,
@@ -1093,7 +1170,7 @@
         compiler_params=local_params(),
         cost_estimate=cost(6 * length * model * width, 8 * length * model),
         name="qkv_project",
-    )(frames, weights, cond_row, hot, weights, *tables)
+    )(frames, weights, table_rows, hot, weights, *tables)
 
 
 def attend_kernel(
@@ -1771,19 +1848,8 @@
     context = prompt.shape[2]
 
     onehot = (bucket_ids[:, None] == jnp.arange(buckets)[None, :]).astype(F32)
-    extra = jnp.concatenate(
-        [
-            first_gain[:, None],
-            second_gain[:, None],
-            third_gain[:, None],
-            jnp.broadcast_to(onehot.astype(BF), (own_rows, buckets)),
-            jnp.zeros((own_rows, 128 - 3 - buckets), BF),
-        ],
-        1,
-    )
-    packed = jnp.concatenate(
-        [attn_query, attn_key, attn_value, extra, cross_query, cross_out, attn_out], 1
-    )
+    gain_rows = jnp.pad(jnp.stack([first_gain, second_gain, third_gain]), ((0, 5), (0, 0)))
+    hot = jnp.pad(onehot, ((0, 0), (3, 128 - 3 - buckets)))
     prompt_blocks = prompt.reshape(-1, count, context // count)
     blank = jnp.zeros_like(prompt_blocks)
     prompts = jnp.concatenate(
@@ -1794,31 +1860,24 @@
         0,
     )
     prompt_share = jnp.concatenate([cross_key, cross_value], 0)
-    glu_share = []
-    for part in range(GLU_PARTS):
-        span = slice(part * unit, (part + 1) * unit)
-        glu_share.append(
-            jnp.concatenate([glu_gate[:, span], glu_up[:, span], glu_down[:, span]], 1)
-        )
-    cond_row = jnp.pad(dot(onehot.astype(BF), cond_table, NN), ((0, 15), (0, 0)))
-    hot = jnp.pad(onehot, ((0, 0), (3, 128 - 3 - buckets)))
-    mark = jnp.pad(jnp.broadcast_to(onehot.T, (buckets, 128)), ((0, SMALL - buckets), (0, 0)))
-    frames_all, grad_all, first = head_gather(frames, grad_out, packed, count)
+    frames_all, grad_all, first, *glu_share = head_gather(
+        frames, grad_out, gain_rows, hot,
+        [attn_query, attn_key, attn_value, attn_out, cross_query, cross_out],
+        [glu_gate, glu_up, glu_down], GLU_PARTS, count,
+    )
 
     tables = rope_tables(length, 1.0)
     scale = sequences * count * own_rows / buckets
     (
         normed_one, queries, keys, values, gains, seq_weight, normed_cond, key0, value0,
-    ) = qkv_project(frames_all, cond_row, hot, first, tables, width, scale)
+    ) = qkv_project(frames_all, cond_table, hot, first, tables, width, scale)
     mixed, aug, cross_full, second, glu_first = attend(
-        queries, keys, values, key0, value0, first, 3 * width + 128, prompt_share,
+        queries, keys, values, key0, value0, first, 4 * width + 128, prompt_share,
         glu_share[0], count,
     )
     cross_full = cross_full.reshape(groups, model, 2 * width)
-    column = 5 * width + 128
-    out_full = first[:, column : column + width]
     self_out, prompt_kv, glu_second = out_project(
-        mixed, out_full, 0, prompts, second, glu_share[1], count
+        mixed, first, 3, prompts, second, glu_share[1], count
     )
     prompt_kv = prompt_kv.reshape(groups, prompts.shape[0], width)
 
@@ -1862,7 +1921,7 @@
     )
     cross_term, grad_mixed, second_pack, glu_sum2 = mid_gather(
         carried_low, grad_kv.reshape(-1, width), normed_two, cross_back, grad_cq, cross_mixed,
-        out_full, 0, mixed, prompts, pack2, groups, count,
+        first, 3, mixed, prompts, pack2, groups, count,
     )
     (
         dq, dk, dv, dk0, dv0, _, grad_out_own, grad_prompt, block1, grad_cross_q, grad_cross_o,
@@ -1895,15 +1954,17 @@
         glu_gate.shape[1],
         [block0, block1, grad_out_own, grad_cross_q, grad_prompt, grad_cross_o], copies,
     )
-    frames_grad, sums, *first_grads = tail_sums(
-        count, buckets, [dq, dk, dv], first, first_pack, frames, carried, gains, grad_gains, mark,
-        cond_row, dk0, dv0,
+    frames_grad, sums, first_grad = tail_sums(
+        count, buckets, [dq, dk, dv], first, first_pack, frames, carried, gains, grad_gains, hot,
+        cond_table, dk0, dv0,
     )
     return (
         block_out,
         frames_grad,
         sums[:buckets],
-        *first_grads,
+        first_grad[:, :width],
+        first_grad[:, width : 2 * width],
+        first_grad[:, 2 * width :],
         grad_out_own,
         grad_cross_q,
         grad_cross_k,

time: 750 us -> 741 us (0.988)
  local copies, waits for them, and re-layouts: 20.4 us -> 12.4 us
where the time goes in v4:
time: 741 us; the launch traced here: 732 us
  Pallas kernels  701 us (95%)
  between operations  16 us (2%)
  local copies, waits for them, and re-layouts  12.4 us (2%)
    pallas_call x1, Pallas kernels, attend_back(): pl.pallas_call(functools.partial(attend_back_kernel, bk, count), grid=(wi...  102 us
    pallas_call x1, Pallas kernels, head_gather(): pl.pallas_call(functools.partial(head_kernel, count), out_shape=(wide, wi...  79.9 us
    pallas_call x1, Pallas kernels, tail_sums(): pl.pallas_call(functools.partial(tail_kernel, count, buckets), grid=(9,),...  73.5 us
    pallas_call x1, Pallas kernels, attend(): pl.pallas_call(functools.partial(attend_kernel, bk, first, count), grid=(...  65.9 us
    pallas_call x1, Pallas kernels, mid_gather(): pl.pallas_call(functools.partial(mid_kernel, count), grid=(12,), in_specs...  57.3 us
    pallas_call x1, Pallas kernels, cross_forward(): pl.pallas_call(functools.partial(cross_kernel, count), grid=(2,), in_spec...  56.3 us
    pallas_call x1, Pallas kernels, out_project(): pl.pallas_call(functools.partial(out_kernel, count), grid=(8,), out_shape...  54.9 us
    pallas_call x1, Pallas kernels, glu_back(): pl.pallas_call(functools.partial(glu_back_kernel, parts, len(weights)), g...  50.3 us
  transfers between devices with their start and end apart: 2, of which 1 were waited for; matrix products, arithmetic and copies ran while one was open for 0% of the time, Pallas kernels for 42%

profile of v4, /device:TPU:0, one launch (start us, length us, event | category | flops | bytes accessed | tf_op | source)
XLA Modules:
  0.0 732.3 jit_solution(16244873876236542850)
XLA Ops:
  7.2 0.0 copy-start
  7.2 0.0 copy-start.1
  7.2 0.0 reduce-scatter.3.cloned.1.call-start
  8.6 0.6 pad_convert_fusion.hot_ref
  9.2 0.7 stack.12
  9.8 0.7 stack.13
  10.5 0.7 stack.14
  11.1 1.1 copy.40
  12.2 0.1 fusion.6
  12.4 0.2 copy.41
  12.6 0.2 copy.42
  12.7 0.0 copy-done
  12.7 0.0 copy-done.1
  12.8 0.7 pad_maximum_fusion.1.w_ref
  13.4 0.9 pad_maximum_fusion.p_ref
  14.4 0.6 fusion.4.gains_ref
  15.0 79.9 %head_gather.1 = (bf16[2048,1536]{1,0:T(8,128)(2,1)}, bf16[2048,1536]{1,0:T(8,128)(2,1)}, bf16[1536,2432]{1,0:T(8,128)(2,1)}, bf16[192,1536]{1,0:T(8,128)(2,1)},...) custom-call(bf16[512,1536]{1,0:T(8,128)(2,1)} %f_ref.5, bf16[512,1536]{1,0:T(8,128)(2,1)} %go_ref.1, ...), custom_call_target="tpu_custom_call" | custom-call | flops 1 | bytes 146800640 | tf_op jit(solution)/shard_map/head_gather/pallas_call | solution.py:643
  94.9 17.8 %qkv_project.1 = (bf16[2048,1536]{1,0:T(8,128)(2,1)}, bf16[2048,384]{1,0:T(8,128)(2,1)}, bf16[2048,384]{1,0:T(8,128)(2,1)}, bf16[2048,384]{1,0:T(8,128)(2,1)}, f...) custom-call(bf16[2048,1536]{1,0:T(8,128)(2,1)} %get-tuple-element.94, ...), custom_call_target="tpu_custom_call" | custom-call | flops 7247757312 | bytes 25165824 | tf_op jit(solution)/shard_map/qkv_project/pallas_call | solution.py:1155
  112.7 65.9 %attend.1 = (bf16[2048,384]{1,0:T(8,128)(2,1)}, bf16[2048,384]{1,0:T(8,128)(2,1)}, bf16[6144,768]{1,0:T(8,128)(2,1)}, bf16[1536,384]{1,0:T(8,128)(2,1)}, bf16[1536,1536]{1,0:T(8,128)(2,1)}) custom-call(bf16[2048,384]{1,0:T(8,128)(2,1)} %get-tuple-element.97.q_ref, bf16[2048,384]{1,0:T(8,128)(2,1)} %get-tuple-element.98.k_ref, ...), custom_call_target="tpu_custom_call" | custom-call | flops 25769803776 | bytes 7864320 | tf_op jit(solution)/shard_map/attend/pallas_call | solution.py:1254
  178.6 54.9 %out_project.1 = (f32[512,1536]{1,0:T(8,128)}, bf16[1024,384]{1,0:T(8,128)(2,1)}, bf16[1536,1536]{1,0:T(8,128)(2,1)}) custom-call(bf16[2048,384]{1,0:T(8,128)(2,1)} %get-tuple-element.104.m_ref.o_ref, bf16[1536,2432]{1,0:T(8,128)(2,1)} %get-tuple-element.95.s_ref.w_ref.x_ref.wq_ref.wk_ref.wv_ref, bf16[256,1536]{1,0:T(8,128)(2,1)} %pad_maximum_fusion.p_ref, ...), custom_call_target="tpu_custom_call" | custom-call | flops 1 | bytes 146800640 | tf_op jit(solution)/shard_map/out_project/pallas_call | solution.py:832
  233.5 56.3 %cross_forward.1 = (f32[512,1536]{1,0:T(8,128)}, bf16[512,1536]{1,0:T(8,128)(2,1)}, bf16[512,1536]{1,0:T(8,128)(2,1)}, bf16[512,1536]{1,0:T(8,128)(2,1)}, f32[51...) custom-call(s32[1]{0:T(128)S(6)} %copy.45.len_ref, bf16[512,1536]{1,0:T(8,128)(2,1)} %f_ref.5, ...), custom_call_target="tpu_custom_call" | custom-call | flops 1 | bytes 146800640 | tf_op jit(solution)/shard_map/cross_forward/pallas_call | solution.py:1525
  289.8 12.6 %glu_block_256.1 = (bf16[2048,256]{1,0:T(8,128)(2,1)}, bf16[2048,512]{1,0:T(8,128)(2,1)}, bf16[2048,1536]{1,0:T(8,128)(2,1)}) custom-call(f32[8,128]{1,0:T(8,128)} %get-tuple-element.105.refs_0_.w_ref, bf16[2048,1536]{1,0:T(8,128)(2,1)} %get-tuple-element.119.refs_1_.n_ref.refs_0_, bf16[2048,1536]{1,0:T(8,128)(2,1)} %get-tuple-element.114.refs_2_, ...), custom_call_target="tpu_custom_call" | custom-call | flops 4831838208 | bytes 18874368 | tf_op jit(solution)/shard_map/glu_block_256/pallas_call | solution.py:1710
  302.4 11.2 %weight_grads_768.1 = bf16[1536,768]{1,0:T(8,128)(2,1)} custom-call(bf16[2048,1536]{1,0:T(8,128)(2,1)} %get-tuple-element.119.refs_1_.n_ref.refs_0_, bf16[2048,1536]{1,0:T(8,128)(2,1)} %get-tuple-element.117.c_ref.refs_1_, bf16[2048,512]{1,0:T(8,128)(2,1)} %get-tuple-element.126.d_ref.d0_ref, bf16[2048,256]{1,0:T(8,128)(2,1)} %get-tuple-element.118.h_ref.h0_ref), custom_call_target="tpu_custom_call" | custom-call | flops 4831838208 | bytes 15728640 | tf_op jit(solution)/shard_map/weight_grads_768/pallas_call | solution.py:1747
  313.6 0.0 reduce-scatter.3.cloned.1.call-update
  313.7 0.0 reduce-scatter.5.cloned.1.call-start
  313.7 34.0 %glu_block_1280.1 = (bf16[2048,1280]{1,0:T(8,128)(2,1)}, bf16[2048,2560]{1,0:T(8,128)(2,1)}) custom-call(bf16[2048,1536]{1,0:T(8,128)(2,1)} %get-tuple-element.119.refs_1_.n_ref.refs_0_, bf16[2048,1536]{1,0:T(8,128)(2,1)} %get-tuple-element.117.c_ref.refs_1_, bf16[1536,1536]{1,0:T(8,128)(2,1)} %get-tuple-element.115.refs_3_.refs_2_.refs_0_, ...), custom_call_target="tpu_custom_call" | custom-call | flops 24159191040 | bytes 18874368 | tf_op jit(solution)/shard_map/glu_block_1280/pallas_call | solution.py:1710
  347.8 32.8 %weight_grads_3840.1 = (bf16[1536,3072]{1,0:T(8,128)(2,1)}, bf16[1536,768]{1,0:T(8,128)(2,1)}) custom-call(bf16[2048,1536]{1,0:T(8,128)(2,1)} %get-tuple-element.119.refs_1_.n_ref.refs_0_, bf16[2048,1536]{1,0:T(8,128)(2,1)} %get-tuple-element.117.c_ref.refs_1_, bf16[2048,2560]{1,0:T(8,128)(2,1)} %get-tuple-element.122.d_ref.d1_ref, ...), custom_call_target="tpu_custom_call" | custom-call | flops 24159191040 | bytes 28311552 | tf_op jit(solution)/shard_map/weight_grads_3840/pallas_call | solution.py:1747
  380.6 0.3 reduce-scatter.3.cloned.1.call-done.refs_0_
  380.9 0.0 reduce-scatter.5.cloned.1.call-update
  380.9 50.3 %glu_back.1 = (f32[512,1536]{1,0:T(8,128)}, bf16[2048,768]{1,0:T(8,128)(2,1)}, bf16[2048,768]{1,0:T(8,128)(2,1)}) custom-call(bf16[2048,512]{1,0:T(8,128)(2,1)} %get-tuple-element.126.d_ref.d0_ref, bf16[2048,2560]{1,0:T(8,128)(2,1)} %get-tuple-element.122.d_ref.d1_ref, bf16[2048,256]{1,0:T(8,128)(2,1)} %get-tuple-element.118.h_ref.h0_ref, ...), custom_call_target="tpu_custom_call" | custom-call | flops 1 | bytes 146800640 | tf_op jit(solution)/shard_map/glu_back/pallas_call | solution.py:932
  431.2 32.8 %cross_backward.1 = (bf16[512,1536]{1,0:T(8,128)(2,1)}, bf16[512,1536]{1,0:T(8,128)(2,1)}, f32[512,1536]{1,0:T(8,128)}, bf16[512,1536]{1,0:T(8,128)(2,1)}, bf16[...) custom-call(s32[1]{0:T(128)S(6)} %copy.45.len_ref, ...), custom_call_target="tpu_custom_call" | custom-call | flops 4831838208 | bytes 28311552 | tf_op jit(solution)/shard_map/cross_backward/pallas_call | solution.py:1632
  464.0 57.3 %mid_gather.1 = (bf16[6144,768]{1,0:T(8,128)(2,1)}, bf16[2048,384]{1,0:T(8,128)(2,1)}, bf16[1536,768]{1,0:T(8,128)(2,1)}, f32[192,768]{1,0:T(8,128)}) custom-call(bf16[512,1536]{1,0:T(8,128)(2,1)} %get-tuple-element.132.c_ref, bf16[1024,384]{1,0:T(8,128)(2,1)} %bitcast.16, bf16[512,1536]{1,0:T(8,128)(2,1)} %get-tuple-element.134.n_ref, ...), custom_call_target="tpu_custom_call" | custom-call | flops 1 | bytes 146800640 | tf_op jit(solution)/shard_map/mid_gather/pallas_call | solution.py:1063
  521.2 101.7 %attend_back.1 = (bf16[2048,384]{1,0:T(8,128)(2,1)}, bf16[2048,384]{1,0:T(8,128)(2,1)}, bf16[2048,384]{1,0:T(8,128)(2,1)}, f32[16,384]{1,0:T(8,128)}, f32[16,384...) custom-call(bf16[2048,384]{1,0:T(8,128)(2,1)} %get-tuple-element.97., ...), custom_call_target="tpu_custom_call" | custom-call | flops 64424509440 | bytes 15728640 | tf_op jit(solution)/shard_map/attend_back/pallas_call | solution.py:1406
  622.9 0.0 reduce-scatter.5.cloned.1.call-done.refs_1_
  623.0 19.7 %last_grads.1 = (bf16[1536,1152]{1,0:T(8,128)(2,1)}, f32[192,1536]{1,0:T(8,128)}, f32[192,1536]{1,0:T(8,128)}, f32[192,1536]{1,0:T(8,128)}, bf16[512,1536]{1,0:T...) custom-call(bf16[2048,1536]{1,0:T(8,128)(2,1)} %get-tuple-element.96, ...), custom_call_target="tpu_custom_call" | custom-call | flops 7247757312 | bytes 11010048 | tf_op jit(solution)/shard_map/last_grads/pallas_call | solution.py:1802
  642.6 73.5 %tail_sums.1 = (f32[512,1536]{1,0:T(8,128)}, f32[16,1536]{1,0:T(8,128)}, f32[192,1152]{1,0:T(8,128)}) custom-call(bf16[2048,384]{1,0:T(8,128)(2,1)} %get-tuple-element.143.q_ref, bf16[2048,384]{1,0:T(8,128)(2,1)} %get-tuple-element.144.k_ref, bf16[2048,384]{1,0:T(8,128)(2,1)} %get-tuple-element.145.v_ref, ...), custom_call_target="tpu_custom_call" | custom-call | flops 1 | bytes 146800640 | tf_op jit(solution)/shard_map/tail_sums/pallas_call | solution.py:764
  716.2 1.6 slice_reduce_fusion
  717.7 1.4 slice.21
  719.1 2.1 fusion.5
  721.2 3.8 copy.46
  (1 shorter events, 0.0 us)
Async XLA Ops:
  7.2 5.5 copy-start
  7.2 5.5 copy-start.1
  7.2 373.7 %reduce-scatter.3.cloned.1.call-start = ((), (), s32[]{:S(2)}) async-start(), calls=%async_computation.2 | async-start | bytes 2654208 | tf_op jit(solution)/shard_map/reduce_scatter | solution.py:1823
  313.7 309.3 %reduce-scatter.5.cloned.1.call-start = ((), (), s32[]{:S(2)}) async-start(), calls=%async_computation.3 | async-start | bytes 10616832 | tf_op jit(solution)/shard_map/reduce_scatter | solution.py:1823
Sparse Core Ops, SparseCore 0:
  313.8 67.0 reduce-scatter.2
  384.5 182.0 reduce-scatter.4

commit v5 on v4

--- a/solution.py
+++ b/solution.py
@@ -374,6 +374,14 @@
     cross = 1 - ((1 - late) * (step % 2) + late * ((step // 2) % 2))
     quarter = (chip + other - 2 * chip * other) * 2 + (core + cross - 2 * core * cross)
     return quarter * 2 + (1 - late) * ((step // 2) % 2) + late * (step % 2)
+
+
+def term_quarter(slot):
+    me = lax.axis_index("mp")
+    chip, core = me // 2, me % 2
+    other = 1 - slot // 2
+    cross = 1 - slot % 2
+    return (chip + other - 2 * chip * other) * 2 + (core + cross - 2 * core * cross)
 
 
 def arrival_quarter(turn):
@@ -665,7 +673,7 @@
 
 
 def tail_kernel(
-    count, buckets, q_ref, k_ref, v_ref, wq_ref, wk_ref, wv_ref,
+    count, buckets, q_ref, k_ref, v_ref, fa_ref, wq_ref, wk_ref, wv_ref,
     a_ref, f_ref, c_ref, g_ref, dg_ref, hot_ref, r_ref, k0_ref, v0_ref,
     o_ref, s_ref, w_ref, *scratch,
 ):
@@ -685,6 +693,7 @@
     def _():
         greet(partners + [ring.ahead, ring.behind])
         ring.start()
+        held[...] = jnp.zeros_like(held)
 
     @pl.when(step < 8)
     def _():
@@ -697,6 +706,12 @@
 
     job.after_step(step)
 
+    @pl.when((step >= 8) & (step < 12))
+    def _():
+        unit, _ = norm_rows(fa_ref[...].astype(F32))
+        part = jnp.sum(unit * job.terms[step - 8].astype(F32), axis=0, keepdims=True)
+        held[buckets : buckets + 1, :] += part
+
     @pl.when(step == 8)
     def _():
         edge = dot(k0_ref[...].astype(BF), wk_ref[...], NT) + dot(
@@ -705,32 +720,41 @@
         unit, spread = norm_rows(bucket_row(hot_ref[...], r_ref[...]))
         edge_back, edge_part = norm_back(edge[0:1, :], unit, spread, g_ref[0:1, :])
         place = lax.broadcasted_iota(jnp.int32, held.shape, 0)
-        held[...] = (
+        held[...] += (
             bucket_column(hot_ref[...], SMALL) * edge_back
             + jnp.where(place == buckets, edge_part, 0.0)
             + jnp.where(place == buckets + 1, dg_ref[1:2, :], 0.0)
             + jnp.where(place == buckets + 2, dg_ref[2:3, :], 0.0)
         )
-        for hop in range(1, ring.half - 1):
+        for hop in range(2, ring.half - 1):
             ring.hop(hop)
-        job.land()
-        unit, spread = norm_rows(f_ref[...].astype(F32))
-        back, part = norm_back(total[...], unit, spread, g_ref[0:1, :])
-        held[buckets : buckets + 1, :] += part
+
+    @pl.when(step == 4)
+    def _():
+        ring.hop(1)
+
+    @pl.when(step == 11)
+    def _():
+        ring.hop(ring.half - 1)
+
+    @pl.when(step == 12)
+    def _():
         copies = [
             remote(sent.at[i], got.at[i], ss.at[i], rs.at[i], partner)
             for i, partner in enumerate(partners)
         ]
         sent[0] = held[...]
         copies[0].start()
-        ring.hop(ring.half - 1)
-        o_ref[...] = c_ref[...] + back
         for i, copy in enumerate(copies):
             copy.wait_recv()
             held[...] += got[i]
             if i + 1 < len(copies):
                 sent[i + 1] = held[...]
                 copies[i + 1].start()
+        job.land()
+        unit, spread = norm_rows(f_ref[...].astype(F32))
+        back, _ = norm_back(total[...], unit, spread, g_ref[0:1, :])
+        o_ref[...] = c_ref[...] + back
         for copy in copies:
             copy.wait_send()
         s_ref[...] = held[...]
@@ -739,7 +763,7 @@
 
 
 def tail_sums(
-    count, buckets, grads_qkv, weights, grads, frames, carried, gains, grad_gains, hot,
+    count, buckets, grads_qkv, frames_all, weights, grads, frames, carried, gains, grad_gains, hot,
     table_rows, dk0, dv0,
 ):
     share, model = frames.shape
@@ -763,12 +787,13 @@
     whole = [frames, carried, gains, grad_gains, hot, table_rows, dk0, dv0]
     return pl.pallas_call(
         functools.partial(tail_kernel, count, buckets),
-        grid=(9,),
+        grid=(13,),
         out_shape=out_shape,
         in_specs=[
             pl.BlockSpec((block, width), lambda i: (order_block(jnp.minimum(i, 7)), 0))
             for _ in range(3)
         ]
+        + [pl.BlockSpec((share, model), lambda i: (term_quarter(jnp.clip(i - 8, 0, 3)), 0))]
         + [
             pl.BlockSpec(
                 (model, width), functools.partial(lambda at, i: (0, at), at), pipeline_mode=once
@@ -785,7 +810,7 @@
         compiler_params=local_params(collective_id=6, has_side_effects=True),
         cost_estimate=BUSY,
         name="tail_sums",
-    )(*grads_qkv, weights, weights, weights, grads, *whole)
+    )(*grads_qkv, frames_all, weights, weights, weights, grads, *whole)
 
 
 def out_kernel(
@@ -1955,7 +1980,7 @@
         [block0, block1, grad_out_own, grad_cross_q, grad_prompt, grad_cross_o], copies,
     )
     frames_grad, sums, first_grad = tail_sums(
-        count, buckets, [dq, dk, dv], first, first_pack, frames, carried, gains, grad_gains, hot,
+        count, buckets, [dq, dk, dv], frames_all, first, first_pack, frames, carried, gains, grad_gains, hot,
         cond_table, dk0, dv0,
     )
     return (

time: 741 us -> 735 us (level)
  no operation moved by 1% of the time
where the time goes in v5:
time: 735 us; the launch traced here: 726 us
  Pallas kernels  695 us (95%)
  between operations  16 us (2%)
  local copies, waits for them, and re-layouts  12.4 us (2%)
    pallas_call x1, Pallas kernels, attend_back(): pl.pallas_call(functools.partial(attend_back_kernel, bk, count), grid=(wi...  102 us
    pallas_call x1, Pallas kernels, head_gather(): pl.pallas_call(functools.partial(head_kernel, count), out_shape=(wide, wi...  79.9 us
    pallas_call x1, Pallas kernels, tail_sums(): pl.pallas_call(functools.partial(tail_kernel, count, buckets), grid=(13,)...  67.9 us
    pallas_call x1, Pallas kernels, attend(): pl.pallas_call(functools.partial(attend_kernel, bk, first, count), grid=(...  66 us
    pallas_call x1, Pallas kernels, mid_gather(): pl.pallas_call(functools.partial(mid_kernel, count), grid=(12,), in_specs...  56.9 us
    pallas_call x1, Pallas kernels, cross_forward(): pl.pallas_call(functools.partial(cross_kernel, count), grid=(2,), in_spec...  56.3 us
    pallas_call x1, Pallas kernels, out_project(): pl.pallas_call(functools.partial(out_kernel, count), grid=(8,), out_shape...  54.9 us
    pallas_call x1, Pallas kernels, glu_back(): pl.pallas_call(functools.partial(glu_back_kernel, parts, len(weights)), g...  50.3 us
  transfers between devices with their start and end apart: 2, of which 1 were waited for; matrix products, arithmetic and copies ran while one was open for 0% of the time, Pallas kernels for 42%

profile of v5, /device:TPU:0, one launch (start us, length us, event | category | flops | bytes accessed | tf_op | source)
XLA Modules:
  0.0 726.2 jit_solution(9545090812781824355)
XLA Ops:
  7.2 0.0 copy-start
  7.2 0.0 copy-start.1
  7.2 0.0 reduce-scatter.3.cloned.1.call-start
  8.6 0.6 pad_convert_fusion.hot_ref
  9.2 0.7 stack.12
  9.8 0.7 stack.13
  10.5 0.7 stack.14
  11.1 1.1 copy.40
  12.2 0.1 fusion.6
  12.4 0.2 copy.41
  12.6 0.2 copy.42
  12.7 0.0 copy-done
  12.7 0.0 copy-done.1
  12.8 0.7 pad_maximum_fusion.1.w_ref
  13.4 0.9 pad_maximum_fusion.p_ref
  14.4 0.6 fusion.4.gains_ref
  15.0 79.9 %head_gather.1 = (bf16[2048,1536]{1,0:T(8,128)(2,1)}, bf16[2048,1536]{1,0:T(8,128)(2,1)}, bf16[1536,2432]{1,0:T(8,128)(2,1)}, bf16[192,1536]{1,0:T(8,128)(2,1)},...) custom-call(bf16[512,1536]{1,0:T(8,128)(2,1)} %f_ref.5, bf16[512,1536]{1,0:T(8,128)(2,1)} %go_ref.1, ...), custom_call_target="tpu_custom_call" | custom-call | flops 1 | bytes 146800640 | tf_op jit(solution)/shard_map/head_gather/pallas_call | solution.py:651
  94.9 17.8 %qkv_project.1 = (bf16[2048,1536]{1,0:T(8,128)(2,1)}, bf16[2048,384]{1,0:T(8,128)(2,1)}, bf16[2048,384]{1,0:T(8,128)(2,1)}, bf16[2048,384]{1,0:T(8,128)(2,1)}, f...) custom-call(bf16[2048,1536]{1,0:T(8,128)(2,1)} %get-tuple-element.94, ...), custom_call_target="tpu_custom_call" | custom-call | flops 7247757312 | bytes 25165824 | tf_op jit(solution)/shard_map/qkv_project/pallas_call | solution.py:1180
  112.7 66.0 %attend.1 = (bf16[2048,384]{1,0:T(8,128)(2,1)}, bf16[2048,384]{1,0:T(8,128)(2,1)}, bf16[6144,768]{1,0:T(8,128)(2,1)}, bf16[1536,384]{1,0:T(8,128)(2,1)}, bf16[1536,1536]{1,0:T(8,128)(2,1)}) custom-call(bf16[2048,384]{1,0:T(8,128)(2,1)} %get-tuple-element.97.q_ref, bf16[2048,384]{1,0:T(8,128)(2,1)} %get-tuple-element.98.k_ref, ...), custom_call_target="tpu_custom_call" | custom-call | flops 25769803776 | bytes 7864320 | tf_op jit(solution)/shard_map/attend/pallas_call | solution.py:1279
  178.7 54.9 %out_project.1 = (f32[512,1536]{1,0:T(8,128)}, bf16[1024,384]{1,0:T(8,128)(2,1)}, bf16[1536,1536]{1,0:T(8,128)(2,1)}) custom-call(bf16[2048,384]{1,0:T(8,128)(2,1)} %get-tuple-element.104.m_ref.o_ref, bf16[1536,2432]{1,0:T(8,128)(2,1)} %get-tuple-element.95.s_ref.w_ref.x_ref.wq_ref.wk_ref.wv_ref, bf16[256,1536]{1,0:T(8,128)(2,1)} %pad_maximum_fusion.p_ref, ...), custom_call_target="tpu_custom_call" | custom-call | flops 1 | bytes 146800640 | tf_op jit(solution)/shard_map/out_project/pallas_call | solution.py:857
  233.6 56.3 %cross_forward.1 = (f32[512,1536]{1,0:T(8,128)}, bf16[512,1536]{1,0:T(8,128)(2,1)}, bf16[512,1536]{1,0:T(8,128)(2,1)}, bf16[512,1536]{1,0:T(8,128)(2,1)}, f32[51...) custom-call(s32[1]{0:T(128)S(6)} %copy.45.len_ref, bf16[512,1536]{1,0:T(8,128)(2,1)} %f_ref.5, ...), custom_call_target="tpu_custom_call" | custom-call | flops 1 | bytes 146800640 | tf_op jit(solution)/shard_map/cross_forward/pallas_call | solution.py:1550
  289.9 12.6 %glu_block_256.1 = (bf16[2048,256]{1,0:T(8,128)(2,1)}, bf16[2048,512]{1,0:T(8,128)(2,1)}, bf16[2048,1536]{1,0:T(8,128)(2,1)}) custom-call(f32[8,128]{1,0:T(8,128)} %get-tuple-element.105.refs_0_.w_ref, bf16[2048,1536]{1,0:T(8,128)(2,1)} %get-tuple-element.119.refs_1_.n_ref.refs_0_, bf16[2048,1536]{1,0:T(8,128)(2,1)} %get-tuple-element.114.refs_2_, ...), custom_call_target="tpu_custom_call" | custom-call | flops 4831838208 | bytes 18874368 | tf_op jit(solution)/shard_map/glu_block_256/pallas_call | solution.py:1735
  302.5 11.1 %weight_grads_768.1 = bf16[1536,768]{1,0:T(8,128)(2,1)} custom-call(bf16[2048,1536]{1,0:T(8,128)(2,1)} %get-tuple-element.119.refs_1_.n_ref.refs_0_, bf16[2048,1536]{1,0:T(8,128)(2,1)} %get-tuple-element.117.c_ref.refs_1_, bf16[2048,512]{1,0:T(8,128)(2,1)} %get-tuple-element.126.d_ref.d0_ref, bf16[2048,256]{1,0:T(8,128)(2,1)} %get-tuple-element.118.h_ref.h0_ref), custom_call_target="tpu_custom_call" | custom-call | flops 4831838208 | bytes 15728640 | tf_op jit(solution)/shard_map/weight_grads_768/pallas_call | solution.py:1772
  313.6 0.0 reduce-scatter.3.cloned.1.call-update
  313.6 0.0 reduce-scatter.5.cloned.1.call-start
  313.7 34.1 %glu_block_1280.1 = (bf16[2048,1280]{1,0:T(8,128)(2,1)}, bf16[2048,2560]{1,0:T(8,128)(2,1)}) custom-call(bf16[2048,1536]{1,0:T(8,128)(2,1)} %get-tuple-element.119.refs_1_.n_ref.refs_0_, bf16[2048,1536]{1,0:T(8,128)(2,1)} %get-tuple-element.117.c_ref.refs_1_, bf16[1536,1536]{1,0:T(8,128)(2,1)} %get-tuple-element.115.refs_3_.refs_2_.refs_0_, ...), custom_call_target="tpu_custom_call" | custom-call | flops 24159191040 | bytes 18874368 | tf_op jit(solution)/shard_map/glu_block_1280/pallas_call | solution.py:1735
  347.8 32.8 %weight_grads_3840.1 = (bf16[1536,3072]{1,0:T(8,128)(2,1)}, bf16[1536,768]{1,0:T(8,128)(2,1)}) custom-call(bf16[2048,1536]{1,0:T(8,128)(2,1)} %get-tuple-element.119.refs_1_.n_ref.refs_0_, bf16[2048,1536]{1,0:T(8,128)(2,1)} %get-tuple-element.117.c_ref.refs_1_, bf16[2048,2560]{1,0:T(8,128)(2,1)} %get-tuple-element.122.d_ref.d1_ref, ...), custom_call_target="tpu_custom_call" | custom-call | flops 24159191040 | bytes 28311552 | tf_op jit(solution)/shard_map/weight_grads_3840/pallas_call | solution.py:1772
  380.6 0.3 reduce-scatter.3.cloned.1.call-done.refs_0_
  380.9 0.0 reduce-scatter.5.cloned.1.call-update
  381.0 50.3 %glu_back.1 = (f32[512,1536]{1,0:T(8,128)}, bf16[2048,768]{1,0:T(8,128)(2,1)}, bf16[2048,768]{1,0:T(8,128)(2,1)}) custom-call(bf16[2048,512]{1,0:T(8,128)(2,1)} %get-tuple-element.126.d_ref.d0_ref, bf16[2048,2560]{1,0:T(8,128)(2,1)} %get-tuple-element.122.d_ref.d1_ref, bf16[2048,256]{1,0:T(8,128)(2,1)} %get-tuple-element.118.h_ref.h0_ref, ...), custom_call_target="tpu_custom_call" | custom-call | flops 1 | bytes 146800640 | tf_op jit(solution)/shard_map/glu_back/pallas_call | solution.py:957
  431.2 32.8 %cross_backward.1 = (bf16[512,1536]{1,0:T(8,128)(2,1)}, bf16[512,1536]{1,0:T(8,128)(2,1)}, f32[512,1536]{1,0:T(8,128)}, bf16[512,1536]{1,0:T(8,128)(2,1)}, bf16[...) custom-call(s32[1]{0:T(128)S(6)} %copy.45.len_ref, ...), custom_call_target="tpu_custom_call" | custom-call | flops 4831838208 | bytes 28311552 | tf_op jit(solution)/shard_map/cross_backward/pallas_call | solution.py:1657
  464.0 56.9 %mid_gather.1 = (bf16[6144,768]{1,0:T(8,128)(2,1)}, bf16[2048,384]{1,0:T(8,128)(2,1)}, bf16[1536,768]{1,0:T(8,128)(2,1)}, f32[192,768]{1,0:T(8,128)}) custom-call(bf16[512,1536]{1,0:T(8,128)(2,1)} %get-tuple-element.132.c_ref, bf16[1024,384]{1,0:T(8,128)(2,1)} %bitcast.16, bf16[512,1536]{1,0:T(8,128)(2,1)} %get-tuple-element.134.n_ref, ...), custom_call_target="tpu_custom_call" | custom-call | flops 1 | bytes 146800640 | tf_op jit(solution)/shard_map/mid_gather/pallas_call | solution.py:1088
  520.9 101.6 %attend_back.1 = (bf16[2048,384]{1,0:T(8,128)(2,1)}, bf16[2048,384]{1,0:T(8,128)(2,1)}, bf16[2048,384]{1,0:T(8,128)(2,1)}, f32[16,384]{1,0:T(8,128)}, f32[16,384...) custom-call(bf16[2048,384]{1,0:T(8,128)(2,1)} %get-tuple-element.97., ...), custom_call_target="tpu_custom_call" | custom-call | flops 64424509440 | bytes 15728640 | tf_op jit(solution)/shard_map/attend_back/pallas_call | solution.py:1431
  622.5 0.0 reduce-scatter.5.cloned.1.call-done.refs_1_
  622.5 19.7 %last_grads.1 = (bf16[1536,1152]{1,0:T(8,128)(2,1)}, f32[192,1536]{1,0:T(8,128)}, f32[192,1536]{1,0:T(8,128)}, f32[192,1536]{1,0:T(8,128)}, bf16[512,1536]{1,0:T...) custom-call(bf16[2048,1536]{1,0:T(8,128)(2,1)} %get-tuple-element.96, ...), custom_call_target="tpu_custom_call" | custom-call | flops 7247757312 | bytes 11010048 | tf_op jit(solution)/shard_map/last_grads/pallas_call | solution.py:1827
  642.2 67.9 %tail_sums.1 = (f32[512,1536]{1,0:T(8,128)}, f32[16,1536]{1,0:T(8,128)}, f32[192,1152]{1,0:T(8,128)}) custom-call(bf16[2048,384]{1,0:T(8,128)(2,1)} %get-tuple-element.143.q_ref, bf16[2048,384]{1,0:T(8,128)(2,1)} %get-tuple-element.144.k_ref, bf16[2048,384]{1,0:T(8,128)(2,1)} %get-tuple-element.145.v_ref, bf16[2048,1536]{1,0:T(8,128)(2,1)} %get-tuple-element.94.x_ref.fa_ref, ...), custom_call_target="tpu_custom_call" | custom-call | flops 1 | bytes 146800640 | tf_op jit(solution)/shard_map/tail_sums/pallas_call | solution.py:788
  710.1 1.6 slice_reduce_fusion
  711.7 1.4 slice.21
  713.1 2.1 fusion.5
  715.1 3.8 copy.46
  (1 shorter events, 0.0 us)
Async XLA Ops:
  7.2 5.5 copy-start
  7.2 5.5 copy-start.1
  7.2 373.7 %reduce-scatter.3.cloned.1.call-start = ((), (), s32[]{:S(2)}) async-start(), calls=%async_computation.2 | async-start | bytes 2654208 | tf_op jit(solution)/shard_map/reduce_scatter | solution.py:1848
  313.6 308.9 %reduce-scatter.5.cloned.1.call-start = ((), (), s32[]{:S(2)}) async-start(), calls=%async_computation.3 | async-start | bytes 10616832 | tf_op jit(solution)/shard_map/reduce_scatter | solution.py:1848
Sparse Core Ops, SparseCore 0:
  313.8 67.1 reduce-scatter.2
  384.5 182.1 reduce-scatter.4

commit v6 on v5

--- a/solution.py
+++ b/solution.py
@@ -1014,10 +1014,14 @@
         beside.start()
         ring.start()
 
-    @pl.when(step == 6)
+    @pl.when(step == 4)
     def _():
         for hop in range(1, ring.half // 2):
             ring.hop(hop)
+
+    @pl.when(step == 8)
+    def _():
+        ring.hop(ring.half // 2)
 
     @pl.when(step == 1)
     def _():
@@ -1045,13 +1049,12 @@
 
     @pl.when(step == 10)
     def _():
-        ring.hop(ring.half // 2)
+        for hop in range(ring.half // 2 + 1, ring.half):
+            ring.hop(hop)
         small.land()
         for k in range(CHUNKS):
             across[k].wait_recv()
             onward[k].start()
-        for hop in range(ring.half // 2 + 1, ring.half):
-            ring.hop(hop)
         total[...] += use(slots[1])
 
     @pl.when(step == 11)

time: 735 us -> 733 us (level)
  no operation moved by 1% of the time
where the time goes in v6:
time: 733 us; the launch traced here: 725 us
  Pallas kernels  693 us (95%)
  between operations  16 us (2%)
  local copies, waits for them, and re-layouts  12.4 us (2%)
    pallas_call x1, Pallas kernels, attend_back(): pl.pallas_call(functools.partial(attend_back_kernel, bk, count), grid=(wi...  105 us
    pallas_call x1, Pallas kernels, head_gather(): pl.pallas_call(functools.partial(head_kernel, count), out_shape=(wide, wi...  79.9 us
    pallas_call x1, Pallas kernels, tail_sums(): pl.pallas_call(functools.partial(tail_kernel, count, buckets), grid=(13,)...  67.2 us
    pallas_call x1, Pallas kernels, attend(): pl.pallas_call(functools.partial(attend_kernel, bk, first, count), grid=(...  66 us
    pallas_call x1, Pallas kernels, cross_forward(): pl.pallas_call(functools.partial(cross_kernel, count), grid=(2,), in_spec...  56.3 us
    pallas_call x1, Pallas kernels, out_project(): pl.pallas_call(functools.partial(out_kernel, count), grid=(8,), out_shape...  54.9 us
    pallas_call x1, Pallas kernels, mid_gather(): pl.pallas_call(functools.partial(mid_kernel, count), grid=(12,), in_specs...  53.1 us
    pallas_call x1, Pallas kernels, glu_back(): pl.pallas_call(functools.partial(glu_back_kernel, parts, len(weights)), g...  50.3 us
  transfers between devices with their start and end apart: 2, of which 1 were waited for; matrix products, arithmetic and copies ran while one was open for 0% of the time, Pallas kernels for 42%

profile of v6, /device:TPU:0, one launch (start us, length us, event | category | flops | bytes accessed | tf_op | source)
XLA Modules:
  0.0 724.6 jit_solution(1046802330449346984)
XLA Ops:
  7.2 0.0 copy-start
  7.2 0.0 copy-start.1
  7.2 0.0 reduce-scatter.3.cloned.1.call-start
  8.6 0.6 pad_convert_fusion.hot_ref
  9.2 0.7 stack.12
  9.8 0.7 stack.13
  10.5 0.7 stack.14
  11.1 1.1 copy.40
  12.2 0.1 fusion.6
  12.4 0.2 copy.41
  12.6 0.2 copy.42
  12.7 0.0 copy-done
  12.7 0.0 copy-done.1
  12.8 0.7 pad_maximum_fusion.1.w_ref
  13.4 0.9 pad_maximum_fusion.p_ref
  14.4 0.6 fusion.4.gains_ref
  15.0 79.9 %head_gather.1 = (bf16[2048,1536]{1,0:T(8,128)(2,1)}, bf16[2048,1536]{1,0:T(8,128)(2,1)}, bf16[1536,2432]{1,0:T(8,128)(2,1)}, bf16[192,1536]{1,0:T(8,128)(2,1)},...) custom-call(bf16[512,1536]{1,0:T(8,128)(2,1)} %f_ref.5, bf16[512,1536]{1,0:T(8,128)(2,1)} %go_ref.1, ...), custom_call_target="tpu_custom_call" | custom-call | flops 1 | bytes 146800640 | tf_op jit(solution)/shard_map/head_gather/pallas_call | solution.py:651
  94.9 17.8 %qkv_project.1 = (bf16[2048,1536]{1,0:T(8,128)(2,1)}, bf16[2048,384]{1,0:T(8,128)(2,1)}, bf16[2048,384]{1,0:T(8,128)(2,1)}, bf16[2048,384]{1,0:T(8,128)(2,1)}, f...) custom-call(bf16[2048,1536]{1,0:T(8,128)(2,1)} %get-tuple-element.94, ...), custom_call_target="tpu_custom_call" | custom-call | flops 7247757312 | bytes 25165824 | tf_op jit(solution)/shard_map/qkv_project/pallas_call | solution.py:1183
  112.7 66.0 %attend.1 = (bf16[2048,384]{1,0:T(8,128)(2,1)}, bf16[2048,384]{1,0:T(8,128)(2,1)}, bf16[6144,768]{1,0:T(8,128)(2,1)}, bf16[1536,384]{1,0:T(8,128)(2,1)}, bf16[1536,1536]{1,0:T(8,128)(2,1)}) custom-call(bf16[2048,384]{1,0:T(8,128)(2,1)} %get-tuple-element.97.q_ref, bf16[2048,384]{1,0:T(8,128)(2,1)} %get-tuple-element.98.k_ref, ...), custom_call_target="tpu_custom_call" | custom-call | flops 25769803776 | bytes 7864320 | tf_op jit(solution)/shard_map/attend/pallas_call | solution.py:1282
  178.7 54.9 %out_project.1 = (f32[512,1536]{1,0:T(8,128)}, bf16[1024,384]{1,0:T(8,128)(2,1)}, bf16[1536,1536]{1,0:T(8,128)(2,1)}) custom-call(bf16[2048,384]{1,0:T(8,128)(2,1)} %get-tuple-element.104.m_ref.o_ref, bf16[1536,2432]{1,0:T(8,128)(2,1)} %get-tuple-element.95.s_ref.w_ref.x_ref.wq_ref.wk_ref.wv_ref, bf16[256,1536]{1,0:T(8,128)(2,1)} %pad_maximum_fusion.p_ref, ...), custom_call_target="tpu_custom_call" | custom-call | flops 1 | bytes 146800640 | tf_op jit(solution)/shard_map/out_project/pallas_call | solution.py:857
  233.6 56.3 %cross_forward.1 = (f32[512,1536]{1,0:T(8,128)}, bf16[512,1536]{1,0:T(8,128)(2,1)}, bf16[512,1536]{1,0:T(8,128)(2,1)}, bf16[512,1536]{1,0:T(8,128)(2,1)}, f32[51...) custom-call(s32[1]{0:T(128)S(6)} %copy.45.len_ref, bf16[512,1536]{1,0:T(8,128)(2,1)} %f_ref.5, ...), custom_call_target="tpu_custom_call" | custom-call | flops 1 | bytes 146800640 | tf_op jit(solution)/shard_map/cross_forward/pallas_call | solution.py:1553
  289.9 12.6 %glu_block_256.1 = (bf16[2048,256]{1,0:T(8,128)(2,1)}, bf16[2048,512]{1,0:T(8,128)(2,1)}, bf16[2048,1536]{1,0:T(8,128)(2,1)}) custom-call(f32[8,128]{1,0:T(8,128)} %get-tuple-element.105.refs_0_.w_ref, bf16[2048,1536]{1,0:T(8,128)(2,1)} %get-tuple-element.119.refs_1_.n_ref.refs_0_, bf16[2048,1536]{1,0:T(8,128)(2,1)} %get-tuple-element.114.refs_2_, ...), custom_call_target="tpu_custom_call" | custom-call | flops 4831838208 | bytes 18874368 | tf_op jit(solution)/shard_map/glu_block_256/pallas_call | solution.py:1738
  302.5 11.1 %weight_grads_768.1 = bf16[1536,768]{1,0:T(8,128)(2,1)} custom-call(bf16[2048,1536]{1,0:T(8,128)(2,1)} %get-tuple-element.119.refs_1_.n_ref.refs_0_, bf16[2048,1536]{1,0:T(8,128)(2,1)} %get-tuple-element.117.c_ref.refs_1_, bf16[2048,512]{1,0:T(8,128)(2,1)} %get-tuple-element.126.d_ref.d0_ref, bf16[2048,256]{1,0:T(8,128)(2,1)} %get-tuple-element.118.h_ref.h0_ref), custom_call_target="tpu_custom_call" | custom-call | flops 4831838208 | bytes 15728640 | tf_op jit(solution)/shard_map/weight_grads_768/pallas_call | solution.py:1775
  313.6 0.0 reduce-scatter.3.cloned.1.call-update
  313.6 0.0 reduce-scatter.5.cloned.1.call-start
  313.7 34.1 %glu_block_1280.1 = (bf16[2048,1280]{1,0:T(8,128)(2,1)}, bf16[2048,2560]{1,0:T(8,128)(2,1)}) custom-call(bf16[2048,1536]{1,0:T(8,128)(2,1)} %get-tuple-element.119.refs_1_.n_ref.refs_0_, bf16[2048,1536]{1,0:T(8,128)(2,1)} %get-tuple-element.117.c_ref.refs_1_, bf16[1536,1536]{1,0:T(8,128)(2,1)} %get-tuple-element.115.refs_3_.refs_2_.refs_0_, ...), custom_call_target="tpu_custom_call" | custom-call | flops 24159191040 | bytes 18874368 | tf_op jit(solution)/shard_map/glu_block_1280/pallas_call | solution.py:1738
  347.8 32.8 %weight_grads_3840.1 = (bf16[1536,3072]{1,0:T(8,128)(2,1)}, bf16[1536,768]{1,0:T(8,128)(2,1)}) custom-call(bf16[2048,1536]{1,0:T(8,128)(2,1)} %get-tuple-element.119.refs_1_.n_ref.refs_0_, bf16[2048,1536]{1,0:T(8,128)(2,1)} %get-tuple-element.117.c_ref.refs_1_, bf16[2048,2560]{1,0:T(8,128)(2,1)} %get-tuple-element.122.d_ref.d1_ref, ...), custom_call_target="tpu_custom_call" | custom-call | flops 24159191040 | bytes 28311552 | tf_op jit(solution)/shard_map/weight_grads_3840/pallas_call | solution.py:1775
  380.6 0.3 reduce-scatter.3.cloned.1.call-done.refs_0_
  380.9 0.0 reduce-scatter.5.cloned.1.call-update
  381.0 50.3 %glu_back.1 = (f32[512,1536]{1,0:T(8,128)}, bf16[2048,768]{1,0:T(8,128)(2,1)}, bf16[2048,768]{1,0:T(8,128)(2,1)}) custom-call(bf16[2048,512]{1,0:T(8,128)(2,1)} %get-tuple-element.126.d_ref.d0_ref, bf16[2048,2560]{1,0:T(8,128)(2,1)} %get-tuple-element.122.d_ref.d1_ref, bf16[2048,256]{1,0:T(8,128)(2,1)} %get-tuple-element.118.h_ref.h0_ref, ...), custom_call_target="tpu_custom_call" | custom-call | flops 1 | bytes 146800640 | tf_op jit(solution)/shard_map/glu_back/pallas_call | solution.py:957
  431.2 32.8 %cross_backward.1 = (bf16[512,1536]{1,0:T(8,128)(2,1)}, bf16[512,1536]{1,0:T(8,128)(2,1)}, f32[512,1536]{1,0:T(8,128)}, bf16[512,1536]{1,0:T(8,128)(2,1)}, bf16[...) custom-call(s32[1]{0:T(128)S(6)} %copy.45.len_ref, ...), custom_call_target="tpu_custom_call" | custom-call | flops 4831838208 | bytes 28311552 | tf_op jit(solution)/shard_map/cross_backward/pallas_call | solution.py:1660
  464.0 53.1 %mid_gather.1 = (bf16[6144,768]{1,0:T(8,128)(2,1)}, bf16[2048,384]{1,0:T(8,128)(2,1)}, bf16[1536,768]{1,0:T(8,128)(2,1)}, f32[192,768]{1,0:T(8,128)}) custom-call(bf16[512,1536]{1,0:T(8,128)(2,1)} %get-tuple-element.132.c_ref, bf16[1024,384]{1,0:T(8,128)(2,1)} %bitcast.16, bf16[512,1536]{1,0:T(8,128)(2,1)} %get-tuple-element.134.n_ref, ...), custom_call_target="tpu_custom_call" | custom-call | flops 1 | bytes 146800640 | tf_op jit(solution)/shard_map/mid_gather/pallas_call | solution.py:1091
  517.1 104.6 %attend_back.1 = (bf16[2048,384]{1,0:T(8,128)(2,1)}, bf16[2048,384]{1,0:T(8,128)(2,1)}, bf16[2048,384]{1,0:T(8,128)(2,1)}, f32[16,384]{1,0:T(8,128)}, f32[16,384...) custom-call(bf16[2048,384]{1,0:T(8,128)(2,1)} %get-tuple-element.97., ...), custom_call_target="tpu_custom_call" | custom-call | flops 64424509440 | bytes 15728640 | tf_op jit(solution)/shard_map/attend_back/pallas_call | solution.py:1434
  621.7 0.0 reduce-scatter.5.cloned.1.call-done.refs_1_
  621.7 19.7 %last_grads.1 = (bf16[1536,1152]{1,0:T(8,128)(2,1)}, f32[192,1536]{1,0:T(8,128)}, f32[192,1536]{1,0:T(8,128)}, f32[192,1536]{1,0:T(8,128)}, bf16[512,1536]{1,0:T...) custom-call(bf16[2048,1536]{1,0:T(8,128)(2,1)} %get-tuple-element.96, ...), custom_call_target="tpu_custom_call" | custom-call | flops 7247757312 | bytes 11010048 | tf_op jit(solution)/shard_map/last_grads/pallas_call | solution.py:1830
  641.4 67.2 %tail_sums.1 = (f32[512,1536]{1,0:T(8,128)}, f32[16,1536]{1,0:T(8,128)}, f32[192,1152]{1,0:T(8,128)}) custom-call(bf16[2048,384]{1,0:T(8,128)(2,1)} %get-tuple-element.143.q_ref, bf16[2048,384]{1,0:T(8,128)(2,1)} %get-tuple-element.144.k_ref, bf16[2048,384]{1,0:T(8,128)(2,1)} %get-tuple-element.145.v_ref, bf16[2048,1536]{1,0:T(8,128)(2,1)} %get-tuple-element.94.x_ref.fa_ref, ...), custom_call_target="tpu_custom_call" | custom-call | flops 1 | bytes 146800640 | tf_op jit(solution)/shard_map/tail_sums/pallas_call | solution.py:788
  708.5 1.6 slice_reduce_fusion
  710.1 1.4 slice.21
  711.5 2.1 fusion.5
  713.6 3.8 copy.46
  (1 shorter events, 0.0 us)
Async XLA Ops:
  7.2 5.5 copy-start
  7.2 5.5 copy-start.1
  7.2 373.7 %reduce-scatter.3.cloned.1.call-start = ((), (), s32[]{:S(2)}) async-start(), calls=%async_computation.2 | async-start | bytes 2654208 | tf_op jit(solution)/shard_map/reduce_scatter | solution.py:1851
  313.6 308.1 %reduce-scatter.5.cloned.1.call-start = ((), (), s32[]{:S(2)}) async-start(), calls=%async_computation.3 | async-start | bytes 10616832 | tf_op jit(solution)/shard_map/reduce_scatter | solution.py:1851
Sparse Core Ops, SparseCore 0:
  313.8 67.1 reduce-scatter.2
  384.5 191.8 reduce-scatter.4
